TPU v7x, 512 devices: a whole 4x8x8 slice. The times are simulated.
512 devices in a mesh: row: 16 (over y, core), col: 32 (over x, z).
Axes of the slice: x: 4, y: 8, z: 8, core: 2. Of those that a mesh axis runs over, the one named last changes fastest.
Arguments:
- a_blocks: bfloat16 [32768, 4096], P(('row', 'col')), may hold values from -0.75 to 0.75
- blk_row: int32 [32768], P(('row', 'col')), may hold values from 0 to 4095, as said below
- blk_col: int32 [32768], P(('row', 'col')), may hold values from 0 to 4095, as said below
- drop_mask: int32 [32768], P(('row', 'col')), may hold values 0 or 1
- prolong: bfloat16 [4096, 1024], P(('row', 'col')), may hold values from -6 to 6
- agg_label: int32 [4096], P(('row', 'col')), may hold values from 0 to 1
- inv_diag: bfloat16 [4096, 4096], P(('row', 'col'))
Outputs:
- coarse: float32 [32768, 1024], P(('row', 'col'))
Inputs may be any that keep to these rules, and one draw needn't show every extreme that they name: `blk_row`: blocks stand 64 to a device, devices in row-major order over (row, col); a block on the device (r, c) has its row element in r * 256 to (r + 1) * 256 - 1. Every element is the row and column of one block. `blk_col`: A block on the device (r, c) has a column element e with (e // 8) % (size of col) = c.
All inputs are finite; a program needn't handle non-finite values. No bound on the sum of `drop_mask` on one device may be relied on, other than what follows from the above.
Results may differ from a plain program's by a relative error of at most 0.0003.
Values may be sent and summed in bfloat16 or wider, within the bound.
No kernel may reach another device: no remote copies, remote signals or barrier semaphores. Data moves between devices by JAX's collectives and lax.ppermute only.
A program may use at most 64 MiB of HBM per device.

v0:
```python
import jax
import jax.numpy as jnp
from jax import lax
from jax.sharding import PartitionSpec as P

BS = 64
PC = 16
NX = 4
NZ = 8
HIGHEST = lax.Precision.HIGHEST
F32 = jnp.float32
BF16 = jnp.bfloat16

X_GROUPS = [[x * NZ + z for x in range(NX)] for z in range(NZ)]
Z_GROUPS = [[x * NZ + z for z in range(NZ)] for x in range(NX)]


def shift_x(step):
    return [(x * NZ + z, (x + step) % NX * NZ + z) for x in range(NX) for z in range(NZ)]


def spread(values, groups):
    count = len(groups[0])
    copies = jnp.broadcast_to(values[None], (count,) + values.shape)
    return lax.all_to_all(copies, "col", 0, 0, axis_index_groups=groups, tiled=True)


def two_parts(values):
    high = lax.reduce_precision(values, 8, 7)
    return high.astype(BF16), (values - high).astype(BF16)


def body(a_blocks, blk_row, blk_col, drop_mask, prolong, agg_label, inv_diag):
    slot_count = a_blocks.shape[0]
    per_device = prolong.shape[0]
    width = prolong.shape[1]
    col_count = lax.axis_size("col")
    row_index = lax.axis_index("row")
    col_index = lax.axis_index("col")
    span = col_count * per_device
    panel_first = row_index * span
    own_first = panel_first + col_index * per_device

    both = spread(jnp.concatenate([prolong, inv_diag], axis=1), Z_GROUPS)
    both = both.reshape(NZ * per_device, width + inv_diag.shape[1])
    row_part = both[:, :width]
    inv_part = both[:, width:]
    row_panel = spread(row_part, X_GROUPS).reshape(span, width)
    inv_parts = [inv_part]
    for k in (1, 2, 3):
        inv_parts.append(lax.ppermute(inv_part, "col", shift_x(k)))

    labelled = jnp.concatenate(
        [prolong, jnp.broadcast_to(agg_label.astype(BF16)[:, None], (per_device, 128))], axis=1
    )
    col_panel = lax.all_gather(labelled, "row", axis=0, tiled=True)

    keep = (drop_mask == 1) | (blk_row == blk_col)
    local_row = blk_row - panel_first
    matrices = a_blocks.reshape(slot_count, BS, BS)

    pick = (local_row[:, None] == jnp.arange(span)[None, :]) & ~keep[:, None]
    row_blocks = jnp.dot(pick.astype(BF16), row_panel, preferred_element_type=F32).astype(BF16)
    drop_terms = jnp.einsum(
        "sij,sjk->sik", matrices, row_blocks.reshape(slot_count, BS, PC), preferred_element_type=F32
    ).reshape(slot_count, width)
    place = (jnp.arange(span)[:, None] == local_row[None, :]).astype(BF16)
    parts = jnp.concatenate(two_parts(drop_terms), axis=0)
    sums = jnp.dot(jnp.concatenate([place, place], axis=1), parts, preferred_element_type=F32)
    sums = sums.reshape(col_count, per_device, width)
    arrived = lax.all_to_all(sums, "col", 0, 0, tiled=True)
    lumped = jnp.sum(arrived.reshape(col_count, per_device, width), axis=0)
    scaled_lumped = jnp.einsum(
        "eij,ejk->eik",
        inv_diag.astype(F32).reshape(per_device, BS, BS),
        lumped.reshape(per_device, BS, PC),
        precision=HIGHEST,
    ).reshape(per_device, width)

    col_place = blk_col // span * per_device + blk_col % per_device
    pick = col_place[:, None] == jnp.arange(col_panel.shape[0])[None, :]
    picked = jnp.dot(pick.astype(BF16), col_panel, preferred_element_type=F32)
    col_label = picked[:, width]
    col_blocks = (picked[:, :width] * keep[:, None].astype(F32)).astype(BF16)
    kept_terms = jnp.einsum(
        "sij,sjk->sik", matrices, col_blocks.reshape(slot_count, BS, PC), preferred_element_type=F32
    ).reshape(slot_count, width)
    col_run = blk_col // per_device
    row_run = blk_row // per_device
    same_group = (
        (blk_row[:, None] == blk_row[None, :])
        & (col_run[:, None] == col_run[None, :])
        & (col_label[:, None] == col_label[None, :])
    )
    same_group = same_group.astype(BF16)
    parts = jnp.concatenate(two_parts(kept_terms), axis=0)
    grouped = jnp.dot(
        jnp.concatenate([same_group, same_group], axis=1), parts, preferred_element_type=F32
    )

    col_x = col_index // NZ
    part_rows = NZ * per_device
    row_x = local_row // part_rows
    inverse = None
    for step, part in enumerate(inv_parts):
        at = jnp.where((col_x - row_x) % NX == step, local_row % part_rows, -1)
        pick = (at[:, None] == jnp.arange(part_rows)[None, :]).astype(BF16)
        piece = jnp.dot(pick, part, preferred_element_type=F32)
        inverse = piece if inverse is None else inverse + piece
    inverse = inverse.astype(BF16).reshape(slot_count, BS, BS)
    parts = [part.reshape(slot_count, BS, PC) for part in two_parts(grouped)]
    coarse = jnp.einsum(
        "sij,sjk->sik", inverse, jnp.concatenate(parts, axis=2), preferred_element_type=F32
    )
    coarse = (coarse[:, :, :PC] + coarse[:, :, PC:]).reshape(slot_count, width)

    target = (
        (blk_row[:, None] == own_first + jnp.arange(per_device)[None, :])
        & (col_run == row_run)[:, None]
        & (col_label[:, None] == agg_label.astype(F32)[None, :])
    )
    return coarse + jnp.dot(target.astype(F32), scaled_lumped, precision=HIGHEST)


def solution(mesh):
    return jax.shard_map(
        body,
        mesh=mesh,
        in_specs=(
            P(("row", "col"), None),
            P(("row", "col")),
            P(("row", "col")),
            P(("row", "col")),
            P(("row", "col"), None),
            P(("row", "col")),
            P(("row", "col"), None),
        ),
        out_specs=P(("row", "col"), None),
        check_vma=False,
    )
```

profile of v0, /device:TPU:1, one launch (start us, length us, event | category | flops | bytes accessed | tf_op | source)
XLA Modules:
  0.0 109.6 jit_solution(2184071769361486969)
XLA Ops:
  0.0 0.8 pad_maximum_fusion
  0.8 0.9 broadcast_in_dim.10
  1.7 11.0 %all-to-all-start = ((bf16[8,8,5120]{2,1,0:T(8,128)(2,1)}), bf16[8,8,5120]{2,1,0:T(8,128)(2,1)S(1)}, u32[]{:S(2)}, u32[]{:S(2)}) async-start(bf16[8,8,5120]{2,1,0:T(8,128)(2,1)} %broadcast_in_dim.10), calls=%async_computation | async-start | bytes 1310720 | tf_op jit(solution)/shard_map/all_to_all | solution.py:25
  12.8 0.6 copy-done.6
  13.5 19.2 %all_gather.3 = bf16[128,1152]{1,0:T(8,128)(2,1)S(1)} all-gather(bf16[8,1152]{1,0:T(8,128)(2,1)S(1)} %pad_maximum_fusion.1), channel_id=1, replica_groups=mesh['row'=16,'col'=32] {'row'}, dimensions={0}, use_global_device_ids=true | all-gather | bytes 313344 | tf_op jit(solution)/shard_map/all_gather | solution.py:56
  34.0 0.5 copy-done
  34.5 1.1 %reshape.74 = bf16[64,64,64]{2,1,0:T(8,128)(2,1)S(1)} reshape(bf16[64,4096]{1,0:T(8,128)(2,1)S(1)} %copy-done) | data formatting | bytes 1048576 | tf_op jit(solution)/shard_map/reshape | solution.py:60
  35.6 0.6 convolution_bitcast_fusion.2
  36.9 0.9 broadcast_in_dim.12
  37.7 4.0 %all-to-all-start.1 = ((bf16[4,64,1024]{2,1,0:T(8,128)(2,1)}), bf16[4,64,1024]{2,1,0:T(8,128)(2,1)S(1)}, u32[]{:S(2)}, u32[]{:S(2)}) async-start(bf16[4,64,1024]{2,1,0:T(8,128)(2,1)} %broadcast_in_dim.12), calls=%async_computation.1 | async-start | bytes 1048576 | tf_op jit(solution)/shard_map/all_to_all | solution.py:25
  41.9 8.9 %all-to-all-done.1 = bf16[4,64,1024]{2,1,0:T(8,128)(2,1)S(1)} async-done(((bf16[4,64,1024]{2,1,0:T(8,128)(2,1)}), bf16[4,64,1024]{2,1,0:T(8,128)(2,1)S(1)}, u32[]{:S(2)}, u32[]{:S(2)}) %all-to-all-start.1) | async-done | bytes 524320 | tf_op jit(solution)/shard_map/all_to_all | solution.py:25
  51.7 0.6 convolution_bitcast_fusion.1
  52.8 1.4 %convolution_bitcast_fusion = f32[32,8,1024]{2,1,0:T(8,128)} fusion(bf16[64,1024]{0,1:T(8,128)(2,1)S(1)} %get-tuple-element.14, bf16[64,1024]{0,1:T(8,128)(2,1)S(1)} %get-tuple-element.13, pred[256,64]{1,0:T(32,128)(4,1)S(1)} %iota_compare_fusion), kind=kOutput, calls=%fused_computation.4 | convolution fusion | flops 67665920 | bytes 1327104 | tf_op jit(solution)/shard_map/dot_general | solution.py:69
  54.2 7.9 %all-to-all-start.2 = ((f32[32,8,1024]{2,1,0:T(8,128)}), f32[32,8,1024]{2,1,0:T(8,128)S(1)}, u32[]{:S(2)}, u32[]{:S(2)}) async-start(f32[32,8,1024]{2,1,0:T(8,128)} %convolution_bitcast_fusion), calls=%async_computation.2 | async-start | bytes 2097152 | tf_op jit(solution)/shard_map/all_to_all | solution.py:71
  62.4 0.9 slice.24
  63.3 4.4 %collective-permute-start.2 = (bf16[64,4096]{1,0:T(8,128)(2,1)}, bf16[64,4096]{1,0:T(8,128)(2,1)}, u32[]{:S(2)}, u32[]{:S(2)}) collective-permute-start(bf16[64,4096]{1,0:T(8,128)(2,1)} %slice.24), channel_id=1, source_target_pairs={{0,24},{1,25},{2,26},{3,27},{4,28},{5,29},{6,30},{7,31},{8,0},{9,1... | collective-permute-start | bytes 1572872 | tf_op jit(solution)/shard_map/ppermute | solution.py:51
  69.0 2.4 %collective-permute-start.1 = (bf16[64,4096]{1,0:T(8,128)(2,1)}, bf16[64,4096]{1,0:T(8,128)(2,1)S(1)}, u32[]{:S(2)}, u32[]{:S(2)}) collective-permute-start(bf16[64,4096]{1,0:T(8,128)(2,1)} %slice.24), channel_id=1, source_target_pairs={{0,16},{1,17},{2,18},{3,19},{4,20},{5,21},{6,22},{7,23},{8,24},{9,... | collective-permute-start | bytes 1572872 | tf_op jit(solution)/shard_map/ppermute | solution.py:51
  71.5 2.5 %collective-permute-start = (bf16[64,4096]{1,0:T(8,128)(2,1)}, bf16[64,4096]{1,0:T(8,128)(2,1)S(1)}, u32[]{:S(2)}, u32[]{:S(2)}) collective-permute-start(bf16[64,4096]{1,0:T(8,128)(2,1)} %slice.24), channel_id=1, source_target_pairs={{0,8},{1,9},{2,10},{3,11},{4,12},{5,13},{6,14},{7,15},{8,16},{9,17... | collective-permute-start | bytes 1572872 | tf_op jit(solution)/shard_map/ppermute | solution.py:51
  74.3 13.5 %collective-permute-done.2 = bf16[64,4096]{1,0:T(8,128)(2,1)} collective-permute-done((bf16[64,4096]{1,0:T(8,128)(2,1)}, bf16[64,4096]{1,0:T(8,128)(2,1)}, u32[]{:S(2)}, u32[]{:S(2)}) %collective-permute-start.2) | collective-permute-done | bytes 524320 | tf_op jit(solution)/shard_map/ppermute | solution.py:51
  87.8 1.4 %fusion.25 = f32[64,4096]{1,0:T(8,128)S(1)} fusion(bf16[64,4096]{1,0:T(8,128)(2,1)} %collective-permute-done.2, s32[64]{0:T(128)S(1)} %get-tuple-element.22), kind=kOutput, calls=%fused_computation.49 | convolution fusion | flops 33558528 | bytes 1573120 | tf_op jit(solution)/shard_map/dot_general | solution.py:108
  89.2 15.4 %collective-permute-done = bf16[64,4096]{1,0:T(8,128)(2,1)S(1)} collective-permute-done((bf16[64,4096]{1,0:T(8,128)(2,1)}, bf16[64,4096]{1,0:T(8,128)(2,1)S(1)}, u32[]{:S(2)}, u32[]{:S(2)}) %collective-permute-start) | collective-permute-done | bytes 524320 | tf_op jit(solution)/shard_map/ppermute | solution.py:51
  105.2 1.1 %reshape.72 = bf16[64,64,64]{2,1,0:T(8,128)(2,1)S(1)} reshape(bf16[64,4096]{1,0:T(8,128)(2,1)S(1)} %fusion.1) | data formatting | bytes 1048576 | tf_op jit(solution)/shard_map/reshape | solution.py:110
  106.4 0.7 fusion.4
  108.5 1.1 convolution_add_fusion.2
  (56 shorter events, 7.5 us)
Async XLA Ops:
  1.7 11.0 %copy-start.4 = (s32[64]{0:T(128)S(1)}, s32[64]{0:T(128)}, u32[]{:S(2)}) copy-start(s32[64]{0:T(128)} %param.9) | copy-start | bytes 772
  1.7 11.7 %copy-start.2 = (bf16[8,1024]{1,0:T(8,128)(2,1)S(1)}, bf16[8,1024]{1,0:T(8,128)(2,1)}, u32[]{:S(2)}) copy-start(bf16[8,1024]{1,0:T(8,128)(2,1)} %param.11) | copy-start | bytes 49156
  1.7 35.1 %all-to-all-start = ((bf16[8,8,5120]{2,1,0:T(8,128)(2,1)}), bf16[8,8,5120]{2,1,0:T(8,128)(2,1)S(1)}, u32[]{:S(2)}, u32[]{:S(2)}) async-start(bf16[8,8,5120]{2,1,0:T(8,128)(2,1)} %broadcast_in_dim.10), calls=%async_computation | async-start | bytes 1310720 | tf_op jit(solution)/shard_map/all_to_all | solution.py:25
  12.7 0.7 copy-start.6
  32.6 0.7 copy-start.3
  32.6 0.7 copy-start.5
  33.4 1.0 copy-start
  37.7 13.1 %all-to-all-start.1 = ((bf16[4,64,1024]{2,1,0:T(8,128)(2,1)}), bf16[4,64,1024]{2,1,0:T(8,128)(2,1)S(1)}, u32[]{:S(2)}, u32[]{:S(2)}) async-start(bf16[4,64,1024]{2,1,0:T(8,128)(2,1)} %broadcast_in_dim.12), calls=%async_computation.1 | async-start | bytes 1048576 | tf_op jit(solution)/shard_map/all_to_all | solution.py:25
  54.2 53.5 %all-to-all-start.2 = ((f32[32,8,1024]{2,1,0:T(8,128)}), f32[32,8,1024]{2,1,0:T(8,128)S(1)}, u32[]{:S(2)}, u32[]{:S(2)}) async-start(f32[32,8,1024]{2,1,0:T(8,128)} %convolution_bitcast_fusion), calls=%async_computation.2 | async-start | bytes 2097152 | tf_op jit(solution)/shard_map/all_to_all | solution.py:71
  62.4 5.3 %copy-start.1 = (bf16[8,4096]{1,0:T(8,128)(2,1)S(1)}, bf16[8,4096]{1,0:T(8,128)(2,1)}, u32[]{:S(2)}) copy-start(bf16[8,4096]{1,0:T(8,128)(2,1)} %param.13) | copy-start | bytes 196612
  63.3 24.5 %collective-permute-start.2 = (bf16[64,4096]{1,0:T(8,128)(2,1)}, bf16[64,4096]{1,0:T(8,128)(2,1)}, u32[]{:S(2)}, u32[]{:S(2)}) collective-permute-start(bf16[64,4096]{1,0:T(8,128)(2,1)} %slice.24), channel_id=1, source_target_pairs={{0,24},{1,25},{2,26},{3,27},{4,28},{5,29},{6,30},{7,31},{8,0},{9,1... | collective-permute-start | bytes 1572872 | tf_op jit(solution)/shard_map/ppermute | solution.py:51
  69.0 35.9 %collective-permute-start.1 = (bf16[64,4096]{1,0:T(8,128)(2,1)}, bf16[64,4096]{1,0:T(8,128)(2,1)S(1)}, u32[]{:S(2)}, u32[]{:S(2)}) collective-permute-start(bf16[64,4096]{1,0:T(8,128)(2,1)} %slice.24), channel_id=1, source_target_pairs={{0,16},{1,17},{2,18},{3,19},{4,20},{5,21},{6,22},{7,23},{8,24},{9,... | collective-permute-start | bytes 1572872 | tf_op jit(solution)/shard_map/ppermute | solution.py:51
  71.5 33.1 %collective-permute-start = (bf16[64,4096]{1,0:T(8,128)(2,1)}, bf16[64,4096]{1,0:T(8,128)(2,1)S(1)}, u32[]{:S(2)}, u32[]{:S(2)}) collective-permute-start(bf16[64,4096]{1,0:T(8,128)(2,1)} %slice.24), channel_id=1, source_target_pairs={{0,8},{1,9},{2,10},{3,11},{4,12},{5,13},{6,14},{7,15},{8,16},{9,17... | collective-permute-start | bytes 1572872 | tf_op jit(solution)/shard_map/ppermute | solution.py:51
where the time goes:
time: 110 us
  waiting for transfers between devices  37.8 us (34%)
  starting transfers between devices  32.2 us (29%)
  blocking collectives  19.2 us (17%)
  local copies, waits for them, and re-layouts  10.7 us (10%)
  matrix products  7.93 us (7%)
  other arithmetic  1.44 us (1%)
    ppermute x3, waiting for transfers between devices, body(): inv_parts.append(lax.ppermute(inv_part, 'col', shift_x(k)))  28.8 us
    all_gather x1, blocking collectives, body(): col_panel = lax.all_gather(labelled, 'row', axis=0, tiled=True)  19.2 us
    all_to_all x2, starting transfers between devices, spread(): lax.all_to_all(copies, 'col', 0, 0, axis_index_groups=groups, tiled=True)  15 us
    ppermute x3, starting transfers between devices, body(): inv_parts.append(lax.ppermute(inv_part, 'col', shift_x(k)))  9.32 us
    all_to_all x2, waiting for transfers between devices, spread(): lax.all_to_all(copies, 'col', 0, 0, axis_index_groups=groups, tiled=True)  8.94 us
    all_to_all x1, starting transfers between devices, body(): arrived = lax.all_to_all(sums, 'col', 0, 0, tiled=True)  7.92 us
    dot_general x4, matrix products, body(): piece = jnp.dot(pick, part, preferred_element_type=F32)  2.4 us
  transfers between devices with their start and end apart: 6, of which 3 were waited for; matrix products, arithmetic and copies ran while one was open for 10% of the time, Pallas kernels for 0%

commit v1 on v0

--- a/solution.py
+++ b/solution.py
@@ -15,14 +15,15 @@
 Z_GROUPS = [[x * NZ + z for z in range(NZ)] for x in range(NX)]
 
 
-def shift_x(step):
-    return [(x * NZ + z, (x + step) % NX * NZ + z) for x in range(NX) for z in range(NZ)]
-
-
 def spread(values, groups):
     count = len(groups[0])
     copies = jnp.broadcast_to(values[None], (count,) + values.shape)
-    return lax.all_to_all(copies, "col", 0, 0, axis_index_groups=groups, tiled=True)
+    moved = lax.all_to_all(copies, "col", 0, 0, axis_index_groups=groups, tiled=True)
+    return moved.reshape((count * values.shape[0],) + values.shape[1:])
+
+
+def shift_x(step):
+    return [(x * NZ + z, (x + step) % NX * NZ + z) for x in range(NX) for z in range(NZ)]
 
 
 def two_parts(values):
@@ -41,14 +42,12 @@
     panel_first = row_index * span
     own_first = panel_first + col_index * per_device
 
-    both = spread(jnp.concatenate([prolong, inv_diag], axis=1), Z_GROUPS)
-    both = both.reshape(NZ * per_device, width + inv_diag.shape[1])
-    row_part = both[:, :width]
-    inv_part = both[:, width:]
-    row_panel = spread(row_part, X_GROUPS).reshape(span, width)
-    inv_parts = [inv_part]
+    both = jnp.concatenate([prolong, inv_diag], axis=1)
+    both = spread(both, Z_GROUPS)
+    row_panel = spread(both[:, :width], X_GROUPS)
+    inv_parts = [both[:, width:]]
     for k in (1, 2, 3):
-        inv_parts.append(lax.ppermute(inv_part, "col", shift_x(k)))
+        inv_parts.append(lax.ppermute(inv_parts[0], "col", shift_x(k)))
 
     labelled = jnp.concatenate(
         [prolong, jnp.broadcast_to(agg_label.astype(BF16)[:, None], (per_device, 128))], axis=1
@@ -62,7 +61,10 @@
     pick = (local_row[:, None] == jnp.arange(span)[None, :]) & ~keep[:, None]
     row_blocks = jnp.dot(pick.astype(BF16), row_panel, preferred_element_type=F32).astype(BF16)
     drop_terms = jnp.einsum(
-        "sij,sjk->sik", matrices, row_blocks.reshape(slot_count, BS, PC), preferred_element_type=F32
+        "sij,sjk->sik",
+        matrices,
+        row_blocks.reshape(slot_count, BS, PC),
+        preferred_element_type=F32,
     ).reshape(slot_count, width)
     place = (jnp.arange(span)[:, None] == local_row[None, :]).astype(BF16)
     parts = jnp.concatenate(two_parts(drop_terms), axis=0)
@@ -83,7 +85,10 @@
     col_label = picked[:, width]
     col_blocks = (picked[:, :width] * keep[:, None].astype(F32)).astype(BF16)
     kept_terms = jnp.einsum(
-        "sij,sjk->sik", matrices, col_blocks.reshape(slot_count, BS, PC), preferred_element_type=F32
+        "sij,sjk->sik",
+        matrices,
+        col_blocks.reshape(slot_count, BS, PC),
+        preferred_element_type=F32,
     ).reshape(slot_count, width)
     col_run = blk_col // per_device
     row_run = blk_row // per_device
@@ -91,23 +96,22 @@
         (blk_row[:, None] == blk_row[None, :])
         & (col_run[:, None] == col_run[None, :])
         & (col_label[:, None] == col_label[None, :])
-    )
-    same_group = same_group.astype(BF16)
+    ).astype(BF16)
     parts = jnp.concatenate(two_parts(kept_terms), axis=0)
     grouped = jnp.dot(
         jnp.concatenate([same_group, same_group], axis=1), parts, preferred_element_type=F32
     )
 
-    col_x = col_index // NZ
     part_rows = NZ * per_device
     row_x = local_row // part_rows
     inverse = None
-    for step, part in enumerate(inv_parts):
-        at = jnp.where((col_x - row_x) % NX == step, local_row % part_rows, -1)
+    for k in (0, 1, 3, 2):
+        at = jnp.where((col_index // NZ - row_x) % NX == k, local_row % part_rows, -1)
         pick = (at[:, None] == jnp.arange(part_rows)[None, :]).astype(BF16)
-        piece = jnp.dot(pick, part, preferred_element_type=F32)
+        piece = jnp.dot(pick, inv_parts[k], preferred_element_type=F32)
         inverse = piece if inverse is None else inverse + piece
-    inverse = inverse.astype(BF16).reshape(slot_count, BS, BS)
+    inverse = inverse.astype(BF16)
+    inverse = inverse.reshape(slot_count, BS, BS)
     parts = [part.reshape(slot_count, BS, PC) for part in two_parts(grouped)]
     coarse = jnp.einsum(
         "sij,sjk->sik", inverse, jnp.concatenate(parts, axis=2), preferred_element_type=F32

time: 110 us -> 107 us (0.973)
  waiting for transfers between devices: 37.8 us -> 34 us
    ppermute x3, waiting for transfers between devices: 28.8 us -> 25 us  [body(): inv_parts.append(lax.ppermute(inv_parts[0], 'col', shift_x(k)))]
where the time goes in v1:
time: 107 us; the launch traced here: 106 us
  waiting for transfers between devices  34 us (32%)
  starting transfers between devices  32.8 us (31%)
  blocking collectives  19.2 us (18%)
  local copies, waits for them, and re-layouts  10.7 us (10%)
  matrix products  7.93 us (7%)
  other arithmetic  1.44 us (1%)
    ppermute x3, waiting for transfers between devices, body(): inv_parts.append(lax.ppermute(inv_parts[0], 'col', shift_x(k)))  25 us
    all_gather x1, blocking collectives, body(): col_panel = lax.all_gather(labelled, 'row', axis=0, tiled=True)  19.2 us
    all_to_all x2, starting transfers between devices, spread(): lax.all_to_all(copies, 'col', 0, 0, axis_index_groups=groups, tiled=True)  15 us
    ppermute x3, starting transfers between devices, body(): inv_parts.append(lax.ppermute(inv_parts[0], 'col', shift_x(k)))  9.92 us
    all_to_all x2, waiting for transfers between devices, spread(): lax.all_to_all(copies, 'col', 0, 0, axis_index_groups=groups, tiled=True)  8.94 us
    all_to_all x1, starting transfers between devices, body(): arrived = lax.all_to_all(sums, 'col', 0, 0, tiled=True)  7.92 us
    dot_general x4, matrix products, body(): piece = jnp.dot(pick, inv_parts[k], preferred_element_type=F32)  2.4 us
  transfers between devices with their start and end apart: 6, of which 3 were waited for; matrix products, arithmetic and copies ran while one was open for 10% of the time, Pallas kernels for 0%

profile of v1, /device:TPU:1, one launch (start us, length us, event | category | flops | bytes accessed | tf_op | source)
XLA Modules:
  0.0 106.4 jit_solution(3056387867990366091)
XLA Ops:
  0.0 0.8 pad_maximum_fusion
  0.8 0.9 broadcast_in_dim.10
  1.7 11.0 %all-to-all-start = ((bf16[8,8,5120]{2,1,0:T(8,128)(2,1)}), bf16[8,8,5120]{2,1,0:T(8,128)(2,1)S(1)}, u32[]{:S(2)}, u32[]{:S(2)}) async-start(bf16[8,8,5120]{2,1,0:T(8,128)(2,1)} %broadcast_in_dim.10), calls=%async_computation | async-start | bytes 1310720 | tf_op jit(solution)/shard_map/all_to_all | solution.py:21
  12.8 0.6 copy-done.6
  13.5 19.2 %all_gather.3 = bf16[128,1152]{1,0:T(8,128)(2,1)S(1)} all-gather(bf16[8,1152]{1,0:T(8,128)(2,1)S(1)} %pad_maximum_fusion.1), channel_id=1, replica_groups=mesh['row'=16,'col'=32] {'row'}, dimensions={0}, use_global_device_ids=true | all-gather | bytes 313344 | tf_op jit(solution)/shard_map/all_gather | solution.py:55
  34.0 0.5 copy-done
  34.5 1.1 %reshape.74 = bf16[64,64,64]{2,1,0:T(8,128)(2,1)S(1)} reshape(bf16[64,4096]{1,0:T(8,128)(2,1)S(1)} %copy-done) | data formatting | bytes 1048576 | tf_op jit(solution)/shard_map/reshape | solution.py:59
  35.6 0.6 convolution_bitcast_fusion.2
  36.9 0.9 broadcast_in_dim.12
  37.7 4.0 %all-to-all-start.1 = ((bf16[4,64,1024]{2,1,0:T(8,128)(2,1)}), bf16[4,64,1024]{2,1,0:T(8,128)(2,1)S(1)}, u32[]{:S(2)}, u32[]{:S(2)}) async-start(bf16[4,64,1024]{2,1,0:T(8,128)(2,1)} %broadcast_in_dim.12), calls=%async_computation.1 | async-start | bytes 1048576 | tf_op jit(solution)/shard_map/all_to_all | solution.py:21
  41.9 8.9 %all-to-all-done.1 = bf16[4,64,1024]{2,1,0:T(8,128)(2,1)S(1)} async-done(((bf16[4,64,1024]{2,1,0:T(8,128)(2,1)}), bf16[4,64,1024]{2,1,0:T(8,128)(2,1)S(1)}, u32[]{:S(2)}, u32[]{:S(2)}) %all-to-all-start.1) | async-done | bytes 524320 | tf_op jit(solution)/shard_map/all_to_all | solution.py:21
  51.7 0.6 convolution_bitcast_fusion.1
  52.8 1.4 %convolution_bitcast_fusion = f32[32,8,1024]{2,1,0:T(8,128)} fusion(bf16[64,1024]{0,1:T(8,128)(2,1)S(1)} %get-tuple-element.14, bf16[64,1024]{0,1:T(8,128)(2,1)S(1)} %get-tuple-element.13, pred[256,64]{1,0:T(32,128)(4,1)S(1)} %iota_compare_fusion), kind=kOutput, calls=%fused_computation.4 | convolution fusion | flops 67665920 | bytes 1327104 | tf_op jit(solution)/shard_map/dot_general | solution.py:71
  54.2 7.9 %all-to-all-start.2 = ((f32[32,8,1024]{2,1,0:T(8,128)}), f32[32,8,1024]{2,1,0:T(8,128)S(1)}, u32[]{:S(2)}, u32[]{:S(2)}) async-start(f32[32,8,1024]{2,1,0:T(8,128)} %convolution_bitcast_fusion), calls=%async_computation.2 | async-start | bytes 2097152 | tf_op jit(solution)/shard_map/all_to_all | solution.py:73
  62.4 0.9 slice.24
  63.3 4.6 %collective-permute-start.2 = (bf16[64,4096]{1,0:T(8,128)(2,1)}, bf16[64,4096]{1,0:T(8,128)(2,1)}, u32[]{:S(2)}, u32[]{:S(2)}) collective-permute-start(bf16[64,4096]{1,0:T(8,128)(2,1)} %slice.24), channel_id=1, source_target_pairs={{0,16},{1,17},{2,18},{3,19},{4,20},{5,21},{6,22},{7,23},{8,24},{9,... | collective-permute-start | bytes 1572872 | tf_op jit(solution)/shard_map/ppermute | solution.py:50
  69.3 2.8 %collective-permute-start.1 = (bf16[64,4096]{1,0:T(8,128)(2,1)}, bf16[64,4096]{1,0:T(8,128)(2,1)S(1)}, u32[]{:S(2)}, u32[]{:S(2)}) collective-permute-start(bf16[64,4096]{1,0:T(8,128)(2,1)} %slice.24), channel_id=1, source_target_pairs={{0,24},{1,25},{2,26},{3,27},{4,28},{5,29},{6,30},{7,31},{8,0},{9,1... | collective-permute-start | bytes 1572872 | tf_op jit(solution)/shard_map/ppermute | solution.py:50
  72.1 2.5 %collective-permute-start = (bf16[64,4096]{1,0:T(8,128)(2,1)}, bf16[64,4096]{1,0:T(8,128)(2,1)S(1)}, u32[]{:S(2)}, u32[]{:S(2)}) collective-permute-start(bf16[64,4096]{1,0:T(8,128)(2,1)} %slice.24), channel_id=1, source_target_pairs={{0,8},{1,9},{2,10},{3,11},{4,12},{5,13},{6,14},{7,15},{8,16},{9,17... | collective-permute-start | bytes 1572872 | tf_op jit(solution)/shard_map/ppermute | solution.py:50
  74.9 13.4 %collective-permute-done.2 = bf16[64,4096]{1,0:T(8,128)(2,1)} collective-permute-done((bf16[64,4096]{1,0:T(8,128)(2,1)}, bf16[64,4096]{1,0:T(8,128)(2,1)}, u32[]{:S(2)}, u32[]{:S(2)}) %collective-permute-start.2) | collective-permute-done | bytes 524320 | tf_op jit(solution)/shard_map/ppermute | solution.py:50
  88.3 1.4 %fusion.25 = f32[64,4096]{1,0:T(8,128)S(1)} fusion(bf16[64,4096]{1,0:T(8,128)(2,1)} %collective-permute-done.2, s32[64]{0:T(128)S(1)} %get-tuple-element.22), kind=kOutput, calls=%fused_computation.49 | convolution fusion | flops 33558528 | bytes 1573120 | tf_op jit(solution)/shard_map/dot_general | solution.py:111
  89.6 11.7 %collective-permute-done = bf16[64,4096]{1,0:T(8,128)(2,1)S(1)} collective-permute-done((bf16[64,4096]{1,0:T(8,128)(2,1)}, bf16[64,4096]{1,0:T(8,128)(2,1)S(1)}, u32[]{:S(2)}, u32[]{:S(2)}) %collective-permute-start) | collective-permute-done | bytes 524320 | tf_op jit(solution)/shard_map/ppermute | solution.py:50
  102.0 1.1 %reshape.72 = bf16[64,64,64]{2,1,0:T(8,128)(2,1)S(1)} reshape(bf16[64,4096]{1,0:T(8,128)(2,1)S(1)} %fusion.1) | data formatting | bytes 1048576 | tf_op jit(solution)/shard_map/reshape | solution.py:114
  103.1 0.7 fusion.4
  105.3 1.1 %convolution_add_fusion.2 = f32[64,1024]{1,0:T(8,128)} fusion(f32[64,1024]{1,0:T(8,128)S(1)} %copy.39, f32[8,1024]{1,0:T(8,128)S(1)} %reshape.85, f32[64]{0:T(128)S(1)} %slice_reduce_fusion, s32[64]{0:T(128)S(1)} %copy-done.3, f32[8]{0:T(128)S(1)} %get-tuple-element.24, s32[8]{0:T(128)S(1)} %iota_add_fusion, pred[64]{0:T(512)(128)(4,1)S(1)} %get-tuple-element.5), kind=kOutput, calls=%fused_computation.7 | convolution fusion | flops 6359040 | bytes 557696 | tf_op jit(solution)/shard_map/dot_general | solution.py:126
  (56 shorter events, 7.5 us)
Async XLA Ops:
  1.7 11.0 %copy-start.4 = (s32[64]{0:T(128)S(1)}, s32[64]{0:T(128)}, u32[]{:S(2)}) copy-start(s32[64]{0:T(128)} %param.9) | copy-start | bytes 772
  1.7 11.7 %copy-start.2 = (bf16[8,1024]{1,0:T(8,128)(2,1)S(1)}, bf16[8,1024]{1,0:T(8,128)(2,1)}, u32[]{:S(2)}) copy-start(bf16[8,1024]{1,0:T(8,128)(2,1)} %param.11) | copy-start | bytes 49156
  1.7 35.1 %all-to-all-start = ((bf16[8,8,5120]{2,1,0:T(8,128)(2,1)}), bf16[8,8,5120]{2,1,0:T(8,128)(2,1)S(1)}, u32[]{:S(2)}, u32[]{:S(2)}) async-start(bf16[8,8,5120]{2,1,0:T(8,128)(2,1)} %broadcast_in_dim.10), calls=%async_computation | async-start | bytes 1310720 | tf_op jit(solution)/shard_map/all_to_all | solution.py:21
  12.7 0.7 copy-start.6
  32.6 0.7 copy-start.3
  32.6 0.7 copy-start.5
  33.4 1.0 copy-start
  37.7 13.1 %all-to-all-start.1 = ((bf16[4,64,1024]{2,1,0:T(8,128)(2,1)}), bf16[4,64,1024]{2,1,0:T(8,128)(2,1)S(1)}, u32[]{:S(2)}, u32[]{:S(2)}) async-start(bf16[4,64,1024]{2,1,0:T(8,128)(2,1)} %broadcast_in_dim.12), calls=%async_computation.1 | async-start | bytes 1048576 | tf_op jit(solution)/shard_map/all_to_all | solution.py:21
  54.2 50.3 %all-to-all-start.2 = ((f32[32,8,1024]{2,1,0:T(8,128)}), f32[32,8,1024]{2,1,0:T(8,128)S(1)}, u32[]{:S(2)}, u32[]{:S(2)}) async-start(f32[32,8,1024]{2,1,0:T(8,128)} %convolution_bitcast_fusion), calls=%async_computation.2 | async-start | bytes 2097152 | tf_op jit(solution)/shard_map/all_to_all | solution.py:73
  62.4 5.5 %copy-start.1 = (bf16[8,4096]{1,0:T(8,128)(2,1)S(1)}, bf16[8,4096]{1,0:T(8,128)(2,1)}, u32[]{:S(2)}) copy-start(bf16[8,4096]{1,0:T(8,128)(2,1)} %param.13) | copy-start | bytes 196612
  63.3 25.0 %collective-permute-start.2 = (bf16[64,4096]{1,0:T(8,128)(2,1)}, bf16[64,4096]{1,0:T(8,128)(2,1)}, u32[]{:S(2)}, u32[]{:S(2)}) collective-permute-start(bf16[64,4096]{1,0:T(8,128)(2,1)} %slice.24), channel_id=1, source_target_pairs={{0,16},{1,17},{2,18},{3,19},{4,20},{5,21},{6,22},{7,23},{8,24},{9,... | collective-permute-start | bytes 1572872 | tf_op jit(solution)/shard_map/ppermute | solution.py:50
  69.3 32.4 %collective-permute-start.1 = (bf16[64,4096]{1,0:T(8,128)(2,1)}, bf16[64,4096]{1,0:T(8,128)(2,1)S(1)}, u32[]{:S(2)}, u32[]{:S(2)}) collective-permute-start(bf16[64,4096]{1,0:T(8,128)(2,1)} %slice.24), channel_id=1, source_target_pairs={{0,24},{1,25},{2,26},{3,27},{4,28},{5,29},{6,30},{7,31},{8,0},{9,1... | collective-permute-start | bytes 1572872 | tf_op jit(solution)/shard_map/ppermute | solution.py:50
  72.1 29.2 %collective-permute-start = (bf16[64,4096]{1,0:T(8,128)(2,1)}, bf16[64,4096]{1,0:T(8,128)(2,1)S(1)}, u32[]{:S(2)}, u32[]{:S(2)}) collective-permute-start(bf16[64,4096]{1,0:T(8,128)(2,1)} %slice.24), channel_id=1, source_target_pairs={{0,8},{1,9},{2,10},{3,11},{4,12},{5,13},{6,14},{7,15},{8,16},{9,17... | collective-permute-start | bytes 1572872 | tf_op jit(solution)/shard_map/ppermute | solution.py:50

commit v2 on v1

--- a/solution.py
+++ b/solution.py
@@ -10,16 +10,6 @@
 HIGHEST = lax.Precision.HIGHEST
 F32 = jnp.float32
 BF16 = jnp.bfloat16
-
-X_GROUPS = [[x * NZ + z for x in range(NX)] for z in range(NZ)]
-Z_GROUPS = [[x * NZ + z for z in range(NZ)] for x in range(NX)]
-
-
-def spread(values, groups):
-    count = len(groups[0])
-    copies = jnp.broadcast_to(values[None], (count,) + values.shape)
-    moved = lax.all_to_all(copies, "col", 0, 0, axis_index_groups=groups, tiled=True)
-    return moved.reshape((count * values.shape[0],) + values.shape[1:])
 
 
 def shift_x(step):
@@ -42,12 +32,19 @@
     panel_first = row_index * span
     own_first = panel_first + col_index * per_device
 
-    both = jnp.concatenate([prolong, inv_diag], axis=1)
-    both = spread(both, Z_GROUPS)
-    row_panel = spread(both[:, :width], X_GROUPS)
-    inv_parts = [both[:, width:]]
-    for k in (1, 2, 3):
-        inv_parts.append(lax.ppermute(inv_parts[0], "col", shift_x(k)))
+    part = inv_diag.shape[1] // NX
+    quarters = inv_diag.reshape(per_device, NX, 1, part).transpose(1, 2, 0, 3)
+    quarters = jnp.broadcast_to(quarters, (NX, NZ, per_device, part))
+    quarters = quarters.reshape(col_count, per_device, part)
+    copies = jnp.broadcast_to(prolong[None], (col_count, per_device, width))
+    first = jnp.concatenate([copies, quarters], axis=2)
+    first = lax.all_to_all(first, "col", 0, 0, tiled=True).reshape(span, width + part)
+    row_panel = first[:, :width]
+    inv_own = first[:, width:]
+    inv_left = lax.ppermute(inv_own, "col", shift_x(1))
+    inv_right = lax.ppermute(inv_own, "col", shift_x(-1))
+    inv_far_a = lax.ppermute(inv_left[: span // 2], "col", shift_x(1))
+    inv_far_b = lax.ppermute(inv_right[span // 2 :], "col", shift_x(-1))
 
     labelled = jnp.concatenate(
         [prolong, jnp.broadcast_to(agg_label.astype(BF16)[:, None], (per_device, 128))], axis=1
@@ -102,21 +99,35 @@
         jnp.concatenate([same_group, same_group], axis=1), parts, preferred_element_type=F32
     )
 
-    part_rows = NZ * per_device
-    row_x = local_row // part_rows
-    inverse = None
-    for k in (0, 1, 3, 2):
-        at = jnp.where((col_index // NZ - row_x) % NX == k, local_row % part_rows, -1)
-        pick = (at[:, None] == jnp.arange(part_rows)[None, :]).astype(BF16)
-        piece = jnp.dot(pick, inv_parts[k], preferred_element_type=F32)
-        inverse = piece if inverse is None else inverse + piece
-    inverse = inverse.astype(BF16)
-    inverse = inverse.reshape(slot_count, BS, BS)
-    parts = [part.reshape(slot_count, BS, PC) for part in two_parts(grouped)]
-    coarse = jnp.einsum(
-        "sij,sjk->sik", inverse, jnp.concatenate(parts, axis=2), preferred_element_type=F32
-    )
-    coarse = (coarse[:, :, :PC] + coarse[:, :, PC:]).reshape(slot_count, width)
+    pick = (local_row[:, None] == jnp.arange(span)[None, :]).astype(BF16)
+    parts = [half.reshape(slot_count, BS, PC) for half in two_parts(grouped)]
+    parts = jnp.concatenate(parts, axis=2)
+
+    def quarter(pieces):
+        taken = None
+        for first_row, piece in pieces:
+            chosen = pick[:, first_row : first_row + piece.shape[0]]
+            term = jnp.dot(chosen, piece, preferred_element_type=F32)
+            taken = term if taken is None else taken + term
+        taken = taken.astype(BF16).reshape(slot_count, BS // NX, BS)
+        terms = jnp.einsum("sij,sjk->sik", taken, parts, preferred_element_type=F32)
+        terms = terms[:, :, :PC] + terms[:, :, PC:]
+        return terms.reshape(slot_count, width // NX)
+
+    by_distance = [
+        quarter([(0, inv_own)]),
+        quarter([(0, inv_right)]),
+        quarter([(0, inv_far_a), (span // 2, inv_far_b)]),
+        quarter([(0, inv_left)]),
+    ]
+    col_x = col_index // NZ
+    in_order = []
+    for q in range(NX):
+        value = by_distance[0]
+        for distance in range(1, NX):
+            value = jnp.where((q - col_x) % NX == distance, by_distance[distance], value)
+        in_order.append(value)
+    coarse = jnp.concatenate(in_order, axis=1)
 
     target = (
         (blk_row[:, None] == own_first + jnp.arange(per_device)[None, :])

time: 107 us -> 96.8 us (0.905)
  waiting for transfers between devices: 34 us -> 10.5 us
  matrix products: 7.93 us -> 11.5 us
  local copies, waits for them, and re-layouts: 10.7 us -> 14.2 us
  starting transfers between devices: 32.8 us -> 36.1 us
  other arithmetic: 1.44 us -> 4.04 us
    ppermute x3 -> x4, waiting for transfers between devices: 25 us -> 10.5 us  [the longest x1 7.14 us: body(): inv_far_a = lax.ppermute(inv_left[:span // 2], 'col', shift_x(1))]
    all_to_all x2 -> x1, waiting for transfers between devices: 8.94 us -> 0.01 us  [body(): lax.all_to_all(first, 'col', 0, 0, tiled=True).reshape(span, width + part)]
    dot_general x5 -> x9, matrix products: 3.05 us -> 6.59 us  [the longest x5 5.07 us: quarter(): term = jnp.dot(chosen, piece, preferred_element_type=F32)]
    slice x2 -> x3, local copies, waits for them, and re-layouts: 0.86 us -> 4.2 us  [the longest x1 1.67 us: body(): inv_far_b = lax.ppermute(inv_right[span // 2:], 'col', shift_x(-1))]
    ppermute x3 -> x4, starting transfers between devices: 9.92 us -> 13.1 us  [the longest x1 4.66 us: body(): inv_right = lax.ppermute(inv_own, 'col', shift_x(-1))]
    select_n x0 -> x8, local copies, waits for them, and re-layouts: none -> 1.28 us  [body(): jnp.where((q - col_x) % NX == distance, by_distance[distance], value)]
    all_to_all x1, starting transfers between devices: 7.92 us -> 9.16 us  [body(): arrived = lax.all_to_all(sums, 'col', 0, 0, tiled=True)]
    all_to_all x2 -> x1, starting transfers between devices: 15 us -> 13.8 us  [body(): lax.all_to_all(first, 'col', 0, 0, tiled=True).reshape(span, width + part)]
  transfers between devices with their start and end apart: 6 -> 6, of which waited for: 3 -> 2; matrix products, arithmetic and copies ran while one was open for 10% -> 24% of each run, Pallas kernels for 0% -> 0%
where the time goes in v2:
time: 96.8 us; the launch traced here: 96.1 us
  starting transfers between devices  36.1 us (37%)
  blocking collectives  19.2 us (20%)
  local copies, waits for them, and re-layouts  14.2 us (15%)
  matrix products  11.5 us (12%)
  waiting for transfers between devices  10.5 us (11%)
  other arithmetic  4.04 us (4%)
    all_gather x1, blocking collectives, body(): col_panel = lax.all_gather(labelled, 'row', axis=0, tiled=True)  19.2 us
    all_to_all x1, starting transfers between devices, body(): lax.all_to_all(first, 'col', 0, 0, tiled=True).reshape(span, width + part)  13.8 us
    all_to_all x1, starting transfers between devices, body(): arrived = lax.all_to_all(sums, 'col', 0, 0, tiled=True)  9.16 us
    ppermute x1, waiting for transfers between devices, body(): inv_far_a = lax.ppermute(inv_left[:span // 2], 'col', shift_x(1))  7.14 us
    dot_general x5, matrix products, quarter(): term = jnp.dot(chosen, piece, preferred_element_type=F32)  5.07 us
    ppermute x1, starting transfers between devices, body(): inv_right = lax.ppermute(inv_own, 'col', shift_x(-1))  4.66 us
    ppermute x1, starting transfers between devices, body(): inv_far_b = lax.ppermute(inv_right[span // 2:], 'col', shift_x(-1))  4.38 us
    ppermute x1, waiting for transfers between devices, body(): inv_far_b = lax.ppermute(inv_right[span // 2:], 'col', shift_x(-1))  3.38 us
  transfers between devices with their start and end apart: 6, of which 2 were waited for; matrix products, arithmetic and copies ran while one was open for 24% of the time, Pallas kernels for 0%

profile of v2, /device:TPU:1, one launch (start us, length us, event | category | flops | bytes accessed | tf_op | source)
XLA Modules:
  0.0 96.1 jit_solution(14939072265129184048)
XLA Ops:
  0.0 0.9 broadcast_in_dim.10
  0.9 0.8 broadcast_in_dim.8
  1.7 1.1 %pad_maximum_fusion = bf16[32,8,2048]{2,1,0:T(8,128)(2,1)} fusion(bf16[32,8,1024]{2,1,0:T(8,128)(2,1)S(1)} %bitcast.48, bf16[32,8,1024]{2,1,0:T(8,128)(2,1)S(1)} %broadcast_in_dim.8), kind=kLoop, calls=%fused_computation.11 | loop fusion | flops 2097152 | bytes 2097152 | tf_op jit(solution)/shard_map/concatenate | solution.py:40
  2.8 13.8 %all-to-all-start = ((bf16[32,8,2048]{2,1,0:T(8,128)(2,1)}), bf16[32,8,2048]{2,1,0:T(8,128)(2,1)S(1)}, u32[]{:S(2)}, u32[]{:S(2)}) async-start(bf16[32,8,2048]{2,1,0:T(8,128)(2,1)} %pad_maximum_fusion), calls=%async_computation | async-start | bytes 2097152 | tf_op jit(solution)/shard_map/all_to_all | solution.py:41
  17.2 19.2 %all_gather.3 = bf16[128,1152]{1,0:T(8,128)(2,1)S(1)} all-gather(bf16[8,1152]{1,0:T(8,128)(2,1)S(1)} %pad_maximum_fusion.2), channel_id=1, replica_groups=mesh['row'=16,'col'=32] {'row'}, dimensions={0}, use_global_device_ids=true | all-gather | bytes 313344 | tf_op jit(solution)/shard_map/all_gather | solution.py:52
  37.2 0.8 reshape.119
  38.0 1.1 %reshape.108 = bf16[64,64,64]{2,1,0:T(8,128)(2,1)S(1)} reshape(bf16[64,4096]{1,0:T(8,128)(2,1)S(1)} %copy-done) | data formatting | bytes 1048576 | tf_op jit(solution)/shard_map/reshape | solution.py:56
  39.8 0.6 convolution_bitcast_fusion.2
  43.9 0.9 slice.64
  44.7 4.7 %collective-permute-start.2 = (bf16[256,1024]{1,0:T(8,128)(2,1)}, bf16[256,1024]{1,0:T(8,128)(2,1)}, u32[]{:S(2)}, u32[]{:S(2)}) collective-permute-start(bf16[256,1024]{1,0:T(8,128)(2,1)} %slice.64), channel_id=1, source_target_pairs={{0,24},{1,25},{2,26},{3,27},{4,28},{5,29},{6,30},{7,31},{8,0},{9,1... | collective-permute-start | bytes 1572872 | tf_op jit(solution)/shard_map/ppermute | solution.py:45
  49.4 1.9 %collective-permute-start = (bf16[256,1024]{1,0:T(8,128)(2,1)}, bf16[256,1024]{1,0:T(8,128)(2,1)}, u32[]{:S(2)}, u32[]{:S(2)}) collective-permute-start(bf16[256,1024]{1,0:T(8,128)(2,1)} %slice.64), channel_id=1, source_target_pairs={{0,8},{1,9},{2,10},{3,11},{4,12},{5,13},{6,14},{7,15},{8,16},{9,17... | collective-permute-start | bytes 1572872 | tf_op jit(solution)/shard_map/ppermute | solution.py:44
  53.5 1.4 %convolution_bitcast_fusion = f32[32,8,1024]{2,1,0:T(8,128)} fusion(bf16[64,1024]{0,1:T(8,128)(2,1)S(1)} %get-tuple-element.20, bf16[64,1024]{0,1:T(8,128)(2,1)S(1)} %get-tuple-element.19, pred[256,64]{1,0:T(32,128)(4,1)S(1)} %iota_compare_fusion), kind=kOutput, calls=%fused_computation | convolution fusion | flops 67665920 | bytes 1327104 | tf_op jit(solution)/shard_map/dot_general | solution.py:68
  54.9 9.2 %all-to-all-start.1 = ((f32[32,8,1024]{2,1,0:T(8,128)}), f32[32,8,1024]{2,1,0:T(8,128)S(1)}, u32[]{:S(2)}, u32[]{:S(2)}) async-start(f32[32,8,1024]{2,1,0:T(8,128)} %convolution_bitcast_fusion), calls=%async_computation.1 | async-start | bytes 2097152 | tf_op jit(solution)/shard_map/all_to_all | solution.py:70
  64.6 1.3 %convolution_convert_fusion.2 = bf16[64,1024]{1,0:T(8,128)(2,1)S(1)} fusion(bf16[256,1024]{1,0:T(8,128)(2,1)} %collective-permute-done.2, s32[64]{0:T(128)S(1)} %broadcast_subtract_fusion), kind=kOutput, calls=%fused_computation.8 | convolution fusion | flops 33636352 | bytes 655616 | tf_op jit(solution)/shard_map/dot_general | solution.py:110
  66.1 1.7 %slice.72 = bf16[128,1024]{1,0:T(8,128)(2,1)} slice(bf16[256,1024]{1,0:T(8,128)(2,1)} %collective-permute-done.2), slice={[128:256], [0:1024]} | slice | bytes 524288 | tf_op jit(solution)/shard_map/slice | solution.py:47
  67.8 4.4 %collective-permute-start.3 = (bf16[128,1024]{1,0:T(8,128)(2,1)}, bf16[128,1024]{1,0:T(8,128)(2,1)}, u32[]{:S(2)}, u32[]{:S(2)}) collective-permute-start(bf16[128,1024]{1,0:T(8,128)(2,1)} %slice.72), channel_id=1, source_target_pairs={{0,24},{1,25},{2,26},{3,27},{4,28},{5,29},{6,30},{7,31},{8,0},{9,1... | collective-permute-start | bytes 786440 | tf_op jit(solution)/shard_map/ppermute | solution.py:47
  72.2 1.7 %slice.70 = bf16[128,1024]{1,0:T(8,128)(2,1)} slice(bf16[256,1024]{1,0:T(8,128)(2,1)} %collective-permute-done), slice={[0:128], [0:1024]} | slice | bytes 524288 | tf_op jit(solution)/shard_map/slice | solution.py:46
  73.9 2.1 %collective-permute-start.1 = (bf16[128,1024]{1,0:T(8,128)(2,1)}, bf16[128,1024]{1,0:T(8,128)(2,1)}, u32[]{:S(2)}, u32[]{:S(2)}) collective-permute-start(bf16[128,1024]{1,0:T(8,128)(2,1)} %slice.70), channel_id=1, source_target_pairs={{0,8},{1,9},{2,10},{3,11},{4,12},{5,13},{6,14},{7,15},{8,16},{9,17... | collective-permute-start | bytes 786440 | tf_op jit(solution)/shard_map/ppermute | solution.py:46
  76.3 1.3 %convolution_convert_fusion.3 = bf16[64,1024]{1,0:T(8,128)(2,1)S(1)} fusion(bf16[256,1024]{1,0:T(8,128)(2,1)} %collective-permute-done, s32[64]{0:T(128)S(1)} %broadcast_subtract_fusion), kind=kOutput, calls=%fused_computation.9 | convolution fusion | flops 33636352 | bytes 655616 | tf_op jit(solution)/shard_map/dot_general | solution.py:110
  78.2 3.4 %collective-permute-done.3 = bf16[128,1024]{1,0:T(8,128)(2,1)} collective-permute-done((bf16[128,1024]{1,0:T(8,128)(2,1)}, bf16[128,1024]{1,0:T(8,128)(2,1)}, u32[]{:S(2)}, u32[]{:S(2)}) %collective-permute-start.3) | collective-permute-done | bytes 262176 | tf_op jit(solution)/shard_map/ppermute | solution.py:47
  81.6 1.1 %fusion.24 = f32[64,1024]{1,0:T(8,128)S(1)} fusion(bf16[128,1024]{1,0:T(8,128)(2,1)} %collective-permute-done.3, pred[64,256]{1,0:T(32,128)(4,1)S(1)} %iota_compare_fusion.1), kind=kOutput, calls=%fused_computation.54 | convolution fusion | flops 16777216 | bytes 532480 | tf_op jit(solution)/shard_map/dot_general | solution.py:110
  82.7 7.1 %collective-permute-done.1 = bf16[128,1024]{1,0:T(8,128)(2,1)} collective-permute-done((bf16[128,1024]{1,0:T(8,128)(2,1)}, bf16[128,1024]{1,0:T(8,128)(2,1)}, u32[]{:S(2)}, u32[]{:S(2)}) %collective-permute-start.1) | collective-permute-done | bytes 262176 | tf_op jit(solution)/shard_map/ppermute | solution.py:46
  89.9 1.1 %fusion = bf16[64,1024]{1,0:T(8,128)(2,1)S(1)} fusion(f32[64,1024]{1,0:T(8,128)S(1)} %fusion.24, bf16[128,1024]{1,0:T(8,128)(2,1)} %collective-permute-done.1, pred[64,256]{1,0:T(32,128)(4,1)S(1)} %iota_compare_fusion.1), kind=kOutput, calls=%fused_computation.5 | convolution fusion | flops 16908288 | bytes 663552 | tf_op jit(solution)/shard_map/dot_general | solution.py:110
  95.0 1.1 %convolution_add_fusion = f32[64,1024]{1,0:T(8,128)} fusion(f32[8,1024]{1,0:T(8,128)S(1)} %reshape.120, f32[64,256]{1,0:T(8,128)S(1)} %copy.46, f32[64,256]{1,0:T(8,128)S(1)} %copy.45, f32[64,256]{1,0:T(8,128)S(1)} %copy.44, f32[64,256]{1,0:T(8,128)S(1)} %copy.43, f32[64]{0:T(128)S(1)} %copy-done.5, s32[64]{0:T(128)S(1)} %copy-done.7, f32[8]{0:T(128)S(1)} %copy-done.9, ...), kind=kOutput, calls=%fused_computation.3 | convolution fusion | flops 6555648 | bytes 557696 | tf_op jit(solution)/shard_map/dot_general | solution.py:137
  (85 shorter events, 12.9 us)
Async XLA Ops:
  2.8 13.9 %copy-start.13 = (s32[8]{0:T(128)S(1)}, s32[8]{0:T(128)}, u32[]{:S(2)}) copy-start(s32[8]{0:T(128)} %param.12) | copy-start | bytes 100
  2.8 14.5 %copy-start.3 = (bf16[8,1024]{1,0:T(8,128)(2,1)S(1)}, bf16[8,1024]{1,0:T(8,128)(2,1)}, u32[]{:S(2)}) copy-start(bf16[8,1024]{1,0:T(8,128)(2,1)} %param.11) | copy-start | bytes 49156
  2.8 33.6 %copy-start.11 = (s32[64]{0:T(128)S(1)}, s32[64]{0:T(128)}, u32[]{:S(2)}) copy-start(s32[64]{0:T(128)} %param.9) | copy-start | bytes 772
  2.8 33.9 %copy-start.6 = (s32[64]{0:T(128)S(1)}, s32[64]{0:T(128)}, u32[]{:S(2)}) copy-start(s32[64]{0:T(128)} %param.8) | copy-start | bytes 772
  2.8 33.9 %copy-start.12 = (s32[64]{0:T(128)S(1)}, s32[64]{0:T(128)}, u32[]{:S(2)}) copy-start(s32[64]{0:T(128)} %param.10) | copy-start | bytes 772
  2.8 34.4 %copy-start.2 = (bf16[8,4096]{1,0:T(8,128)(2,1)S(1)}, bf16[8,4096]{1,0:T(8,128)(2,1)}, u32[]{:S(2)}) copy-start(bf16[8,4096]{1,0:T(8,128)(2,1)} %param.13) | copy-start | bytes 196612
  2.8 41.1 %all-to-all-start = ((bf16[32,8,2048]{2,1,0:T(8,128)(2,1)}), bf16[32,8,2048]{2,1,0:T(8,128)(2,1)S(1)}, u32[]{:S(2)}, u32[]{:S(2)}) async-start(bf16[32,8,2048]{2,1,0:T(8,128)(2,1)} %pad_maximum_fusion), calls=%async_computation | async-start | bytes 2097152 | tf_op jit(solution)/shard_map/all_to_all | solution.py:41
  16.7 21.4 %copy-start = (bf16[64,4096]{1,0:T(8,128)(2,1)S(1)}, bf16[64,4096]{1,0:T(8,128)(2,1)}, u32[]{:S(2)}) copy-start(bf16[64,4096]{1,0:T(8,128)(2,1)} %param.7) | copy-start | bytes 1572868
  41.0 0.5 copy-start.4
  44.7 19.9 %collective-permute-start.2 = (bf16[256,1024]{1,0:T(8,128)(2,1)}, bf16[256,1024]{1,0:T(8,128)(2,1)}, u32[]{:S(2)}, u32[]{:S(2)}) collective-permute-start(bf16[256,1024]{1,0:T(8,128)(2,1)} %slice.64), channel_id=1, source_target_pairs={{0,24},{1,25},{2,26},{3,27},{4,28},{5,29},{6,30},{7,31},{8,0},{9,1... | collective-permute-start | bytes 1572872 | tf_op jit(solution)/shard_map/ppermute | solution.py:45
  49.4 22.8 %collective-permute-start = (bf16[256,1024]{1,0:T(8,128)(2,1)}, bf16[256,1024]{1,0:T(8,128)(2,1)}, u32[]{:S(2)}, u32[]{:S(2)}) collective-permute-start(bf16[256,1024]{1,0:T(8,128)(2,1)} %slice.64), channel_id=1, source_target_pairs={{0,8},{1,9},{2,10},{3,11},{4,12},{5,13},{6,14},{7,15},{8,16},{9,17... | collective-permute-start | bytes 1572872 | tf_op jit(solution)/shard_map/ppermute | solution.py:44
  54.9 38.8 %all-to-all-start.1 = ((f32[32,8,1024]{2,1,0:T(8,128)}), f32[32,8,1024]{2,1,0:T(8,128)S(1)}, u32[]{:S(2)}, u32[]{:S(2)}) async-start(f32[32,8,1024]{2,1,0:T(8,128)} %convolution_bitcast_fusion), calls=%async_computation.1 | async-start | bytes 2097152 | tf_op jit(solution)/shard_map/all_to_all | solution.py:70
  67.8 13.8 %collective-permute-start.3 = (bf16[128,1024]{1,0:T(8,128)(2,1)}, bf16[128,1024]{1,0:T(8,128)(2,1)}, u32[]{:S(2)}, u32[]{:S(2)}) collective-permute-start(bf16[128,1024]{1,0:T(8,128)(2,1)} %slice.72), channel_id=1, source_target_pairs={{0,24},{1,25},{2,26},{3,27},{4,28},{5,29},{6,30},{7,31},{8,0},{9,1... | collective-permute-start | bytes 786440 | tf_op jit(solution)/shard_map/ppermute | solution.py:47
  73.9 16.0 %collective-permute-start.1 = (bf16[128,1024]{1,0:T(8,128)(2,1)}, bf16[128,1024]{1,0:T(8,128)(2,1)}, u32[]{:S(2)}, u32[]{:S(2)}) collective-permute-start(bf16[128,1024]{1,0:T(8,128)(2,1)} %slice.70), channel_id=1, source_target_pairs={{0,8},{1,9},{2,10},{3,11},{4,12},{5,13},{6,14},{7,15},{8,16},{9,17... | collective-permute-start | bytes 786440 | tf_op jit(solution)/shard_map/ppermute | solution.py:46
  93.3 0.9 copy-start.1
  93.7 1.2 %copy-start.5 = (f32[64]{0:T(128)S(1)}, f32[64]{0:T(128)}, u32[]{:S(2)}) copy-start(f32[64]{0:T(128)} %copy-done.4) | copy-start | bytes 772
  93.7 1.2 %copy-start.7 = (s32[64]{0:T(128)S(1)}, s32[64]{0:T(128)}, u32[]{:S(2)}) copy-start(s32[64]{0:T(128)} %param.8) | copy-start | bytes 772
  93.7 1.2 %copy-start.8 = (pred[64]{0:T(512)(128)(4,1)S(1)}, pred[64]{0:T(512)(128)(4,1)}, u32[]{:S(2)}) copy-start(pred[64]{0:T(512)(128)(4,1)} %get-tuple-element.5) | copy-start | bytes 196
  93.7 1.2 %copy-start.9 = (f32[8]{0:T(128)S(1)}, f32[8]{0:T(128)}, u32[]{:S(2)}) copy-start(f32[8]{0:T(128)} %get-tuple-element.25) | copy-start | bytes 100
  93.7 1.2 %copy-start.10 = (s32[8]{0:T(128)S(1)}, s32[8]{0:T(128)}, u32[]{:S(2)}) copy-start(s32[8]{0:T(128)} %iota_add_fusion) | copy-start | bytes 100

commit v3 on v1

--- a/solution.py
+++ b/solution.py
@@ -42,8 +42,10 @@
     panel_first = row_index * span
     own_first = panel_first + col_index * per_device
 
-    both = jnp.concatenate([prolong, inv_diag], axis=1)
-    both = spread(both, Z_GROUPS)
+    copies = [jnp.broadcast_to(part[None], (NZ,) + part.shape) for part in (prolong, inv_diag)]
+    both = lax.all_to_all(
+        jnp.concatenate(copies, axis=2), "col", 0, 0, axis_index_groups=Z_GROUPS, tiled=True
+    ).reshape(NZ * per_device, width + inv_diag.shape[1])
     row_panel = spread(both[:, :width], X_GROUPS)
     inv_parts = [both[:, width:]]
     for k in (1, 2, 3):
@@ -105,7 +107,7 @@
     part_rows = NZ * per_device
     row_x = local_row // part_rows
     inverse = None
-    for k in (0, 1, 3, 2):
+    for k in (0, 1, 2, 3):
         at = jnp.where((col_index // NZ - row_x) % NX == k, local_row % part_rows, -1)
         pick = (at[:, None] == jnp.arange(part_rows)[None, :]).astype(BF16)
         piece = jnp.dot(pick, inv_parts[k], preferred_element_type=F32)

time: 107 us -> 110 us (1.028)
  waiting for transfers between devices: 34 us -> 37.8 us
    all_to_all x2 -> x1, starting transfers between devices: 15 us -> 4.01 us  [spread(): lax.all_to_all(copies, 'col', 0, 0, axis_index_groups=groups, tiled=True)]
    all_to_all x0 -> x1, starting transfers between devices: none -> 11 us  [body(): lax.all_to_all(jnp.concatenate(copies, axis=2), 'col', 0, 0, axis_index_g...]
    ppermute x3, waiting for transfers between devices: 25 us -> 28.8 us  [body(): inv_parts.append(lax.ppermute(inv_parts[0], 'col', shift_x(k)))]
    broadcast_in_dim x0 -> x2, local copies, waits for them, and re-layouts: none -> 1.6 us  [body(): jnp.broadcast_to(part[None], (NZ,) + part.shape)]
    unnamed x14, local copies, waits for them, and re-layouts: 1.55 us -> 0.37 us
    all_to_all x2 -> x1, waiting for transfers between devices: 8.94 us -> 8.94 us  [spread(): lax.all_to_all(copies, 'col', 0, 0, axis_index_groups=groups, tiled=True)]
where the time goes in v3:
time: 110 us; the launch traced here: 109 us
  waiting for transfers between devices  37.8 us (34%)
  starting transfers between devices  32.2 us (29%)
  blocking collectives  19.2 us (17%)
  local copies, waits for them, and re-layouts  10.2 us (9%)
  matrix products  7.93 us (7%)
  other arithmetic  1.48 us (1%)
    ppermute x3, waiting for transfers between devices, body(): inv_parts.append(lax.ppermute(inv_parts[0], 'col', shift_x(k)))  28.8 us
    all_gather x1, blocking collectives, body(): col_panel = lax.all_gather(labelled, 'row', axis=0, tiled=True)  19.2 us
    all_to_all x1, starting transfers between devices, body(): lax.all_to_all(jnp.concatenate(copies, axis=2), 'col', 0, 0, axis_index_g...  11 us
    ppermute x3, starting transfers between devices, body(): inv_parts.append(lax.ppermute(inv_parts[0], 'col', shift_x(k)))  9.32 us
    all_to_all x1, waiting for transfers between devices, spread(): lax.all_to_all(copies, 'col', 0, 0, axis_index_groups=groups, tiled=True)  8.94 us
    all_to_all x1, starting transfers between devices, body(): arrived = lax.all_to_all(sums, 'col', 0, 0, tiled=True)  7.92 us
    all_to_all x1, starting transfers between devices, spread(): lax.all_to_all(copies, 'col', 0, 0, axis_index_groups=groups, tiled=True)  4.01 us
    dot_general x4, matrix products, body(): piece = jnp.dot(pick, inv_parts[k], preferred_element_type=F32)  2.4 us
  transfers between devices with their start and end apart: 6, of which 3 were waited for; matrix products, arithmetic and copies ran while one was open for 10% of the time, Pallas kernels for 0%

profile of v3, /device:TPU:1, one launch (start us, length us, event | category | flops | bytes accessed | tf_op | source)
XLA Modules:
  0.0 109.2 jit_solution(14680813477215552101)
XLA Ops:
  0.0 0.7 broadcast_in_dim.12
  0.7 0.9 broadcast_in_dim.13
  1.6 0.9 pad_maximum_fusion
  2.5 11.0 %all-to-all-start = ((bf16[8,8,5120]{2,1,0:T(8,128)(2,1)}), bf16[8,8,5120]{2,1,0:T(8,128)(2,1)S(1)}, u32[]{:S(2)}, u32[]{:S(2)}) async-start(bf16[8,8,5120]{2,1,0:T(8,128)(2,1)} %pad_maximum_fusion), calls=%async_computation | async-start | bytes 1310720 | tf_op jit(solution)/shard_map/all_to_all | solution.py:46
  13.6 19.2 %all_gather.3 = bf16[128,1152]{1,0:T(8,128)(2,1)S(1)} all-gather(bf16[8,1152]{1,0:T(8,128)(2,1)S(1)} %pad_maximum_fusion.1), channel_id=1, replica_groups=mesh['row'=16,'col'=32] {'row'}, dimensions={0}, use_global_device_ids=true | all-gather | bytes 313344 | tf_op jit(solution)/shard_map/all_gather | solution.py:57
  33.4 0.4 copy.27
  34.1 1.1 %reshape.75 = bf16[64,64,64]{2,1,0:T(8,128)(2,1)S(1)} reshape(bf16[64,4096]{1,0:T(8,128)(2,1)S(1)} %copy-done) | data formatting | bytes 1048576 | tf_op jit(solution)/shard_map/reshape | solution.py:61
  35.2 0.6 convolution_bitcast_fusion.2
  36.5 0.9 broadcast_in_dim.15
  37.3 4.0 %all-to-all-start.1 = ((bf16[4,64,1024]{2,1,0:T(8,128)(2,1)}), bf16[4,64,1024]{2,1,0:T(8,128)(2,1)S(1)}, u32[]{:S(2)}, u32[]{:S(2)}) async-start(bf16[4,64,1024]{2,1,0:T(8,128)(2,1)} %broadcast_in_dim.15), calls=%async_computation.1 | async-start | bytes 1048576 | tf_op jit(solution)/shard_map/all_to_all | solution.py:21
  41.5 8.9 %all-to-all-done.1 = bf16[4,64,1024]{2,1,0:T(8,128)(2,1)S(1)} async-done(((bf16[4,64,1024]{2,1,0:T(8,128)(2,1)}), bf16[4,64,1024]{2,1,0:T(8,128)(2,1)S(1)}, u32[]{:S(2)}, u32[]{:S(2)}) %all-to-all-start.1) | async-done | bytes 524320 | tf_op jit(solution)/shard_map/all_to_all | solution.py:21
  51.3 0.6 convolution_bitcast_fusion.1
  52.4 1.4 %convolution_bitcast_fusion = f32[32,8,1024]{2,1,0:T(8,128)} fusion(bf16[64,1024]{0,1:T(8,128)(2,1)S(1)} %get-tuple-element.14, bf16[64,1024]{0,1:T(8,128)(2,1)S(1)} %get-tuple-element.13, pred[256,64]{1,0:T(32,128)(4,1)S(1)} %iota_compare_fusion), kind=kOutput, calls=%fused_computation.4 | convolution fusion | flops 67665920 | bytes 1327104 | tf_op jit(solution)/shard_map/dot_general | solution.py:73
  53.8 7.9 %all-to-all-start.2 = ((f32[32,8,1024]{2,1,0:T(8,128)}), f32[32,8,1024]{2,1,0:T(8,128)S(1)}, u32[]{:S(2)}, u32[]{:S(2)}) async-start(f32[32,8,1024]{2,1,0:T(8,128)} %convolution_bitcast_fusion), calls=%async_computation.2 | async-start | bytes 2097152 | tf_op jit(solution)/shard_map/all_to_all | solution.py:75
  62.0 0.9 slice.24
  62.9 4.4 %collective-permute-start.2 = (bf16[64,4096]{1,0:T(8,128)(2,1)}, bf16[64,4096]{1,0:T(8,128)(2,1)}, u32[]{:S(2)}, u32[]{:S(2)}) collective-permute-start(bf16[64,4096]{1,0:T(8,128)(2,1)} %slice.24), channel_id=1, source_target_pairs={{0,24},{1,25},{2,26},{3,27},{4,28},{5,29},{6,30},{7,31},{8,0},{9,1... | collective-permute-start | bytes 1572872 | tf_op jit(solution)/shard_map/ppermute | solution.py:52
  68.6 2.4 %collective-permute-start.1 = (bf16[64,4096]{1,0:T(8,128)(2,1)}, bf16[64,4096]{1,0:T(8,128)(2,1)S(1)}, u32[]{:S(2)}, u32[]{:S(2)}) collective-permute-start(bf16[64,4096]{1,0:T(8,128)(2,1)} %slice.24), channel_id=1, source_target_pairs={{0,16},{1,17},{2,18},{3,19},{4,20},{5,21},{6,22},{7,23},{8,24},{9,... | collective-permute-start | bytes 1572872 | tf_op jit(solution)/shard_map/ppermute | solution.py:52
  71.1 2.5 %collective-permute-start = (bf16[64,4096]{1,0:T(8,128)(2,1)}, bf16[64,4096]{1,0:T(8,128)(2,1)S(1)}, u32[]{:S(2)}, u32[]{:S(2)}) collective-permute-start(bf16[64,4096]{1,0:T(8,128)(2,1)} %slice.24), channel_id=1, source_target_pairs={{0,8},{1,9},{2,10},{3,11},{4,12},{5,13},{6,14},{7,15},{8,16},{9,17... | collective-permute-start | bytes 1572872 | tf_op jit(solution)/shard_map/ppermute | solution.py:52
  73.9 13.5 %collective-permute-done.2 = bf16[64,4096]{1,0:T(8,128)(2,1)} collective-permute-done((bf16[64,4096]{1,0:T(8,128)(2,1)}, bf16[64,4096]{1,0:T(8,128)(2,1)}, u32[]{:S(2)}, u32[]{:S(2)}) %collective-permute-start.2) | collective-permute-done | bytes 524320 | tf_op jit(solution)/shard_map/ppermute | solution.py:52
  87.4 1.4 %fusion.25 = f32[64,4096]{1,0:T(8,128)S(1)} fusion(bf16[64,4096]{1,0:T(8,128)(2,1)} %collective-permute-done.2, s32[64]{0:T(128)S(1)} %get-tuple-element.22), kind=kOutput, calls=%fused_computation.49 | convolution fusion | flops 33558528 | bytes 1573120 | tf_op jit(solution)/shard_map/dot_general | solution.py:113
  88.8 15.4 %collective-permute-done = bf16[64,4096]{1,0:T(8,128)(2,1)S(1)} collective-permute-done((bf16[64,4096]{1,0:T(8,128)(2,1)}, bf16[64,4096]{1,0:T(8,128)(2,1)S(1)}, u32[]{:S(2)}, u32[]{:S(2)}) %collective-permute-start) | collective-permute-done | bytes 524320 | tf_op jit(solution)/shard_map/ppermute | solution.py:52
  104.8 1.1 %reshape.73 = bf16[64,64,64]{2,1,0:T(8,128)(2,1)S(1)} reshape(bf16[64,4096]{1,0:T(8,128)(2,1)S(1)} %fusion.1) | data formatting | bytes 1048576 | tf_op jit(solution)/shard_map/reshape | solution.py:116
  106.0 0.7 fusion.4
  108.1 1.1 convolution_add_fusion.2
  (57 shorter events, 7.0 us)
Async XLA Ops:
  1.6 11.9 %copy-start.4 = (s32[64]{0:T(128)S(1)}, s32[64]{0:T(128)}, u32[]{:S(2)}) copy-start(s32[64]{0:T(128)} %param.9) | copy-start | bytes 772
  1.6 11.9 %copy-start.6 = (s32[8]{0:T(128)S(1)}, s32[8]{0:T(128)}, u32[]{:S(2)}) copy-start(s32[8]{0:T(128)} %param.12) | copy-start | bytes 100
  1.6 12.0 %copy-start.2 = (bf16[8,1024]{1,0:T(8,128)(2,1)S(1)}, bf16[8,1024]{1,0:T(8,128)(2,1)}, u32[]{:S(2)}) copy-start(bf16[8,1024]{1,0:T(8,128)(2,1)} %param.11) | copy-start | bytes 49156
  2.5 30.5 %copy-start.3 = (s32[64]{0:T(128)S(1)}, s32[64]{0:T(128)}, u32[]{:S(2)}) copy-start(s32[64]{0:T(128)} %param.8) | copy-start | bytes 772
  2.5 30.5 %copy-start.5 = (s32[64]{0:T(128)S(1)}, s32[64]{0:T(128)}, u32[]{:S(2)}) copy-start(s32[64]{0:T(128)} %param.10) | copy-start | bytes 772
  2.5 33.9 %all-to-all-start = ((bf16[8,8,5120]{2,1,0:T(8,128)(2,1)}), bf16[8,8,5120]{2,1,0:T(8,128)(2,1)S(1)}, u32[]{:S(2)}, u32[]{:S(2)}) async-start(bf16[8,8,5120]{2,1,0:T(8,128)(2,1)} %pad_maximum_fusion), calls=%async_computation | async-start | bytes 1310720 | tf_op jit(solution)/shard_map/all_to_all | solution.py:46
  33.1 1.0 copy-start
  37.3 13.1 %all-to-all-start.1 = ((bf16[4,64,1024]{2,1,0:T(8,128)(2,1)}), bf16[4,64,1024]{2,1,0:T(8,128)(2,1)S(1)}, u32[]{:S(2)}, u32[]{:S(2)}) async-start(bf16[4,64,1024]{2,1,0:T(8,128)(2,1)} %broadcast_in_dim.15), calls=%async_computation.1 | async-start | bytes 1048576 | tf_op jit(solution)/shard_map/all_to_all | solution.py:21
  53.8 53.5 %all-to-all-start.2 = ((f32[32,8,1024]{2,1,0:T(8,128)}), f32[32,8,1024]{2,1,0:T(8,128)S(1)}, u32[]{:S(2)}, u32[]{:S(2)}) async-start(f32[32,8,1024]{2,1,0:T(8,128)} %convolution_bitcast_fusion), calls=%async_computation.2 | async-start | bytes 2097152 | tf_op jit(solution)/shard_map/all_to_all | solution.py:75
  61.7 5.6 %copy-start.1 = (bf16[8,4096]{1,0:T(8,128)(2,1)S(1)}, bf16[8,4096]{1,0:T(8,128)(2,1)}, u32[]{:S(2)}) copy-start(bf16[8,4096]{1,0:T(8,128)(2,1)} %param.13) | copy-start | bytes 196612
  62.9 24.5 %collective-permute-start.2 = (bf16[64,4096]{1,0:T(8,128)(2,1)}, bf16[64,4096]{1,0:T(8,128)(2,1)}, u32[]{:S(2)}, u32[]{:S(2)}) collective-permute-start(bf16[64,4096]{1,0:T(8,128)(2,1)} %slice.24), channel_id=1, source_target_pairs={{0,24},{1,25},{2,26},{3,27},{4,28},{5,29},{6,30},{7,31},{8,0},{9,1... | collective-permute-start | bytes 1572872 | tf_op jit(solution)/shard_map/ppermute | solution.py:52
  68.6 35.8 %collective-permute-start.1 = (bf16[64,4096]{1,0:T(8,128)(2,1)}, bf16[64,4096]{1,0:T(8,128)(2,1)S(1)}, u32[]{:S(2)}, u32[]{:S(2)}) collective-permute-start(bf16[64,4096]{1,0:T(8,128)(2,1)} %slice.24), channel_id=1, source_target_pairs={{0,16},{1,17},{2,18},{3,19},{4,20},{5,21},{6,22},{7,23},{8,24},{9,... | collective-permute-start | bytes 1572872 | tf_op jit(solution)/shard_map/ppermute | solution.py:52
  71.1 33.1 %collective-permute-start = (bf16[64,4096]{1,0:T(8,128)(2,1)}, bf16[64,4096]{1,0:T(8,128)(2,1)S(1)}, u32[]{:S(2)}, u32[]{:S(2)}) collective-permute-start(bf16[64,4096]{1,0:T(8,128)(2,1)} %slice.24), channel_id=1, source_target_pairs={{0,8},{1,9},{2,10},{3,11},{4,12},{5,13},{6,14},{7,15},{8,16},{9,17... | collective-permute-start | bytes 1572872 | tf_op jit(solution)/shard_map/ppermute | solution.py:52

commit v4 on v3

--- a/solution.py
+++ b/solution.py
@@ -47,9 +47,19 @@
         jnp.concatenate(copies, axis=2), "col", 0, 0, axis_index_groups=Z_GROUPS, tiled=True
     ).reshape(NZ * per_device, width + inv_diag.shape[1])
     row_panel = spread(both[:, :width], X_GROUPS)
-    inv_parts = [both[:, width:]]
-    for k in (1, 2, 3):
-        inv_parts.append(lax.ppermute(inv_parts[0], "col", shift_x(k)))
+    inv_own = both[:, width:]
+    half = inv_own.shape[0] // 2
+    inv_left = lax.ppermute(inv_own, "col", shift_x(1))
+    inv_right = lax.ppermute(inv_own, "col", shift_x(-1))
+    inv_far_a = lax.ppermute(inv_left[:half], "col", shift_x(1))
+    inv_far_b = lax.ppermute(inv_right[half:], "col", shift_x(-1))
+    inv_parts = (
+        (0, 0, inv_own),
+        (1, 0, inv_left),
+        (3, 0, inv_right),
+        (2, 0, inv_far_a),
+        (2, half, inv_far_b),
+    )
 
     labelled = jnp.concatenate(
         [prolong, jnp.broadcast_to(agg_label.astype(BF16)[:, None], (per_device, 128))], axis=1
@@ -107,10 +117,10 @@
     part_rows = NZ * per_device
     row_x = local_row // part_rows
     inverse = None
-    for k in (0, 1, 2, 3):
-        at = jnp.where((col_index // NZ - row_x) % NX == k, local_row % part_rows, -1)
-        pick = (at[:, None] == jnp.arange(part_rows)[None, :]).astype(BF16)
-        piece = jnp.dot(pick, inv_parts[k], preferred_element_type=F32)
+    for distance, first_row, rows in inv_parts:
+        at = jnp.where((col_index // NZ - row_x) % NX == distance, local_row % part_rows, -1)
+        pick = (at[:, None] == first_row + jnp.arange(rows.shape[0])[None, :]).astype(BF16)
+        piece = jnp.dot(pick, rows, preferred_element_type=F32)
         inverse = piece if inverse is None else inverse + piece
     inverse = inverse.astype(BF16)
     inverse = inverse.reshape(slot_count, BS, BS)

time: 110 us -> 94.2 us (0.86)
  the two profiles are of different devices: /device:TPU:1 before, /device:TPU:64 now
where the time goes in v4:
time: 94.2 us; the launch traced here: 93.5 us
  starting transfers between devices  35.7 us (38%)
  blocking collectives  18.5 us (20%)
  waiting for transfers between devices  17.3 us (18%)
  local copies, waits for them, and re-layouts  11.7 us (12%)
  matrix products  8.26 us (9%)
  other arithmetic  1.5 us (2%)
    all_gather x1, blocking collectives, body(): col_panel = lax.all_gather(labelled, 'row', axis=0, tiled=True)  18.5 us
    all_to_all x1, starting transfers between devices, body(): lax.all_to_all(jnp.concatenate(copies, axis=2), 'col', 0, 0, axis_index_g...  9.96 us
    all_to_all x1, starting transfers between devices, body(): arrived = lax.all_to_all(sums, 'col', 0, 0, tiled=True)  7.36 us
    ppermute x1, waiting for transfers between devices, body(): inv_far_a = lax.ppermute(inv_left[:half], 'col', shift_x(1))  6.92 us
    all_to_all x1, waiting for transfers between devices, body(): arrived = lax.all_to_all(sums, 'col', 0, 0, tiled=True)  5.89 us
    all_to_all x1, starting transfers between devices, spread(): lax.all_to_all(copies, 'col', 0, 0, axis_index_groups=groups, tiled=True)  4.29 us
    ppermute x1, starting transfers between devices, body(): inv_left = lax.ppermute(inv_own, 'col', shift_x(1))  3.92 us
    ppermute x1, starting transfers between devices, body(): inv_far_b = lax.ppermute(inv_right[half:], 'col', shift_x(-1))  3.69 us
  transfers between devices with their start and end apart: 7, of which 4 were waited for; matrix products, arithmetic and copies ran while one was open for 17% of the time, Pallas kernels for 0%

profile of v4, /device:TPU:64, one launch (start us, length us, event | category | flops | bytes accessed | tf_op | source)
XLA Modules:
  0.0 93.5 jit_solution(2774201891629387724)
XLA Ops:
  0.0 0.9 broadcast_in_dim.14
  0.9 0.7 broadcast_in_dim.13
  1.7 0.9 pad_maximum_fusion
  2.6 10.0 %all-to-all-start = ((bf16[8,8,5120]{2,1,0:T(8,128)(2,1)}), bf16[8,8,5120]{2,1,0:T(8,128)(2,1)S(1)}, u32[]{:S(2)}, u32[]{:S(2)}) async-start(bf16[8,8,5120]{2,1,0:T(8,128)(2,1)} %pad_maximum_fusion), calls=%async_computation | async-start | bytes 1310720 | tf_op jit(solution)/shard_map/all_to_all | solution.py:46
  12.7 18.5 %all_gather.3 = bf16[128,1152]{1,0:T(8,128)(2,1)S(1)} all-gather(bf16[8,1152]{1,0:T(8,128)(2,1)S(1)} %pad_maximum_fusion.1), channel_id=1, replica_groups=mesh['row'=16,'col'=32] {'row'}, dimensions={0}, use_global_device_ids=true | all-gather | bytes 313344 | tf_op jit(solution)/shard_map/all_gather | solution.py:67
  32.1 1.1 %reshape.80 = bf16[64,64,64]{2,1,0:T(8,128)(2,1)S(1)} reshape(bf16[64,4096]{1,0:T(8,128)(2,1)S(1)} %copy-done.1) | data formatting | bytes 1048576 | tf_op jit(solution)/shard_map/reshape | solution.py:71
  36.0 1.1 %copy.32 = bf16[64,64,16]{1,2,0:T(8,128)(2,1)} copy(bf16[64,64,16]{0,2,1:T(8,128)(2,1)S(1)} %bitcast.42) | data formatting | bytes 262144 | tf_op jit(solution)/shard_map/reshape | solution.py:127
  37.1 0.9 broadcast_in_dim.16
  38.0 4.3 %all-to-all-start.1 = ((bf16[4,64,1024]{2,1,0:T(8,128)(2,1)}), bf16[4,64,1024]{2,1,0:T(8,128)(2,1)S(1)}, u32[]{:S(2)}, u32[]{:S(2)}) async-start(bf16[4,64,1024]{2,1,0:T(8,128)(2,1)} %broadcast_in_dim.16), calls=%async_computation.1 | async-start | bytes 1048576 | tf_op jit(solution)/shard_map/all_to_all | solution.py:21
  42.3 0.9 slice.32
  43.2 3.9 %collective-permute-start = (bf16[64,4096]{1,0:T(8,128)(2,1)}, bf16[64,4096]{1,0:T(8,128)(2,1)}, u32[]{:S(2)}, u32[]{:S(2)}) collective-permute-start(bf16[64,4096]{1,0:T(8,128)(2,1)} %slice.32), channel_id=1, source_target_pairs={{0,8},{1,9},{2,10},{3,11},{4,12},{5,13},{6,14},{7,15},{8,16},{9,17... | collective-permute-start | bytes 1572872 | tf_op jit(solution)/shard_map/ppermute | solution.py:52
  47.1 3.1 %collective-permute-start.1 = (bf16[64,4096]{1,0:T(8,128)(2,1)}, bf16[64,4096]{1,0:T(8,128)(2,1)S(1)}, u32[]{:S(2)}, u32[]{:S(2)}) collective-permute-start(bf16[64,4096]{1,0:T(8,128)(2,1)} %slice.32), channel_id=1, source_target_pairs={{0,24},{1,25},{2,26},{3,27},{4,28},{5,29},{6,30},{7,31},{8,0},{9,1... | collective-permute-start | bytes 1572872 | tf_op jit(solution)/shard_map/ppermute | solution.py:53
  50.2 3.0 %all-to-all-done.1 = bf16[4,64,1024]{2,1,0:T(8,128)(2,1)S(1)} async-done(((bf16[4,64,1024]{2,1,0:T(8,128)(2,1)}), bf16[4,64,1024]{2,1,0:T(8,128)(2,1)S(1)}, u32[]{:S(2)}, u32[]{:S(2)}) %all-to-all-start.1) | async-done | bytes 524320 | tf_op jit(solution)/shard_map/all_to_all | solution.py:21
  55.2 1.4 %convolution_bitcast_fusion = f32[32,8,1024]{2,1,0:T(8,128)} fusion(bf16[64,1024]{0,1:T(8,128)(2,1)S(1)} %get-tuple-element.14, bf16[64,1024]{0,1:T(8,128)(2,1)S(1)} %get-tuple-element.13, pred[256,64]{1,0:T(32,128)(4,1)S(1)} %iota_compare_fusion), kind=kOutput, calls=%fused_computation.5 | convolution fusion | flops 67665920 | bytes 1327104 | tf_op jit(solution)/shard_map/dot_general | solution.py:83
  56.5 7.4 %all-to-all-start.2 = ((f32[32,8,1024]{2,1,0:T(8,128)}), f32[32,8,1024]{2,1,0:T(8,128)S(1)}, u32[]{:S(2)}, u32[]{:S(2)}) async-start(f32[32,8,1024]{2,1,0:T(8,128)} %convolution_bitcast_fusion), calls=%async_computation.2 | async-start | bytes 2097152 | tf_op jit(solution)/shard_map/all_to_all | solution.py:85
  64.3 1.0 %slice.33 = bf16[32,4096]{1,0:T(8,128)(2,1)S(1)} slice(bf16[64,4096]{1,0:T(8,128)(2,1)} %collective-permute-done), slice={[0:32], [0:4096]} | slice | bytes 524288 | tf_op jit(solution)/shard_map/slice | solution.py:54
  65.2 3.4 %collective-permute-start.2 = (bf16[32,4096]{1,0:T(8,128)(2,1)S(1)}, bf16[32,4096]{1,0:T(8,128)(2,1)S(1)}, u32[]{:S(2)}, u32[]{:S(2)}) collective-permute-start(bf16[32,4096]{1,0:T(8,128)(2,1)S(1)} %slice.33), channel_id=1, source_target_pairs={{0,8},{1,9},{2,10},{3,11},{4,12},{5,13},{6,14},{7,15},{8,16},{9,17... | collective-permute-start | bytes 786440 | tf_op jit(solution)/shard_map/ppermute | solution.py:54
  68.7 3.7 %collective-permute-start.3 = (bf16[32,4096]{1,0:T(8,128)(2,1)S(1)}, bf16[32,4096]{1,0:T(8,128)(2,1)S(1)}, u32[]{:S(2)}, u32[]{:S(2)}) collective-permute-start(bf16[32,4096]{1,0:T(8,128)(2,1)S(1)} %slice.34), channel_id=1, source_target_pairs={{0,24},{1,25},{2,26},{3,27},{4,28},{5,29},{6,30},{7,31},{8,0},{9,1... | collective-permute-start | bytes 786440 | tf_op jit(solution)/shard_map/ppermute | solution.py:55
  72.4 1.4 %convolution_add_fusion.1 = f32[64,4096]{1,0:T(8,128)S(1)} fusion(f32[64,4096]{1,0:T(8,128)S(1)} %fusion.25, bf16[64,4096]{1,0:T(8,128)(2,1)} %collective-permute-done, s32[64]{0:T(128)S(1)} %get-tuple-element.21), kind=kOutput, calls=%fused_computation.1 | convolution fusion | flops 33820672 | bytes 2621696 | tf_op jit(solution)/shard_map/dot_general | solution.py:123
  73.7 6.9 %collective-permute-done.2 = bf16[32,4096]{1,0:T(8,128)(2,1)S(1)} collective-permute-done((bf16[32,4096]{1,0:T(8,128)(2,1)S(1)}, bf16[32,4096]{1,0:T(8,128)(2,1)S(1)}, u32[]{:S(2)}, u32[]{:S(2)}) %collective-permute-start.2) | collective-permute-done | bytes 262176 | tf_op jit(solution)/shard_map/ppermute | solution.py:54
  81.0 1.5 %collective-permute-done.3 = bf16[32,4096]{1,0:T(8,128)(2,1)S(1)} collective-permute-done((bf16[32,4096]{1,0:T(8,128)(2,1)S(1)}, bf16[32,4096]{1,0:T(8,128)(2,1)S(1)}, u32[]{:S(2)}, u32[]{:S(2)}) %collective-permute-start.3) | collective-permute-done | bytes 262176 | tf_op jit(solution)/shard_map/ppermute | solution.py:55
  83.2 1.1 %reshape.78 = bf16[64,64,64]{2,1,0:T(8,128)(2,1)S(1)} reshape(bf16[64,4096]{1,0:T(8,128)(2,1)S(1)} %fusion.2) | data formatting | bytes 1048576 | tf_op jit(solution)/shard_map/reshape | solution.py:126
  85.6 5.9 %all-to-all-done.2 = f32[32,8,1024]{2,1,0:T(8,128)S(1)} async-done(((f32[32,8,1024]{2,1,0:T(8,128)}), f32[32,8,1024]{2,1,0:T(8,128)S(1)}, u32[]{:S(2)}, u32[]{:S(2)}) %all-to-all-start.2) | async-done | bytes 1048608 | tf_op jit(solution)/shard_map/all_to_all | solution.py:85
  92.4 1.1 %convolution_add_fusion.2 = f32[64,1024]{1,0:T(8,128)} fusion(f32[64,1024]{1,0:T(8,128)S(1)} %copy.39, f32[8,1024]{1,0:T(8,128)S(1)} %reshape.91, f32[64]{0:T(128)S(1)} %slice_reduce_fusion, s32[64]{0:T(128)S(1)} %copy-done.4, f32[8]{0:T(128)S(1)} %get-tuple-element.24, s32[8]{0:T(128)S(1)} %iota_add_fusion, pred[64]{0:T(512)(128)(4,1)S(1)} %get-tuple-element.5), kind=kOutput, calls=%fused_computation.8 | convolution fusion | flops 6359040 | bytes 557696 | tf_op jit(solution)/shard_map/dot_general | solution.py:138
  (65 shorter events, 9.2 us)
Async XLA Ops:
  1.6 10.9 %copy-start.5 = (s32[64]{0:T(128)S(1)}, s32[64]{0:T(128)}, u32[]{:S(2)}) copy-start(s32[64]{0:T(128)} %param.9) | copy-start | bytes 772
  1.6 10.9 %copy-start.4 = (s32[64]{0:T(128)S(1)}, s32[64]{0:T(128)}, u32[]{:S(2)}) copy-start(s32[64]{0:T(128)} %param.8) | copy-start | bytes 772
  1.6 10.9 %copy-start.6 = (s32[64]{0:T(128)S(1)}, s32[64]{0:T(128)}, u32[]{:S(2)}) copy-start(s32[64]{0:T(128)} %param.10) | copy-start | bytes 772
  1.6 11.0 %copy-start.7 = (s32[8]{0:T(128)S(1)}, s32[8]{0:T(128)}, u32[]{:S(2)}) copy-start(s32[8]{0:T(128)} %param.12) | copy-start | bytes 100
  1.7 11.0 %copy-start.3 = (bf16[8,1024]{1,0:T(8,128)(2,1)S(1)}, bf16[8,1024]{1,0:T(8,128)(2,1)}, u32[]{:S(2)}) copy-start(bf16[8,1024]{1,0:T(8,128)(2,1)} %param.11) | copy-start | bytes 49156
  2.6 34.5 %all-to-all-start = ((bf16[8,8,5120]{2,1,0:T(8,128)(2,1)}), bf16[8,8,5120]{2,1,0:T(8,128)(2,1)S(1)}, u32[]{:S(2)}, u32[]{:S(2)}) async-start(bf16[8,8,5120]{2,1,0:T(8,128)(2,1)} %pad_maximum_fusion), calls=%async_computation | async-start | bytes 1310720 | tf_op jit(solution)/shard_map/all_to_all | solution.py:46
  12.7 19.4 %copy-start.1 = (bf16[64,4096]{1,0:T(8,128)(2,1)S(1)}, bf16[64,4096]{1,0:T(8,128)(2,1)}, u32[]{:S(2)}) copy-start(bf16[64,4096]{1,0:T(8,128)(2,1)} %param.7) | copy-start | bytes 1572868
  33.3 0.8 copy-start.2
  38.0 15.2 %all-to-all-start.1 = ((bf16[4,64,1024]{2,1,0:T(8,128)(2,1)}), bf16[4,64,1024]{2,1,0:T(8,128)(2,1)S(1)}, u32[]{:S(2)}, u32[]{:S(2)}) async-start(bf16[4,64,1024]{2,1,0:T(8,128)(2,1)} %broadcast_in_dim.16), calls=%async_computation.1 | async-start | bytes 1048576 | tf_op jit(solution)/shard_map/all_to_all | solution.py:21
  43.2 21.1 %collective-permute-start = (bf16[64,4096]{1,0:T(8,128)(2,1)}, bf16[64,4096]{1,0:T(8,128)(2,1)}, u32[]{:S(2)}, u32[]{:S(2)}) collective-permute-start(bf16[64,4096]{1,0:T(8,128)(2,1)} %slice.32), channel_id=1, source_target_pairs={{0,8},{1,9},{2,10},{3,11},{4,12},{5,13},{6,14},{7,15},{8,16},{9,17... | collective-permute-start | bytes 1572872 | tf_op jit(solution)/shard_map/ppermute | solution.py:52
  47.1 21.5 %collective-permute-start.1 = (bf16[64,4096]{1,0:T(8,128)(2,1)}, bf16[64,4096]{1,0:T(8,128)(2,1)S(1)}, u32[]{:S(2)}, u32[]{:S(2)}) collective-permute-start(bf16[64,4096]{1,0:T(8,128)(2,1)} %slice.32), channel_id=1, source_target_pairs={{0,24},{1,25},{2,26},{3,27},{4,28},{5,29},{6,30},{7,31},{8,0},{9,1... | collective-permute-start | bytes 1572872 | tf_op jit(solution)/shard_map/ppermute | solution.py:53
  56.5 35.0 %all-to-all-start.2 = ((f32[32,8,1024]{2,1,0:T(8,128)}), f32[32,8,1024]{2,1,0:T(8,128)S(1)}, u32[]{:S(2)}, u32[]{:S(2)}) async-start(f32[32,8,1024]{2,1,0:T(8,128)} %convolution_bitcast_fusion), calls=%async_computation.2 | async-start | bytes 2097152 | tf_op jit(solution)/shard_map/all_to_all | solution.py:85
  65.2 15.4 %collective-permute-start.2 = (bf16[32,4096]{1,0:T(8,128)(2,1)S(1)}, bf16[32,4096]{1,0:T(8,128)(2,1)S(1)}, u32[]{:S(2)}, u32[]{:S(2)}) collective-permute-start(bf16[32,4096]{1,0:T(8,128)(2,1)S(1)} %slice.33), channel_id=1, source_target_pairs={{0,8},{1,9},{2,10},{3,11},{4,12},{5,13},{6,14},{7,15},{8,16},{9,17... | collective-permute-start | bytes 786440 | tf_op jit(solution)/shard_map/ppermute | solution.py:54
  68.7 13.8 %collective-permute-start.3 = (bf16[32,4096]{1,0:T(8,128)(2,1)S(1)}, bf16[32,4096]{1,0:T(8,128)(2,1)S(1)}, u32[]{:S(2)}, u32[]{:S(2)}) collective-permute-start(bf16[32,4096]{1,0:T(8,128)(2,1)S(1)} %slice.34), channel_id=1, source_target_pairs={{0,24},{1,25},{2,26},{3,27},{4,28},{5,29},{6,30},{7,31},{8,0},{9,1... | collective-permute-start | bytes 786440 | tf_op jit(solution)/shard_map/ppermute | solution.py:55
  83.2 1.1 %copy-start = (bf16[64,64,16]{1,2,0:T(8,128)(2,1)S(1)}, bf16[64,64,16]{1,2,0:T(8,128)(2,1)}, u32[]{:S(2)}) copy-start(bf16[64,64,16]{1,2,0:T(8,128)(2,1)} %copy.32) | copy-start | bytes 393220

commit v5 on v4

--- a/solution.py
+++ b/solution.py
@@ -42,10 +42,18 @@
     panel_first = row_index * span
     own_first = panel_first + col_index * per_device
 
-    copies = [jnp.broadcast_to(part[None], (NZ,) + part.shape) for part in (prolong, inv_diag)]
-    both = lax.all_to_all(
-        jnp.concatenate(copies, axis=2), "col", 0, 0, axis_index_groups=Z_GROUPS, tiled=True
-    ).reshape(NZ * per_device, width + inv_diag.shape[1])
+    both = spread(jnp.concatenate([prolong, inv_diag], axis=1), Z_GROUPS)
+
+    labelled = jnp.concatenate(
+        [prolong, jnp.broadcast_to(agg_label.astype(BF16)[:, None], (per_device, 128))], axis=1
+    )
+    col_panel = lax.all_gather(labelled, "row", axis=0, tiled=True)
+
+    both, col_panel, a_blocks, blk_row, blk_col, drop_mask, own_label, own_inv = (
+        lax.optimization_barrier(
+            (both, col_panel, a_blocks, blk_row, blk_col, drop_mask, agg_label, inv_diag)
+        )
+    )
     row_panel = spread(both[:, :width], X_GROUPS)
     inv_own = both[:, width:]
     half = inv_own.shape[0] // 2
@@ -60,11 +68,6 @@
         (2, 0, inv_far_a),
         (2, half, inv_far_b),
     )
-
-    labelled = jnp.concatenate(
-        [prolong, jnp.broadcast_to(agg_label.astype(BF16)[:, None], (per_device, 128))], axis=1
-    )
-    col_panel = lax.all_gather(labelled, "row", axis=0, tiled=True)
 
     keep = (drop_mask == 1) | (blk_row == blk_col)
     local_row = blk_row - panel_first
@@ -86,7 +89,7 @@
     lumped = jnp.sum(arrived.reshape(col_count, per_device, width), axis=0)
     scaled_lumped = jnp.einsum(
         "eij,ejk->eik",
-        inv_diag.astype(F32).reshape(per_device, BS, BS),
+        own_inv.astype(F32).reshape(per_device, BS, BS),
         lumped.reshape(per_device, BS, PC),
         precision=HIGHEST,
     ).reshape(per_device, width)
@@ -119,7 +122,7 @@
     inverse = None
     for distance, first_row, rows in inv_parts:
         at = jnp.where((col_index // NZ - row_x) % NX == distance, local_row % part_rows, -1)
-        pick = (at[:, None] == first_row + jnp.arange(rows.shape[0])[None, :]).astype(BF16)
+        pick = ((at - first_row)[:, None] == jnp.arange(rows.shape[0])[None, :]).astype(BF16)
         piece = jnp.dot(pick, rows, preferred_element_type=F32)
         inverse = piece if inverse is None else inverse + piece
     inverse = inverse.astype(BF16)
@@ -133,9 +136,13 @@
     target = (
         (blk_row[:, None] == own_first + jnp.arange(per_device)[None, :])
         & (col_run == row_run)[:, None]
-        & (col_label[:, None] == agg_label.astype(F32)[None, :])
+        & (col_label[:, None] == own_label.astype(F32)[None, :])
     )
-    return coarse + jnp.dot(target.astype(F32), scaled_lumped, precision=HIGHEST)
+    target = target.astype(BF16)
+    parts = jnp.concatenate(two_parts(scaled_lumped), axis=0)
+    return coarse + jnp.dot(
+        jnp.concatenate([target, target], axis=1), parts, preferred_element_type=F32
+    )
 
 
 def solution(mesh):

time: 94.2 us -> 102 us (1.083)
  local copies, waits for them, and re-layouts: 11.7 us -> 15.7 us
  other arithmetic: 1.5 us -> 4.42 us
  starting transfers between devices: 35.7 us -> 38.3 us
  waiting for transfers between devices: 17.3 us -> 15.2 us
    all_to_all x1 -> x0, starting transfers between devices: 9.96 us -> none  [body(): lax.all_to_all(jnp.concatenate(copies, axis=2), 'col', 0, 0, axis_index_g...]
    all_to_all x1 -> x2, starting transfers between devices: 4.29 us -> 13.6 us  [spread(): lax.all_to_all(copies, 'col', 0, 0, axis_index_groups=groups, tiled=True)]
    all_to_all x1, waiting for transfers between devices: 5.89 us -> 2.06 us  [body(): arrived = lax.all_to_all(sums, 'col', 0, 0, tiled=True)]
    unnamed x16 -> x32, local copies, waits for them, and re-layouts: 0.24 us -> 4.03 us
    all_to_all x1, starting transfers between devices: 7.36 us -> 10.5 us  [body(): arrived = lax.all_to_all(sums, 'col', 0, 0, tiled=True)]
    all_to_all x1 -> x2, waiting for transfers between devices: 2.99 us -> 5.41 us  [spread(): lax.all_to_all(copies, 'col', 0, 0, axis_index_groups=groups, tiled=True)]
    broadcast_in_dim x2 -> x0, local copies, waits for them, and re-layouts: 1.6 us -> none  [body(): jnp.broadcast_to(part[None], (NZ,) + part.shape)]
    ppermute x1, waiting for transfers between devices: 6.92 us -> 5.57 us  [body(): inv_far_a = lax.ppermute(inv_left[:half], 'col', shift_x(1))]
  transfers between devices with their start and end apart: 7 -> 7, of which waited for: 4 -> 4; matrix products, arithmetic and copies ran while one was open for 17% -> 21% of each run, Pallas kernels for 0% -> 0%
where the time goes in v5:
time: 102 us; the launch traced here: 101 us
  starting transfers between devices  38.3 us (38%)
  blocking collectives  18.4 us (18%)
  local copies, waits for them, and re-layouts  15.7 us (15%)
  waiting for transfers between devices  15.2 us (15%)
  matrix products  9.07 us (9%)
  other arithmetic  4.42 us (4%)
    all_gather x1, blocking collectives, body(): col_panel = lax.all_gather(labelled, 'row', axis=0, tiled=True)  18.4 us
    all_to_all x2, starting transfers between devices, spread(): lax.all_to_all(copies, 'col', 0, 0, axis_index_groups=groups, tiled=True)  13.6 us
    all_to_all x1, starting transfers between devices, body(): arrived = lax.all_to_all(sums, 'col', 0, 0, tiled=True)  10.5 us
    ppermute x1, waiting for transfers between devices, body(): inv_far_a = lax.ppermute(inv_left[:half], 'col', shift_x(1))  5.57 us
    all_to_all x2, waiting for transfers between devices, spread(): lax.all_to_all(copies, 'col', 0, 0, axis_index_groups=groups, tiled=True)  5.41 us
    unnamed x32, local copies, waits for them, and re-layouts  4.03 us
    dot_general x5, matrix products, body(): piece = jnp.dot(pick, rows, preferred_element_type=F32)  3.78 us
    ppermute x1, starting transfers between devices, body(): inv_far_b = lax.ppermute(inv_right[half:], 'col', shift_x(-1))  3.67 us
  transfers between devices with their start and end apart: 7, of which 4 were waited for; matrix products, arithmetic and copies ran while one was open for 21% of the time, Pallas kernels for 0%

profile of v5, /device:TPU:64, one launch (start us, length us, event | category | flops | bytes accessed | tf_op | source)
XLA Modules:
  0.0 101.4 jit_solution(5717433028904207810)
XLA Ops:
  0.0 0.8 pad_maximum_fusion
  0.8 0.9 broadcast_in_dim.11
  1.7 10.0 %all-to-all-start = ((bf16[8,8,5120]{2,1,0:T(8,128)(2,1)}), bf16[8,8,5120]{2,1,0:T(8,128)(2,1)S(1)}, u32[]{:S(2)}, u32[]{:S(2)}) async-start(bf16[8,8,5120]{2,1,0:T(8,128)(2,1)} %broadcast_in_dim.11), calls=%async_computation | async-start | bytes 1310720 | tf_op jit(solution)/shard_map/all_to_all | solution.py:21
  12.4 18.4 %all_gather.3 = bf16[128,1152]{1,0:T(8,128)(2,1)S(1)} all-gather(bf16[8,1152]{1,0:T(8,128)(2,1)S(1)} %pad_maximum_fusion.1), channel_id=1, replica_groups=mesh['row'=16,'col'=32] {'row'}, dimensions={0}, use_global_device_ids=true | all-gather | bytes 313344 | tf_op jit(solution)/shard_map/all_gather | solution.py:50
  31.7 3.5 %collective-permute-start = (bf16[64,4096]{1,0:T(8,128)(2,1)}, bf16[64,4096]{1,0:T(8,128)(2,1)}, u32[]{:S(2)}, u32[]{:S(2)}) collective-permute-start(bf16[64,4096]{1,0:T(8,128)(2,1)} %slice.24), channel_id=1, source_target_pairs={{0,8},{1,9},{2,10},{3,11},{4,12},{5,13},{6,14},{7,15},{8,16},{9,17... | collective-permute-start | bytes 1572872 | tf_op jit(solution)/shard_map/ppermute | solution.py:60
  35.2 3.7 %collective-permute-start.1 = (bf16[64,4096]{1,0:T(8,128)(2,1)}, bf16[64,4096]{1,0:T(8,128)(2,1)}, u32[]{:S(2)}, u32[]{:S(2)}) collective-permute-start(bf16[64,4096]{1,0:T(8,128)(2,1)} %slice.24), channel_id=1, source_target_pairs={{0,24},{1,25},{2,26},{3,27},{4,28},{5,29},{6,30},{7,31},{8,0},{9,1... | collective-permute-start | bytes 1572872 | tf_op jit(solution)/shard_map/ppermute | solution.py:61
  40.1 0.9 broadcast_in_dim.13
  41.0 3.6 %all-to-all-start.1 = ((bf16[4,64,1024]{2,1,0:T(8,128)(2,1)}), bf16[4,64,1024]{2,1,0:T(8,128)(2,1)S(1)}, u32[]{:S(2)}, u32[]{:S(2)}) async-start(bf16[4,64,1024]{2,1,0:T(8,128)(2,1)} %broadcast_in_dim.13), calls=%async_computation.1 | async-start | bytes 1048576 | tf_op jit(solution)/shard_map/all_to_all | solution.py:21
  44.6 1.1 %reshape.74 = bf16[64,64,64]{2,1,0:T(8,128)(2,1)S(1)} reshape(bf16[64,4096]{1,0:T(8,128)(2,1)S(1)} %copy-done.1) | data formatting | bytes 1048576 | tf_op jit(solution)/shard_map/reshape | solution.py:74
  46.4 0.8 reshape.80
  50.8 5.4 %all-to-all-done.1 = bf16[4,64,1024]{2,1,0:T(8,128)(2,1)S(1)} async-done(((bf16[4,64,1024]{2,1,0:T(8,128)(2,1)}), bf16[4,64,1024]{2,1,0:T(8,128)(2,1)S(1)}, u32[]{:S(2)}, u32[]{:S(2)}) %all-to-all-start.1) | async-done | bytes 524320 | tf_op jit(solution)/shard_map/all_to_all | solution.py:21
  59.4 1.4 %convolution_bitcast_fusion = f32[32,8,1024]{2,1,0:T(8,128)} fusion(bf16[64,1024]{0,1:T(8,128)(2,1)S(1)} %get-tuple-element.32, bf16[64,1024]{0,1:T(8,128)(2,1)S(1)} %get-tuple-element.31, pred[256,64]{1,0:T(32,128)(4,1)S(1)} %copy-done.4), kind=kOutput, calls=%fused_computation.5 | convolution fusion | flops 67665920 | bytes 1327104 | tf_op jit(solution)/shard_map/dot_general | solution.py:86
  60.8 10.5 %all-to-all-start.2 = ((f32[32,8,1024]{2,1,0:T(8,128)}), f32[32,8,1024]{2,1,0:T(8,128)S(1)}, u32[]{:S(2)}, u32[]{:S(2)}) async-start(f32[32,8,1024]{2,1,0:T(8,128)} %convolution_bitcast_fusion), calls=%async_computation.2 | async-start | bytes 2097152 | tf_op jit(solution)/shard_map/all_to_all | solution.py:88
  73.7 1.0 slice.32
  74.7 3.4 %collective-permute-start.2 = (bf16[32,4096]{1,0:T(8,128)(2,1)S(1)}, bf16[32,4096]{1,0:T(8,128)(2,1)S(1)}, u32[]{:S(2)}, u32[]{:S(2)}) collective-permute-start(bf16[32,4096]{1,0:T(8,128)(2,1)S(1)} %slice.32), channel_id=1, source_target_pairs={{0,8},{1,9},{2,10},{3,11},{4,12},{5,13},{6,14},{7,15},{8,16},{9,17... | collective-permute-start | bytes 786440 | tf_op jit(solution)/shard_map/ppermute | solution.py:62
  78.1 1.0 slice.33
  79.1 3.7 %collective-permute-start.3 = (bf16[32,4096]{1,0:T(8,128)(2,1)S(1)}, bf16[32,4096]{1,0:T(8,128)(2,1)S(1)}, u32[]{:S(2)}, u32[]{:S(2)}) collective-permute-start(bf16[32,4096]{1,0:T(8,128)(2,1)S(1)} %slice.33), channel_id=1, source_target_pairs={{0,24},{1,25},{2,26},{3,27},{4,28},{5,29},{6,30},{7,31},{8,0},{9,1... | collective-permute-start | bytes 786440 | tf_op jit(solution)/shard_map/ppermute | solution.py:63
  82.8 1.4 %convolution_add_fusion.1 = f32[64,4096]{1,0:T(8,128)S(1)} fusion(f32[64,4096]{1,0:T(8,128)S(1)} %fusion.29, bf16[64,4096]{1,0:T(8,128)(2,1)} %collective-permute-done, s32[64]{0:T(128)S(1)} %copy-done.12), kind=kOutput, calls=%fused_computation.1 | convolution fusion | flops 33820672 | bytes 2621696 | tf_op jit(solution)/shard_map/dot_general | solution.py:126
  84.2 5.6 %collective-permute-done.2 = bf16[32,4096]{1,0:T(8,128)(2,1)S(1)} collective-permute-done((bf16[32,4096]{1,0:T(8,128)(2,1)S(1)}, bf16[32,4096]{1,0:T(8,128)(2,1)S(1)}, u32[]{:S(2)}, u32[]{:S(2)}) %collective-permute-start.2) | collective-permute-done | bytes 262176 | tf_op jit(solution)/shard_map/ppermute | solution.py:62
  90.1 2.2 %collective-permute-done.3 = bf16[32,4096]{1,0:T(8,128)(2,1)S(1)} collective-permute-done((bf16[32,4096]{1,0:T(8,128)(2,1)S(1)}, bf16[32,4096]{1,0:T(8,128)(2,1)S(1)}, u32[]{:S(2)}, u32[]{:S(2)}) %collective-permute-start.3) | collective-permute-done | bytes 262176 | tf_op jit(solution)/shard_map/ppermute | solution.py:63
  93.2 1.4 %fusion.2 = bf16[64,4096]{1,0:T(8,128)(2,1)S(1)} fusion(f32[64,4096]{1,0:T(8,128)S(1)} %fusion.31, f32[64,4096]{1,0:T(8,128)S(1)} %fusion.30, f32[64,4096]{1,0:T(8,128)S(1)} %convolution_add_fusion.1, bf16[64,4096]{1,0:T(8,128)(2,1)} %collective-permute-done.1, s32[64]{0:T(128)S(1)} %copy-done.7), kind=kOutput, calls=%fused_computation.4 | convolution fusion | flops 34607104 | bytes 4194560 | tf_op jit(solution)/shard_map/dot_general | solution.py:126
  94.6 1.1 %reshape.73 = bf16[64,64,64]{2,1,0:T(8,128)(2,1)S(1)} reshape(bf16[64,4096]{1,0:T(8,128)(2,1)S(1)} %fusion.2) | data formatting | bytes 1048576 | tf_op jit(solution)/shard_map/reshape | solution.py:129
  97.0 2.1 %all-to-all-done.2 = f32[32,8,1024]{2,1,0:T(8,128)S(1)} async-done(((f32[32,8,1024]{2,1,0:T(8,128)}), f32[32,8,1024]{2,1,0:T(8,128)S(1)}, u32[]{:S(2)}, u32[]{:S(2)}) %all-to-all-start.2) | async-done | bytes 1048608 | tf_op jit(solution)/shard_map/all_to_all | solution.py:88
  100.5 0.9 convolution_add_fusion.2
  (81 shorter events, 16.4 us)
Async XLA Ops:
  1.7 29.1 %all-to-all-start = ((bf16[8,8,5120]{2,1,0:T(8,128)(2,1)}), bf16[8,8,5120]{2,1,0:T(8,128)(2,1)S(1)}, u32[]{:S(2)}, u32[]{:S(2)}) async-start(bf16[8,8,5120]{2,1,0:T(8,128)(2,1)} %broadcast_in_dim.11), calls=%async_computation | async-start | bytes 1310720 | tf_op jit(solution)/shard_map/all_to_all | solution.py:21
  11.7 0.7 copy-start.15
  11.7 0.7 copy-start.5
  30.8 8.0 %copy-start.13 = (s32[64]{0:T(128)S(1)}, s32[64]{0:T(128)}, u32[]{:S(2)}) copy-start(s32[64]{0:T(128)} %param.9) | copy-start | bytes 772
  31.7 7.2 %copy-start.6 = (s32[64]{0:T(128)S(1)}, s32[64]{0:T(128)}, u32[]{:S(2)}) copy-start(s32[64]{0:T(128)} %param.8) | copy-start | bytes 772
  31.7 42.0 %collective-permute-start = (bf16[64,4096]{1,0:T(8,128)(2,1)}, bf16[64,4096]{1,0:T(8,128)(2,1)}, u32[]{:S(2)}, u32[]{:S(2)}) collective-permute-start(bf16[64,4096]{1,0:T(8,128)(2,1)} %slice.24), channel_id=1, source_target_pairs={{0,8},{1,9},{2,10},{3,11},{4,12},{5,13},{6,14},{7,15},{8,16},{9,17... | collective-permute-start | bytes 1572872 | tf_op jit(solution)/shard_map/ppermute | solution.py:60
  35.2 42.9 %collective-permute-start.1 = (bf16[64,4096]{1,0:T(8,128)(2,1)}, bf16[64,4096]{1,0:T(8,128)(2,1)}, u32[]{:S(2)}, u32[]{:S(2)}) collective-permute-start(bf16[64,4096]{1,0:T(8,128)(2,1)} %slice.24), channel_id=1, source_target_pairs={{0,24},{1,25},{2,26},{3,27},{4,28},{5,29},{6,30},{7,31},{8,0},{9,1... | collective-permute-start | bytes 1572872 | tf_op jit(solution)/shard_map/ppermute | solution.py:61
  38.9 0.7 copy-start.14
  41.0 3.6 %copy-start.1 = (bf16[64,4096]{1,0:T(8,128)(2,1)S(1)}, bf16[64,4096]{1,0:T(8,128)(2,1)}, u32[]{:S(2)}) copy-start(bf16[64,4096]{1,0:T(8,128)(2,1)} %param.7) | copy-start | bytes 1572868
  41.0 15.3 %all-to-all-start.1 = ((bf16[4,64,1024]{2,1,0:T(8,128)(2,1)}), bf16[4,64,1024]{2,1,0:T(8,128)(2,1)S(1)}, u32[]{:S(2)}, u32[]{:S(2)}) async-start(bf16[4,64,1024]{2,1,0:T(8,128)(2,1)} %broadcast_in_dim.13), calls=%async_computation.1 | async-start | bytes 1048576 | tf_op jit(solution)/shard_map/all_to_all | solution.py:21
  44.6 1.8 %copy-start.3 = (bf16[8,4096]{1,0:T(8,128)(2,1)S(1)}, bf16[8,4096]{1,0:T(8,128)(2,1)}, u32[]{:S(2)}) copy-start(bf16[8,4096]{1,0:T(8,128)(2,1)} %param.13) | copy-start | bytes 196612
  56.2 0.6 copy-start.8
  58.7 0.8 copy-start.4
  60.8 10.5 %copy-start = (bf16[64,1024]{0,1:T(8,128)(2,1)S(1)}, bf16[64,1024]{0,1:T(8,128)(2,1)}, u32[]{:S(2)}) copy-start(bf16[64,1024]{0,1:T(8,128)(2,1)} %get-tuple-element.34) | copy-start | bytes 393220
  60.8 38.2 %all-to-all-start.2 = ((f32[32,8,1024]{2,1,0:T(8,128)}), f32[32,8,1024]{2,1,0:T(8,128)S(1)}, u32[]{:S(2)}, u32[]{:S(2)}) async-start(f32[32,8,1024]{2,1,0:T(8,128)} %convolution_bitcast_fusion), calls=%async_computation.2 | async-start | bytes 2097152 | tf_op jit(solution)/shard_map/all_to_all | solution.py:88
  72.8 0.6 copy-start.11
  74.7 15.0 %collective-permute-start.2 = (bf16[32,4096]{1,0:T(8,128)(2,1)S(1)}, bf16[32,4096]{1,0:T(8,128)(2,1)S(1)}, u32[]{:S(2)}, u32[]{:S(2)}) collective-permute-start(bf16[32,4096]{1,0:T(8,128)(2,1)S(1)} %slice.32), channel_id=1, source_target_pairs={{0,8},{1,9},{2,10},{3,11},{4,12},{5,13},{6,14},{7,15},{8,16},{9,17... | collective-permute-start | bytes 786440 | tf_op jit(solution)/shard_map/ppermute | solution.py:62
  79.1 3.7 %copy-start.12 = (s32[64]{0:T(128)S(1)}, s32[64]{0:T(128)}, u32[]{:S(2)}) copy-start(s32[64]{0:T(128)} %get-tuple-element.41) | copy-start | bytes 772
  79.1 13.2 %collective-permute-start.3 = (bf16[32,4096]{1,0:T(8,128)(2,1)S(1)}, bf16[32,4096]{1,0:T(8,128)(2,1)S(1)}, u32[]{:S(2)}, u32[]{:S(2)}) collective-permute-start(bf16[32,4096]{1,0:T(8,128)(2,1)S(1)} %slice.33), channel_id=1, source_target_pairs={{0,24},{1,25},{2,26},{3,27},{4,28},{5,29},{6,30},{7,31},{8,0},{9,1... | collective-permute-start | bytes 786440 | tf_op jit(solution)/shard_map/ppermute | solution.py:63
  84.2 5.6 %copy-start.10 = (s32[64]{0:T(128)S(1)}, s32[64]{0:T(128)}, u32[]{:S(2)}) copy-start(s32[64]{0:T(128)} %get-tuple-element.30) | copy-start | bytes 772
  90.1 2.2 %copy-start.9 = (s32[64]{0:T(128)S(1)}, s32[64]{0:T(128)}, u32[]{:S(2)}) copy-start(s32[64]{0:T(128)} %get-tuple-element.29) | copy-start | bytes 772
  92.6 0.6 copy-start.7
  99.1 0.9 copy-start.2

commit v6 on v5

--- a/solution.py
+++ b/solution.py
@@ -10,6 +10,7 @@
 HIGHEST = lax.Precision.HIGHEST
 F32 = jnp.float32
 BF16 = jnp.bfloat16
+F16 = jnp.float16
 
 X_GROUPS = [[x * NZ + z for x in range(NX)] for z in range(NZ)]
 Z_GROUPS = [[x * NZ + z for z in range(NZ)] for x in range(NX)]
@@ -24,6 +25,10 @@
 
 def shift_x(step):
     return [(x * NZ + z, (x + step) % NX * NZ + z) for x in range(NX) for z in range(NZ)]
+
+
+def power_of_two(exponent):
+    return lax.reduce_precision(jnp.exp2(exponent), 8, 7)
 
 
 def two_parts(values):
@@ -55,19 +60,9 @@
         )
     )
     row_panel = spread(both[:, :width], X_GROUPS)
-    inv_own = both[:, width:]
-    half = inv_own.shape[0] // 2
-    inv_left = lax.ppermute(inv_own, "col", shift_x(1))
-    inv_right = lax.ppermute(inv_own, "col", shift_x(-1))
-    inv_far_a = lax.ppermute(inv_left[:half], "col", shift_x(1))
-    inv_far_b = lax.ppermute(inv_right[half:], "col", shift_x(-1))
-    inv_parts = (
-        (0, 0, inv_own),
-        (1, 0, inv_left),
-        (3, 0, inv_right),
-        (2, 0, inv_far_a),
-        (2, half, inv_far_b),
-    )
+    inv_parts = [both[:, width:]]
+    for k in (1, 2, 3):
+        inv_parts.append(lax.ppermute(inv_parts[0], "col", shift_x(k)))
 
     keep = (drop_mask == 1) | (blk_row == blk_col)
     local_row = blk_row - panel_first
@@ -81,12 +76,24 @@
         row_blocks.reshape(slot_count, BS, PC),
         preferred_element_type=F32,
     ).reshape(slot_count, width)
-    place = (jnp.arange(span)[:, None] == local_row[None, :]).astype(BF16)
-    parts = jnp.concatenate(two_parts(drop_terms), axis=0)
-    sums = jnp.dot(jnp.concatenate([place, place], axis=1), parts, preferred_element_type=F32)
-    sums = sums.reshape(col_count, per_device, width)
+    drop_parts = jnp.concatenate(two_parts(drop_terms), axis=0)
+    largest = jnp.max(jnp.abs(drop_terms), axis=1)
+    remote = (local_row // per_device != col_index) & ~keep
+    place = (jnp.arange(span)[:, None] == local_row[None, :]) & remote[None, :]
+    largest = jnp.max(jnp.where(place, largest[None, :], 0.0), axis=1)
+    exponent = jnp.floor(jnp.log2(jnp.clip(largest, 1e-30, 1e30)))
+    place = jnp.where(place, power_of_two(-exponent)[:, None], 0.0).astype(BF16)
+    sums = jnp.dot(jnp.concatenate([place, place], axis=1), drop_parts, preferred_element_type=F32)
+    sums = jnp.concatenate(
+        [sums.astype(F16), jnp.broadcast_to(exponent.astype(F16)[:, None], (span, 128))], axis=1
+    ).reshape(col_count, per_device, width + 128)
     arrived = lax.all_to_all(sums, "col", 0, 0, tiled=True)
-    lumped = jnp.sum(arrived.reshape(col_count, per_device, width), axis=0)
+    arrived = arrived.reshape(col_count, per_device, width + 128)
+    factor = power_of_two(arrived[:, :, width:].astype(F32))[:, :, :1]
+    own = (blk_row[None, :] == own_first + jnp.arange(per_device)[:, None]) & ~keep[None, :]
+    own = own.astype(BF16)
+    lumped = jnp.dot(jnp.concatenate([own, own], axis=1), drop_parts, preferred_element_type=F32)
+    lumped = lumped + jnp.sum(arrived[:, :, :width].astype(F32) * factor, axis=0)
     scaled_lumped = jnp.einsum(
         "eij,ejk->eik",
         own_inv.astype(F32).reshape(per_device, BS, BS),
@@ -120,10 +127,10 @@
     part_rows = NZ * per_device
     row_x = local_row // part_rows
     inverse = None
-    for distance, first_row, rows in inv_parts:
-        at = jnp.where((col_index // NZ - row_x) % NX == distance, local_row % part_rows, -1)
-        pick = ((at - first_row)[:, None] == jnp.arange(rows.shape[0])[None, :]).astype(BF16)
-        piece = jnp.dot(pick, rows, preferred_element_type=F32)
+    for k in range(NX):
+        at = jnp.where((col_index // NZ - row_x) % NX == k, local_row % part_rows, -1)
+        pick = (at[:, None] == jnp.arange(part_rows)[None, :]).astype(BF16)
+        piece = jnp.dot(pick, inv_parts[k], preferred_element_type=F32)
         inverse = piece if inverse is None else inverse + piece
     inverse = inverse.astype(BF16)
     inverse = inverse.reshape(slot_count, BS, BS)

time: 102 us -> 105 us (1.029)
  starting transfers between devices: 38.3 us -> 34.8 us
  waiting for transfers between devices: 15.2 us -> 18.5 us
  other arithmetic: 4.42 us -> 6.81 us
    all_to_all x1, waiting for transfers between devices: 2.06 us -> 10.3 us  [body(): arrived = lax.all_to_all(sums, 'col', 0, 0, tiled=True)]
    ppermute x4 -> x3, waiting for transfers between devices: 7.73 us -> 0.01 us  [body(): inv_parts.append(lax.ppermute(inv_parts[0], 'col', shift_x(k)))]
    ppermute x4 -> x3, starting transfers between devices: 14.2 us -> 10.9 us  [body(): inv_parts.append(lax.ppermute(inv_parts[0], 'col', shift_x(k)))]
    all_to_all x2, waiting for transfers between devices: 5.41 us -> 8.21 us  [spread(): lax.all_to_all(copies, 'col', 0, 0, axis_index_groups=groups, tiled=True)]
    slice x3 -> x2, local copies, waits for them, and re-layouts: 2.77 us -> 0.86 us  [the longest x1 0.85 us: body(): inv_parts = [both[:, width:]]]
    unnamed x32 -> x38, local copies, waits for them, and re-layouts: 4.03 us -> 5.81 us
  transfers between devices with their start and end apart: 7 -> 6, of which waited for: 4 -> 2; matrix products, arithmetic and copies ran while one was open for 21% -> 21% of each run, Pallas kernels for 0% -> 0%
where the time goes in v6:
time: 105 us
  starting transfers between devices  34.8 us (33%)
  waiting for transfers between devices  18.5 us (18%)
  blocking collectives  18.4 us (18%)
  local copies, waits for them, and re-layouts  16.5 us (16%)
  matrix products  9.18 us (9%)
  other arithmetic  6.81 us (6%)
    all_gather x1, blocking collectives, body(): col_panel = lax.all_gather(labelled, 'row', axis=0, tiled=True)  18.4 us
    all_to_all x2, starting transfers between devices, spread(): lax.all_to_all(copies, 'col', 0, 0, axis_index_groups=groups, tiled=True)  13.6 us
    ppermute x3, starting transfers between devices, body(): inv_parts.append(lax.ppermute(inv_parts[0], 'col', shift_x(k)))  10.9 us
    all_to_all x1, starting transfers between devices, body(): arrived = lax.all_to_all(sums, 'col', 0, 0, tiled=True)  10.4 us
    all_to_all x1, waiting for transfers between devices, body(): arrived = lax.all_to_all(sums, 'col', 0, 0, tiled=True)  10.3 us
    all_to_all x2, waiting for transfers between devices, spread(): lax.all_to_all(copies, 'col', 0, 0, axis_index_groups=groups, tiled=True)  8.21 us
    unnamed x38, local copies, waits for them, and re-layouts  5.81 us
    dot_general x4, matrix products, body(): piece = jnp.dot(pick, inv_parts[k], preferred_element_type=F32)  4.47 us
  transfers between devices with their start and end apart: 6, of which 2 were waited for; matrix products, arithmetic and copies ran while one was open for 21% of the time, Pallas kernels for 0%

profile of v6, /device:TPU:64, one launch (start us, length us, event | category | flops | bytes accessed | tf_op | source)
XLA Modules:
  0.0 104.6 jit_solution(12720433676506754625)
XLA Ops:
  0.0 0.8 pad_maximum_fusion.1
  0.8 0.9 broadcast_in_dim.30
  1.8 10.0 %all-to-all-start = ((bf16[8,8,5120]{2,1,0:T(8,128)(2,1)}), bf16[8,8,5120]{2,1,0:T(8,128)(2,1)S(1)}, u32[]{:S(2)}, u32[]{:S(2)}) async-start(bf16[8,8,5120]{2,1,0:T(8,128)(2,1)} %broadcast_in_dim.30), calls=%async_computation | async-start | bytes 1310720 | tf_op jit(solution)/shard_map/all_to_all | solution.py:22
  13.1 18.4 %all_gather.3 = bf16[128,1152]{1,0:T(8,128)(2,1)S(1)} all-gather(bf16[8,1152]{1,0:T(8,128)(2,1)S(1)} %pad_maximum_fusion.4), channel_id=1, replica_groups=mesh['row'=16,'col'=32] {'row'}, dimensions={0}, use_global_device_ids=true | all-gather | bytes 313344 | tf_op jit(solution)/shard_map/all_gather | solution.py:55
  31.5 0.8 slice.27
  32.3 3.5 %collective-permute-start = (bf16[64,4096]{1,0:T(8,128)(2,1)}, bf16[64,4096]{1,0:T(8,128)(2,1)}, u32[]{:S(2)}, u32[]{:S(2)}) collective-permute-start(bf16[64,4096]{1,0:T(8,128)(2,1)} %slice.27), channel_id=1, source_target_pairs={{0,8},{1,9},{2,10},{3,11},{4,12},{5,13},{6,14},{7,15},{8,16},{9,17... | collective-permute-start | bytes 1572872 | tf_op jit(solution)/shard_map/ppermute | solution.py:65
  35.9 3.7 %collective-permute-start.2 = (bf16[64,4096]{1,0:T(8,128)(2,1)}, bf16[64,4096]{1,0:T(8,128)(2,1)}, u32[]{:S(2)}, u32[]{:S(2)}) collective-permute-start(bf16[64,4096]{1,0:T(8,128)(2,1)} %slice.27), channel_id=1, source_target_pairs={{0,24},{1,25},{2,26},{3,27},{4,28},{5,29},{6,30},{7,31},{8,0},{9,1... | collective-permute-start | bytes 1572872 | tf_op jit(solution)/shard_map/ppermute | solution.py:65
  39.5 3.7 %collective-permute-start.1 = (bf16[64,4096]{1,0:T(8,128)(2,1)}, bf16[64,4096]{1,0:T(8,128)(2,1)}, u32[]{:S(2)}, u32[]{:S(2)}) collective-permute-start(bf16[64,4096]{1,0:T(8,128)(2,1)} %slice.27), channel_id=1, source_target_pairs={{0,16},{1,17},{2,18},{3,19},{4,20},{5,21},{6,22},{7,23},{8,24},{9,... | collective-permute-start | bytes 1572872 | tf_op jit(solution)/shard_map/ppermute | solution.py:65
  44.4 0.9 broadcast_in_dim.36
  45.3 3.6 %all-to-all-start.1 = ((bf16[4,64,1024]{2,1,0:T(8,128)(2,1)}), bf16[4,64,1024]{2,1,0:T(8,128)(2,1)S(1)}, u32[]{:S(2)}, u32[]{:S(2)}) async-start(bf16[4,64,1024]{2,1,0:T(8,128)(2,1)} %broadcast_in_dim.36), calls=%async_computation.1 | async-start | bytes 1048576 | tf_op jit(solution)/shard_map/all_to_all | solution.py:22
  48.9 1.1 %reshape.95 = bf16[64,64,64]{2,1,0:T(8,128)(2,1)S(1)} reshape(bf16[64,4096]{1,0:T(8,128)(2,1)S(1)} %copy-done.1) | data formatting | bytes 1048576 | tf_op jit(solution)/shard_map/reshape | solution.py:69
  50.1 0.8 reshape.101
  54.8 1.1 %copy.70 = bf16[64,64,16]{1,2,0:T(8,128)(2,1)} copy(bf16[64,64,16]{0,2,1:T(8,128)(2,1)S(1)} %bitcast.36) | data formatting | bytes 262144 | tf_op jit(solution)/shard_map/reshape | solution.py:137
  59.9 8.2 %all-to-all-done.1 = bf16[4,64,1024]{2,1,0:T(8,128)(2,1)S(1)} async-done(((bf16[4,64,1024]{2,1,0:T(8,128)(2,1)}), bf16[4,64,1024]{2,1,0:T(8,128)(2,1)S(1)}, u32[]{:S(2)}, u32[]{:S(2)}) %all-to-all-start.1) | async-done | bytes 524320 | tf_op jit(solution)/shard_map/all_to_all | solution.py:22
  69.0 0.8 abs_reduce_fusion
  71.0 1.0 maximum_bitcast_fusion
  72.0 10.4 %all-to-all-start.2 = ((f16[32,8,1152]{2,1,0:T(8,128)(2,1)}), f16[32,8,1152]{2,1,0:T(8,128)(2,1)S(1)}, u32[]{:S(2)}, u32[]{:S(2)}) async-start(f16[32,8,1152]{2,1,0:T(8,128)(2,1)} %maximum_bitcast_fusion), calls=%async_computation.2 | async-start | bytes 1179648 | tf_op jit(solution)/shard_map/all_to_all | solution.py:90
  82.3 1.4 %fusion.27 = f32[64,4096]{1,0:T(8,128)S(1)} fusion(bf16[64,4096]{1,0:T(8,128)(2,1)} %collective-permute-done.2, s32[64]{0:T(128)S(1)} %get-tuple-element.41), kind=kOutput, calls=%fused_computation.58 | convolution fusion | flops 33558528 | bytes 1573120 | tf_op jit(solution)/shard_map/dot_general | solution.py:133
  84.4 1.4 %convolution_add_fusion.1 = f32[64,4096]{1,0:T(8,128)S(1)} fusion(f32[64,4096]{1,0:T(8,128)S(1)} %fusion.26, bf16[64,4096]{1,0:T(8,128)(2,1)} %collective-permute-done, s32[64]{0:T(128)S(1)} %copy-done.14), kind=kOutput, calls=%fused_computation.1 | convolution fusion | flops 33820672 | bytes 2621696 | tf_op jit(solution)/shard_map/dot_general | solution.py:133
  86.3 1.4 %fusion.1 = bf16[64,4096]{1,0:T(8,128)(2,1)S(1)} fusion(f32[64,4096]{1,0:T(8,128)S(1)} %fusion.27, f32[64,4096]{1,0:T(8,128)S(1)} %convolution_add_fusion.1, bf16[64,4096]{1,0:T(8,128)(2,1)} %collective-permute-done.1, s32[64]{0:T(128)S(1)} %copy-done.13), kind=kOutput, calls=%fused_computation.3 | convolution fusion | flops 34344960 | bytes 3145984 | tf_op jit(solution)/shard_map/dot_general | solution.py:133
  87.7 1.1 %reshape.94 = bf16[64,64,64]{2,1,0:T(8,128)(2,1)S(1)} reshape(bf16[64,4096]{1,0:T(8,128)(2,1)S(1)} %fusion.1) | data formatting | bytes 1048576 | tf_op jit(solution)/shard_map/reshape | solution.py:136
  90.2 10.3 %all-to-all-done.2 = f16[32,8,1152]{2,1,0:T(8,128)(2,1)S(1)} async-done(((f16[32,8,1152]{2,1,0:T(8,128)(2,1)}), f16[32,8,1152]{2,1,0:T(8,128)(2,1)S(1)}, u32[]{:S(2)}, u32[]{:S(2)}) %all-to-all-start.2) | async-done | bytes 589856 | tf_op jit(solution)/shard_map/all_to_all | solution.py:90
  101.8 0.8 copy-done.2
  103.7 0.9 convolution_add_fusion.2
  (92 shorter events, 17.3 us)
Async XLA Ops:
  1.8 29.7 %all-to-all-start = ((bf16[8,8,5120]{2,1,0:T(8,128)(2,1)}), bf16[8,8,5120]{2,1,0:T(8,128)(2,1)S(1)}, u32[]{:S(2)}, u32[]{:S(2)}) async-start(bf16[8,8,5120]{2,1,0:T(8,128)(2,1)} %broadcast_in_dim.30), calls=%async_computation | async-start | bytes 1310720 | tf_op jit(solution)/shard_map/all_to_all | solution.py:22
  11.7 0.7 copy-start.17
  12.4 0.7 copy-start.4
  31.5 11.8 %copy-start.15 = (s32[64]{0:T(128)S(1)}, s32[64]{0:T(128)}, u32[]{:S(2)}) copy-start(s32[64]{0:T(128)} %param.9) | copy-start | bytes 772
  32.3 11.0 %copy-start.5 = (s32[64]{0:T(128)S(1)}, s32[64]{0:T(128)}, u32[]{:S(2)}) copy-start(s32[64]{0:T(128)} %param.8) | copy-start | bytes 772
  32.3 11.0 %copy-start.16 = (s32[64]{0:T(128)S(1)}, s32[64]{0:T(128)}, u32[]{:S(2)}) copy-start(s32[64]{0:T(128)} %param.10) | copy-start | bytes 772
  32.3 51.4 %collective-permute-start = (bf16[64,4096]{1,0:T(8,128)(2,1)}, bf16[64,4096]{1,0:T(8,128)(2,1)}, u32[]{:S(2)}, u32[]{:S(2)}) collective-permute-start(bf16[64,4096]{1,0:T(8,128)(2,1)} %slice.27), channel_id=1, source_target_pairs={{0,8},{1,9},{2,10},{3,11},{4,12},{5,13},{6,14},{7,15},{8,16},{9,17... | collective-permute-start | bytes 1572872 | tf_op jit(solution)/shard_map/ppermute | solution.py:65
  35.9 46.5 %collective-permute-start.2 = (bf16[64,4096]{1,0:T(8,128)(2,1)}, bf16[64,4096]{1,0:T(8,128)(2,1)}, u32[]{:S(2)}, u32[]{:S(2)}) collective-permute-start(bf16[64,4096]{1,0:T(8,128)(2,1)} %slice.27), channel_id=1, source_target_pairs={{0,24},{1,25},{2,26},{3,27},{4,28},{5,29},{6,30},{7,31},{8,0},{9,1... | collective-permute-start | bytes 1572872 | tf_op jit(solution)/shard_map/ppermute | solution.py:65
  39.5 46.2 %collective-permute-start.1 = (bf16[64,4096]{1,0:T(8,128)(2,1)}, bf16[64,4096]{1,0:T(8,128)(2,1)}, u32[]{:S(2)}, u32[]{:S(2)}) collective-permute-start(bf16[64,4096]{1,0:T(8,128)(2,1)} %slice.27), channel_id=1, source_target_pairs={{0,16},{1,17},{2,18},{3,19},{4,20},{5,21},{6,22},{7,23},{8,24},{9,... | collective-permute-start | bytes 1572872 | tf_op jit(solution)/shard_map/ppermute | solution.py:65
  45.3 3.6 %copy-start.1 = (bf16[64,4096]{1,0:T(8,128)(2,1)S(1)}, bf16[64,4096]{1,0:T(8,128)(2,1)}, u32[]{:S(2)}) copy-start(bf16[64,4096]{1,0:T(8,128)(2,1)} %param.7) | copy-start | bytes 1572868
  45.3 22.8 %all-to-all-start.1 = ((bf16[4,64,1024]{2,1,0:T(8,128)(2,1)}), bf16[4,64,1024]{2,1,0:T(8,128)(2,1)S(1)}, u32[]{:S(2)}, u32[]{:S(2)}) async-start(bf16[4,64,1024]{2,1,0:T(8,128)(2,1)} %broadcast_in_dim.36), calls=%async_computation.1 | async-start | bytes 1048576 | tf_op jit(solution)/shard_map/all_to_all | solution.py:22
  48.9 1.1 %copy-start.3 = (bf16[8,4096]{1,0:T(8,128)(2,1)S(1)}, bf16[8,4096]{1,0:T(8,128)(2,1)}, u32[]{:S(2)}) copy-start(bf16[8,4096]{1,0:T(8,128)(2,1)} %param.13) | copy-start | bytes 196612
  53.0 0.7 copy-start.6
  54.8 1.1 %copy-start.18 = (s32[8]{0:T(128)S(1)}, s32[8]{0:T(128)}, u32[]{:S(2)}) copy-start(s32[8]{0:T(128)} %param.12) | copy-start | bytes 100
  55.9 0.7 copy-start.9
  55.9 0.7 copy-start.11
  59.9 8.2 %copy-start.10 = (pred[64]{0:T(512)(128)(4,1)S(1)}, pred[64]{0:T(512)(128)(4,1)}, u32[]{:S(2)}) copy-start(pred[64]{0:T(512)(128)(4,1)} %get-tuple-element.43) | copy-start | bytes 196
  72.0 28.4 %all-to-all-start.2 = ((f16[32,8,1152]{2,1,0:T(8,128)(2,1)}), f16[32,8,1152]{2,1,0:T(8,128)(2,1)S(1)}, u32[]{:S(2)}, u32[]{:S(2)}) async-start(f16[32,8,1152]{2,1,0:T(8,128)(2,1)} %maximum_bitcast_fusion), calls=%async_computation.2 | async-start | bytes 1179648 | tf_op jit(solution)/shard_map/all_to_all | solution.py:90
  83.7 0.6 copy-start.14
  85.7 0.6 copy-start.13
  87.7 1.1 %copy-start = (bf16[64,64,16]{1,2,0:T(8,128)(2,1)S(1)}, bf16[64,64,16]{1,2,0:T(8,128)(2,1)}, u32[]{:S(2)}) copy-start(bf16[64,64,16]{1,2,0:T(8,128)(2,1)} %copy.70) | copy-start | bytes 393220
  100.7 0.7 copy-start.8
  101.7 0.9 copy-start.2
  103.0 0.7 copy-start.7
  (1 other events, 0.6 us)

commit v7 on v6

--- a/solution.py
+++ b/solution.py
@@ -47,11 +47,15 @@
     panel_first = row_index * span
     own_first = panel_first + col_index * per_device
 
-    both = spread(jnp.concatenate([prolong, inv_diag], axis=1), Z_GROUPS)
+    lead = 128
+    labelled = jnp.concatenate(
+        [jnp.broadcast_to(agg_label.astype(BF16)[:, None], (per_device, lead)), prolong], axis=1
+    )
+    joined = jnp.concatenate([prolong, inv_diag], axis=1)
+    copies = jnp.broadcast_to(joined[None], (NZ,) + joined.shape)
+    both = lax.all_to_all(copies, "col", 0, 0, axis_index_groups=Z_GROUPS, tiled=True)
+    both = both.reshape(NZ * per_device, joined.shape[1])
 
-    labelled = jnp.concatenate(
-        [prolong, jnp.broadcast_to(agg_label.astype(BF16)[:, None], (per_device, 128))], axis=1
-    )
     col_panel = lax.all_gather(labelled, "row", axis=0, tiled=True)
 
     both, col_panel, a_blocks, blk_row, blk_col, drop_mask, own_label, own_inv = (
@@ -104,8 +108,8 @@
     col_place = blk_col // span * per_device + blk_col % per_device
     pick = col_place[:, None] == jnp.arange(col_panel.shape[0])[None, :]
     picked = jnp.dot(pick.astype(BF16), col_panel, preferred_element_type=F32)
-    col_label = picked[:, width]
-    col_blocks = (picked[:, :width] * keep[:, None].astype(F32)).astype(BF16)
+    col_label = picked[:, 0]
+    col_blocks = (picked[:, lead:] * keep[:, None].astype(F32)).astype(BF16)
     kept_terms = jnp.einsum(
         "sij,sjk->sik",
         matrices,
@@ -127,7 +131,7 @@
     part_rows = NZ * per_device
     row_x = local_row // part_rows
     inverse = None
-    for k in range(NX):
+    for k in (0, 1, 3, 2):
         at = jnp.where((col_index // NZ - row_x) % NX == k, local_row % part_rows, -1)
         pick = (at[:, None] == jnp.arange(part_rows)[None, :]).astype(BF16)
         piece = jnp.dot(pick, inv_parts[k], preferred_element_type=F32)

time: 105 us -> 106 us (level)
  starting transfers between devices: 34.8 us -> 36.1 us
    all_to_all x0 -> x1, starting transfers between devices: none -> 9.96 us  [body(): lax.all_to_all(copies, 'col', 0, 0, axis_index_groups=Z_GROUPS, tiled=True)]
    all_to_all x2 -> x1, starting transfers between devices: 13.6 us -> 3.6 us  [spread(): lax.all_to_all(copies, 'col', 0, 0, axis_index_groups=groups, tiled=True)]
    all_to_all x2 -> x1, waiting for transfers between devices: 8.21 us -> 7.31 us  [spread(): lax.all_to_all(copies, 'col', 0, 0, axis_index_groups=groups, tiled=True)]
where the time goes in v7:
time: 106 us; the launch traced here: 105 us
  starting transfers between devices  36.1 us (34%)
  blocking collectives  18.4 us (17%)
  waiting for transfers between devices  17.8 us (17%)
  local copies, waits for them, and re-layouts  16.5 us (16%)
  matrix products  9.18 us (9%)
  other arithmetic  6.82 us (6%)
    all_gather x1, blocking collectives, body(): col_panel = lax.all_gather(labelled, 'row', axis=0, tiled=True)  18.4 us
    ppermute x3, starting transfers between devices, body(): inv_parts.append(lax.ppermute(inv_parts[0], 'col', shift_x(k)))  11.5 us
    all_to_all x1, starting transfers between devices, body(): arrived = lax.all_to_all(sums, 'col', 0, 0, tiled=True)  11 us
    all_to_all x1, waiting for transfers between devices, body(): arrived = lax.all_to_all(sums, 'col', 0, 0, tiled=True)  10.5 us
    all_to_all x1, starting transfers between devices, body(): lax.all_to_all(copies, 'col', 0, 0, axis_index_groups=Z_GROUPS, tiled=True)  9.96 us
    all_to_all x1, waiting for transfers between devices, spread(): lax.all_to_all(copies, 'col', 0, 0, axis_index_groups=groups, tiled=True)  7.31 us
    unnamed x38, local copies, waits for them, and re-layouts  5.81 us
    dot_general x4, matrix products, body(): piece = jnp.dot(pick, inv_parts[k], preferred_element_type=F32)  4.47 us
  transfers between devices with their start and end apart: 6, of which 2 were waited for; matrix products, arithmetic and copies ran while one was open for 21% of the time, Pallas kernels for 0%

profile of v7, /device:TPU:64, one launch (start us, length us, event | category | flops | bytes accessed | tf_op | source)
XLA Modules:
  0.0 105.2 jit_solution(14341701387789660587)
XLA Ops:
  0.0 0.8 pad_maximum_fusion.1
  0.8 0.9 broadcast_in_dim.30
  1.8 10.0 %all-to-all-start = ((bf16[8,8,5120]{2,1,0:T(8,128)(2,1)}), bf16[8,8,5120]{2,1,0:T(8,128)(2,1)S(1)}, u32[]{:S(2)}, u32[]{:S(2)}) async-start(bf16[8,8,5120]{2,1,0:T(8,128)(2,1)} %broadcast_in_dim.30), calls=%async_computation | async-start | bytes 1310720 | tf_op jit(solution)/shard_map/all_to_all | solution.py:56
  13.1 18.4 %all_gather.3 = bf16[128,1152]{1,0:T(8,128)(2,1)S(1)} all-gather(bf16[8,1152]{1,0:T(8,128)(2,1)S(1)} %pad_maximum_fusion.4), channel_id=1, replica_groups=mesh['row'=16,'col'=32] {'row'}, dimensions={0}, use_global_device_ids=true | all-gather | bytes 313344 | tf_op jit(solution)/shard_map/all_gather | solution.py:59
  31.5 0.8 slice.27
  32.3 3.5 %collective-permute-start = (bf16[64,4096]{1,0:T(8,128)(2,1)}, bf16[64,4096]{1,0:T(8,128)(2,1)}, u32[]{:S(2)}, u32[]{:S(2)}) collective-permute-start(bf16[64,4096]{1,0:T(8,128)(2,1)} %slice.27), channel_id=1, source_target_pairs={{0,8},{1,9},{2,10},{3,11},{4,12},{5,13},{6,14},{7,15},{8,16},{9,17... | collective-permute-start | bytes 1572872 | tf_op jit(solution)/shard_map/ppermute | solution.py:69
  35.9 4.6 %collective-permute-start.2 = (bf16[64,4096]{1,0:T(8,128)(2,1)}, bf16[64,4096]{1,0:T(8,128)(2,1)}, u32[]{:S(2)}, u32[]{:S(2)}) collective-permute-start(bf16[64,4096]{1,0:T(8,128)(2,1)} %slice.27), channel_id=1, source_target_pairs={{0,16},{1,17},{2,18},{3,19},{4,20},{5,21},{6,22},{7,23},{8,24},{9,... | collective-permute-start | bytes 1572872 | tf_op jit(solution)/shard_map/ppermute | solution.py:69
  40.5 3.3 %collective-permute-start.1 = (bf16[64,4096]{1,0:T(8,128)(2,1)}, bf16[64,4096]{1,0:T(8,128)(2,1)}, u32[]{:S(2)}, u32[]{:S(2)}) collective-permute-start(bf16[64,4096]{1,0:T(8,128)(2,1)} %slice.27), channel_id=1, source_target_pairs={{0,24},{1,25},{2,26},{3,27},{4,28},{5,29},{6,30},{7,31},{8,0},{9,1... | collective-permute-start | bytes 1572872 | tf_op jit(solution)/shard_map/ppermute | solution.py:69
  45.0 0.9 broadcast_in_dim.36
  45.9 3.6 %all-to-all-start.1 = ((bf16[4,64,1024]{2,1,0:T(8,128)(2,1)}), bf16[4,64,1024]{2,1,0:T(8,128)(2,1)S(1)}, u32[]{:S(2)}, u32[]{:S(2)}) async-start(bf16[4,64,1024]{2,1,0:T(8,128)(2,1)} %broadcast_in_dim.36), calls=%async_computation.1 | async-start | bytes 1048576 | tf_op jit(solution)/shard_map/all_to_all | solution.py:22
  49.5 1.1 %reshape.95 = bf16[64,64,64]{2,1,0:T(8,128)(2,1)S(1)} reshape(bf16[64,4096]{1,0:T(8,128)(2,1)S(1)} %copy-done.1) | data formatting | bytes 1048576 | tf_op jit(solution)/shard_map/reshape | solution.py:73
  50.7 0.8 reshape.101
  55.4 1.1 %copy.70 = bf16[64,64,16]{1,2,0:T(8,128)(2,1)} copy(bf16[64,64,16]{0,2,1:T(8,128)(2,1)S(1)} %bitcast.36) | data formatting | bytes 262144 | tf_op jit(solution)/shard_map/reshape | solution.py:141
  60.5 7.3 %all-to-all-done.1 = bf16[4,64,1024]{2,1,0:T(8,128)(2,1)S(1)} async-done(((bf16[4,64,1024]{2,1,0:T(8,128)(2,1)}), bf16[4,64,1024]{2,1,0:T(8,128)(2,1)S(1)}, u32[]{:S(2)}, u32[]{:S(2)}) %all-to-all-start.1) | async-done | bytes 524320 | tf_op jit(solution)/shard_map/all_to_all | solution.py:22
  68.7 0.8 abs_reduce_fusion
  70.7 1.0 maximum_bitcast_fusion
  71.7 11.0 %all-to-all-start.2 = ((f16[32,8,1152]{2,1,0:T(8,128)(2,1)}), f16[32,8,1152]{2,1,0:T(8,128)(2,1)S(1)}, u32[]{:S(2)}, u32[]{:S(2)}) async-start(f16[32,8,1152]{2,1,0:T(8,128)(2,1)} %maximum_bitcast_fusion), calls=%async_computation.2 | async-start | bytes 1179648 | tf_op jit(solution)/shard_map/all_to_all | solution.py:94
  82.7 1.4 %fusion.27 = f32[64,4096]{1,0:T(8,128)S(1)} fusion(bf16[64,4096]{1,0:T(8,128)(2,1)} %collective-permute-done.2, s32[64]{0:T(128)S(1)} %get-tuple-element.41), kind=kOutput, calls=%fused_computation.58 | convolution fusion | flops 33558528 | bytes 1573120 | tf_op jit(solution)/shard_map/dot_general | solution.py:137
  84.7 1.4 %convolution_add_fusion.1 = f32[64,4096]{1,0:T(8,128)S(1)} fusion(f32[64,4096]{1,0:T(8,128)S(1)} %fusion.26, bf16[64,4096]{1,0:T(8,128)(2,1)} %collective-permute-done, s32[64]{0:T(128)S(1)} %copy-done.14), kind=kOutput, calls=%fused_computation.1 | convolution fusion | flops 33820672 | bytes 2621696 | tf_op jit(solution)/shard_map/dot_general | solution.py:137
  86.7 1.4 %fusion.1 = bf16[64,4096]{1,0:T(8,128)(2,1)S(1)} fusion(f32[64,4096]{1,0:T(8,128)S(1)} %fusion.27, f32[64,4096]{1,0:T(8,128)S(1)} %convolution_add_fusion.1, bf16[64,4096]{1,0:T(8,128)(2,1)} %collective-permute-done.1, s32[64]{0:T(128)S(1)} %copy-done.13), kind=kOutput, calls=%fused_computation.3 | convolution fusion | flops 34344960 | bytes 3145984 | tf_op jit(solution)/shard_map/dot_general | solution.py:137
  88.1 1.1 %reshape.94 = bf16[64,64,64]{2,1,0:T(8,128)(2,1)S(1)} reshape(bf16[64,4096]{1,0:T(8,128)(2,1)S(1)} %fusion.1) | data formatting | bytes 1048576 | tf_op jit(solution)/shard_map/reshape | solution.py:140
  90.5 10.5 %all-to-all-done.2 = f16[32,8,1152]{2,1,0:T(8,128)(2,1)S(1)} async-done(((f16[32,8,1152]{2,1,0:T(8,128)(2,1)}), f16[32,8,1152]{2,1,0:T(8,128)(2,1)S(1)}, u32[]{:S(2)}, u32[]{:S(2)}) %all-to-all-start.2) | async-done | bytes 589856 | tf_op jit(solution)/shard_map/all_to_all | solution.py:94
  102.4 0.8 copy-done.2
  104.3 0.9 convolution_add_fusion.2
  (92 shorter events, 17.3 us)
Async XLA Ops:
  1.8 29.7 %all-to-all-start = ((bf16[8,8,5120]{2,1,0:T(8,128)(2,1)}), bf16[8,8,5120]{2,1,0:T(8,128)(2,1)S(1)}, u32[]{:S(2)}, u32[]{:S(2)}) async-start(bf16[8,8,5120]{2,1,0:T(8,128)(2,1)} %broadcast_in_dim.30), calls=%async_computation | async-start | bytes 1310720 | tf_op jit(solution)/shard_map/all_to_all | solution.py:56
  11.7 0.7 copy-start.17
  12.4 0.7 copy-start.4
  31.5 12.4 %copy-start.15 = (s32[64]{0:T(128)S(1)}, s32[64]{0:T(128)}, u32[]{:S(2)}) copy-start(s32[64]{0:T(128)} %param.9) | copy-start | bytes 772
  32.3 11.6 %copy-start.5 = (s32[64]{0:T(128)S(1)}, s32[64]{0:T(128)}, u32[]{:S(2)}) copy-start(s32[64]{0:T(128)} %param.8) | copy-start | bytes 772
  32.3 11.6 %copy-start.16 = (s32[64]{0:T(128)S(1)}, s32[64]{0:T(128)}, u32[]{:S(2)}) copy-start(s32[64]{0:T(128)} %param.10) | copy-start | bytes 772
  32.3 51.7 %collective-permute-start = (bf16[64,4096]{1,0:T(8,128)(2,1)}, bf16[64,4096]{1,0:T(8,128)(2,1)}, u32[]{:S(2)}, u32[]{:S(2)}) collective-permute-start(bf16[64,4096]{1,0:T(8,128)(2,1)} %slice.27), channel_id=1, source_target_pairs={{0,8},{1,9},{2,10},{3,11},{4,12},{5,13},{6,14},{7,15},{8,16},{9,17... | collective-permute-start | bytes 1572872 | tf_op jit(solution)/shard_map/ppermute | solution.py:69
  35.9 46.8 %collective-permute-start.2 = (bf16[64,4096]{1,0:T(8,128)(2,1)}, bf16[64,4096]{1,0:T(8,128)(2,1)}, u32[]{:S(2)}, u32[]{:S(2)}) collective-permute-start(bf16[64,4096]{1,0:T(8,128)(2,1)} %slice.27), channel_id=1, source_target_pairs={{0,16},{1,17},{2,18},{3,19},{4,20},{5,21},{6,22},{7,23},{8,24},{9,... | collective-permute-start | bytes 1572872 | tf_op jit(solution)/shard_map/ppermute | solution.py:69
  40.5 45.6 %collective-permute-start.1 = (bf16[64,4096]{1,0:T(8,128)(2,1)}, bf16[64,4096]{1,0:T(8,128)(2,1)}, u32[]{:S(2)}, u32[]{:S(2)}) collective-permute-start(bf16[64,4096]{1,0:T(8,128)(2,1)} %slice.27), channel_id=1, source_target_pairs={{0,24},{1,25},{2,26},{3,27},{4,28},{5,29},{6,30},{7,31},{8,0},{9,1... | collective-permute-start | bytes 1572872 | tf_op jit(solution)/shard_map/ppermute | solution.py:69
  45.9 3.6 %copy-start.1 = (bf16[64,4096]{1,0:T(8,128)(2,1)S(1)}, bf16[64,4096]{1,0:T(8,128)(2,1)}, u32[]{:S(2)}) copy-start(bf16[64,4096]{1,0:T(8,128)(2,1)} %param.7) | copy-start | bytes 1572868
  45.9 21.9 %all-to-all-start.1 = ((bf16[4,64,1024]{2,1,0:T(8,128)(2,1)}), bf16[4,64,1024]{2,1,0:T(8,128)(2,1)S(1)}, u32[]{:S(2)}, u32[]{:S(2)}) async-start(bf16[4,64,1024]{2,1,0:T(8,128)(2,1)} %broadcast_in_dim.36), calls=%async_computation.1 | async-start | bytes 1048576 | tf_op jit(solution)/shard_map/all_to_all | solution.py:22
  49.5 1.1 %copy-start.3 = (bf16[8,4096]{1,0:T(8,128)(2,1)S(1)}, bf16[8,4096]{1,0:T(8,128)(2,1)}, u32[]{:S(2)}) copy-start(bf16[8,4096]{1,0:T(8,128)(2,1)} %param.13) | copy-start | bytes 196612
  53.6 0.7 copy-start.6
  55.4 1.1 %copy-start.18 = (s32[8]{0:T(128)S(1)}, s32[8]{0:T(128)}, u32[]{:S(2)}) copy-start(s32[8]{0:T(128)} %param.12) | copy-start | bytes 100
  56.5 0.7 copy-start.9
  56.5 0.7 copy-start.11
  60.5 7.3 %copy-start.10 = (pred[64]{0:T(512)(128)(4,1)S(1)}, pred[64]{0:T(512)(128)(4,1)}, u32[]{:S(2)}) copy-start(pred[64]{0:T(512)(128)(4,1)} %get-tuple-element.43) | copy-start | bytes 196
  71.7 29.3 %all-to-all-start.2 = ((f16[32,8,1152]{2,1,0:T(8,128)(2,1)}), f16[32,8,1152]{2,1,0:T(8,128)(2,1)S(1)}, u32[]{:S(2)}, u32[]{:S(2)}) async-start(f16[32,8,1152]{2,1,0:T(8,128)(2,1)} %maximum_bitcast_fusion), calls=%async_computation.2 | async-start | bytes 1179648 | tf_op jit(solution)/shard_map/all_to_all | solution.py:94
  84.1 0.6 copy-start.14
  86.1 0.6 copy-start.13
  88.1 1.1 %copy-start = (bf16[64,64,16]{1,2,0:T(8,128)(2,1)S(1)}, bf16[64,64,16]{1,2,0:T(8,128)(2,1)}, u32[]{:S(2)}) copy-start(bf16[64,64,16]{1,2,0:T(8,128)(2,1)} %copy.70) | copy-start | bytes 393220
  101.3 0.7 copy-start.8
  102.2 0.9 copy-start.2
  103.6 0.7 copy-start.7
  (1 other events, 0.6 us)

commit v8 on v6

--- a/solution.py
+++ b/solution.py
@@ -54,10 +54,8 @@
     )
     col_panel = lax.all_gather(labelled, "row", axis=0, tiled=True)
 
-    both, col_panel, a_blocks, blk_row, blk_col, drop_mask, own_label, own_inv = (
-        lax.optimization_barrier(
-            (both, col_panel, a_blocks, blk_row, blk_col, drop_mask, agg_label, inv_diag)
-        )
+    both, col_panel, blk_row, blk_col, drop_mask, own_label, own_inv = lax.optimization_barrier(
+        (both, col_panel, blk_row, blk_col, drop_mask, agg_label, inv_diag)
     )
     row_panel = spread(both[:, :width], X_GROUPS)
     inv_parts = [both[:, width:]]

time: 105 us -> 107 us (1.019)
  waiting for transfers between devices: 18.5 us -> 20.2 us
    all_to_all x2, waiting for transfers between devices: 8.21 us -> 9.9 us  [spread(): lax.all_to_all(copies, 'col', 0, 0, axis_index_groups=groups, tiled=True)]
    unnamed x38 -> x36, local copies, waits for them, and re-layouts: 5.81 us -> 5.17 us
where the time goes in v8:
time: 107 us; the launch traced here: 106 us
  starting transfers between devices  35 us (33%)
  waiting for transfers between devices  20.2 us (19%)
  blocking collectives  18.4 us (17%)
  local copies, waits for them, and re-layouts  15.9 us (15%)
  matrix products  9.2 us (9%)
  other arithmetic  6.84 us (6%)
    all_gather x1, blocking collectives, body(): col_panel = lax.all_gather(labelled, 'row', axis=0, tiled=True)  18.4 us
    all_to_all x2, starting transfers between devices, spread(): lax.all_to_all(copies, 'col', 0, 0, axis_index_groups=groups, tiled=True)  13.7 us
    ppermute x3, starting transfers between devices, body(): inv_parts.append(lax.ppermute(inv_parts[0], 'col', shift_x(k)))  10.9 us
    all_to_all x1, starting transfers between devices, body(): arrived = lax.all_to_all(sums, 'col', 0, 0, tiled=True)  10.4 us
    all_to_all x1, waiting for transfers between devices, body(): arrived = lax.all_to_all(sums, 'col', 0, 0, tiled=True)  10.3 us
    all_to_all x2, waiting for transfers between devices, spread(): lax.all_to_all(copies, 'col', 0, 0, axis_index_groups=groups, tiled=True)  9.9 us
    unnamed x36, local copies, waits for them, and re-layouts  5.17 us
    dot_general x4, matrix products, body(): piece = jnp.dot(pick, inv_parts[k], preferred_element_type=F32)  4.47 us
  transfers between devices with their start and end apart: 6, of which 2 were waited for; matrix products, arithmetic and copies ran while one was open for 21% of the time, Pallas kernels for 0%

profile of v8, /device:TPU:64, one launch (start us, length us, event | category | flops | bytes accessed | tf_op | source)
XLA Modules:
  0.0 105.9 jit_solution(11121738072315276298)
XLA Ops:
  0.0 0.8 pad_maximum_fusion.1
  0.8 0.9 broadcast_in_dim.30
  1.8 10.1 %all-to-all-start = ((bf16[8,8,5120]{2,1,0:T(8,128)(2,1)}), bf16[8,8,5120]{2,1,0:T(8,128)(2,1)S(1)}, u32[]{:S(2)}, u32[]{:S(2)}) async-start(bf16[8,8,5120]{2,1,0:T(8,128)(2,1)} %broadcast_in_dim.30), calls=%async_computation | async-start | bytes 1310720 | tf_op jit(solution)/shard_map/all_to_all | solution.py:22
  12.5 1.1 %reshape.96 = bf16[64,64,64]{2,1,0:T(8,128)(2,1)S(1)} reshape(bf16[64,4096]{1,0:T(8,128)(2,1)S(1)} %copy-done.1) | data formatting | bytes 1048576 | tf_op jit(solution)/shard_map/reshape | solution.py:67
  14.4 18.4 %all_gather.3 = bf16[128,1152]{1,0:T(8,128)(2,1)S(1)} all-gather(bf16[8,1152]{1,0:T(8,128)(2,1)S(1)} %pad_maximum_fusion.4), channel_id=1, replica_groups=mesh['row'=16,'col'=32] {'row'}, dimensions={0}, use_global_device_ids=true | all-gather | bytes 313344 | tf_op jit(solution)/shard_map/all_gather | solution.py:55
  32.8 0.9 slice.27
  33.6 3.5 %collective-permute-start = (bf16[64,4096]{1,0:T(8,128)(2,1)}, bf16[64,4096]{1,0:T(8,128)(2,1)}, u32[]{:S(2)}, u32[]{:S(2)}) collective-permute-start(bf16[64,4096]{1,0:T(8,128)(2,1)} %slice.27), channel_id=1, source_target_pairs={{0,8},{1,9},{2,10},{3,11},{4,12},{5,13},{6,14},{7,15},{8,16},{9,17... | collective-permute-start | bytes 1572872 | tf_op jit(solution)/shard_map/ppermute | solution.py:63
  37.2 3.7 %collective-permute-start.2 = (bf16[64,4096]{1,0:T(8,128)(2,1)}, bf16[64,4096]{1,0:T(8,128)(2,1)}, u32[]{:S(2)}, u32[]{:S(2)}) collective-permute-start(bf16[64,4096]{1,0:T(8,128)(2,1)} %slice.27), channel_id=1, source_target_pairs={{0,24},{1,25},{2,26},{3,27},{4,28},{5,29},{6,30},{7,31},{8,0},{9,1... | collective-permute-start | bytes 1572872 | tf_op jit(solution)/shard_map/ppermute | solution.py:63
  40.8 3.7 %collective-permute-start.1 = (bf16[64,4096]{1,0:T(8,128)(2,1)}, bf16[64,4096]{1,0:T(8,128)(2,1)}, u32[]{:S(2)}, u32[]{:S(2)}) collective-permute-start(bf16[64,4096]{1,0:T(8,128)(2,1)} %slice.27), channel_id=1, source_target_pairs={{0,16},{1,17},{2,18},{3,19},{4,20},{5,21},{6,22},{7,23},{8,24},{9,... | collective-permute-start | bytes 1572872 | tf_op jit(solution)/shard_map/ppermute | solution.py:63
  45.8 0.9 broadcast_in_dim.36
  46.6 3.6 %all-to-all-start.1 = ((bf16[4,64,1024]{2,1,0:T(8,128)(2,1)}), bf16[4,64,1024]{2,1,0:T(8,128)(2,1)S(1)}, u32[]{:S(2)}, u32[]{:S(2)}) async-start(bf16[4,64,1024]{2,1,0:T(8,128)(2,1)} %broadcast_in_dim.36), calls=%async_computation.1 | async-start | bytes 1048576 | tf_op jit(solution)/shard_map/all_to_all | solution.py:22
  50.3 0.8 reshape.101
  54.4 1.1 %copy.70 = bf16[64,64,16]{1,2,0:T(8,128)(2,1)} copy(bf16[64,64,16]{0,2,1:T(8,128)(2,1)S(1)} %bitcast.40) | data formatting | bytes 262144 | tf_op jit(solution)/shard_map/reshape | solution.py:135
  59.5 9.9 %all-to-all-done.1 = bf16[4,64,1024]{2,1,0:T(8,128)(2,1)S(1)} async-done(((bf16[4,64,1024]{2,1,0:T(8,128)(2,1)}), bf16[4,64,1024]{2,1,0:T(8,128)(2,1)S(1)}, u32[]{:S(2)}, u32[]{:S(2)}) %all-to-all-start.1) | async-done | bytes 524320 | tf_op jit(solution)/shard_map/all_to_all | solution.py:22
  70.2 0.8 abs_reduce_fusion
  72.3 1.0 maximum_bitcast_fusion
  73.3 10.4 %all-to-all-start.2 = ((f16[32,8,1152]{2,1,0:T(8,128)(2,1)}), f16[32,8,1152]{2,1,0:T(8,128)(2,1)S(1)}, u32[]{:S(2)}, u32[]{:S(2)}) async-start(f16[32,8,1152]{2,1,0:T(8,128)(2,1)} %maximum_bitcast_fusion), calls=%async_computation.2 | async-start | bytes 1179648 | tf_op jit(solution)/shard_map/all_to_all | solution.py:88
  83.6 1.4 %fusion.27 = f32[64,4096]{1,0:T(8,128)S(1)} fusion(bf16[64,4096]{1,0:T(8,128)(2,1)} %collective-permute-done.2, s32[64]{0:T(128)S(1)} %get-tuple-element.39), kind=kOutput, calls=%fused_computation.60 | convolution fusion | flops 33558528 | bytes 1573120 | tf_op jit(solution)/shard_map/dot_general | solution.py:131
  85.6 1.4 %convolution_add_fusion.1 = f32[64,4096]{1,0:T(8,128)S(1)} fusion(f32[64,4096]{1,0:T(8,128)S(1)} %fusion.26, bf16[64,4096]{1,0:T(8,128)(2,1)} %collective-permute-done, s32[64]{0:T(128)S(1)} %copy-done.13), kind=kOutput, calls=%fused_computation.1 | convolution fusion | flops 33820672 | bytes 2621696 | tf_op jit(solution)/shard_map/dot_general | solution.py:131
  87.6 1.4 %fusion.1 = bf16[64,4096]{1,0:T(8,128)(2,1)S(1)} fusion(f32[64,4096]{1,0:T(8,128)S(1)} %fusion.27, f32[64,4096]{1,0:T(8,128)S(1)} %convolution_add_fusion.1, bf16[64,4096]{1,0:T(8,128)(2,1)} %collective-permute-done.1, s32[64]{0:T(128)S(1)} %copy-done.12), kind=kOutput, calls=%fused_computation.3 | convolution fusion | flops 34344960 | bytes 3145984 | tf_op jit(solution)/shard_map/dot_general | solution.py:131
  89.0 1.1 %reshape.94 = bf16[64,64,64]{2,1,0:T(8,128)(2,1)S(1)} reshape(bf16[64,4096]{1,0:T(8,128)(2,1)S(1)} %fusion.1) | data formatting | bytes 1048576 | tf_op jit(solution)/shard_map/reshape | solution.py:134
  91.4 10.3 %all-to-all-done.2 = f16[32,8,1152]{2,1,0:T(8,128)(2,1)S(1)} async-done(((f16[32,8,1152]{2,1,0:T(8,128)(2,1)}), f16[32,8,1152]{2,1,0:T(8,128)(2,1)S(1)}, u32[]{:S(2)}, u32[]{:S(2)}) %all-to-all-start.2) | async-done | bytes 589856 | tf_op jit(solution)/shard_map/all_to_all | solution.py:88
  103.1 0.8 copy-done.2
  105.0 0.9 convolution_add_fusion.2
  (90 shorter events, 16.7 us)
Async XLA Ops:
  1.8 10.8 %copy-start.1 = (bf16[64,4096]{1,0:T(8,128)(2,1)S(1)}, bf16[64,4096]{1,0:T(8,128)(2,1)}, u32[]{:S(2)}) copy-start(bf16[64,4096]{1,0:T(8,128)(2,1)} %param.7) | copy-start | bytes 1572868
  1.8 31.0 %all-to-all-start = ((bf16[8,8,5120]{2,1,0:T(8,128)(2,1)}), bf16[8,8,5120]{2,1,0:T(8,128)(2,1)S(1)}, u32[]{:S(2)}, u32[]{:S(2)}) async-start(bf16[8,8,5120]{2,1,0:T(8,128)(2,1)} %broadcast_in_dim.30), calls=%async_computation | async-start | bytes 1310720 | tf_op jit(solution)/shard_map/all_to_all | solution.py:22
  11.9 0.7 copy-start.16
  13.7 0.7 copy-start.4
  32.8 11.8 %copy-start.14 = (s32[64]{0:T(128)S(1)}, s32[64]{0:T(128)}, u32[]{:S(2)}) copy-start(s32[64]{0:T(128)} %param.9) | copy-start | bytes 772
  33.6 11.0 %copy-start.5 = (s32[64]{0:T(128)S(1)}, s32[64]{0:T(128)}, u32[]{:S(2)}) copy-start(s32[64]{0:T(128)} %param.8) | copy-start | bytes 772
  33.6 11.0 %copy-start.15 = (s32[64]{0:T(128)S(1)}, s32[64]{0:T(128)}, u32[]{:S(2)}) copy-start(s32[64]{0:T(128)} %param.10) | copy-start | bytes 772
  33.6 51.4 %collective-permute-start = (bf16[64,4096]{1,0:T(8,128)(2,1)}, bf16[64,4096]{1,0:T(8,128)(2,1)}, u32[]{:S(2)}, u32[]{:S(2)}) collective-permute-start(bf16[64,4096]{1,0:T(8,128)(2,1)} %slice.27), channel_id=1, source_target_pairs={{0,8},{1,9},{2,10},{3,11},{4,12},{5,13},{6,14},{7,15},{8,16},{9,17... | collective-permute-start | bytes 1572872 | tf_op jit(solution)/shard_map/ppermute | solution.py:63
  37.2 46.5 %collective-permute-start.2 = (bf16[64,4096]{1,0:T(8,128)(2,1)}, bf16[64,4096]{1,0:T(8,128)(2,1)}, u32[]{:S(2)}, u32[]{:S(2)}) collective-permute-start(bf16[64,4096]{1,0:T(8,128)(2,1)} %slice.27), channel_id=1, source_target_pairs={{0,24},{1,25},{2,26},{3,27},{4,28},{5,29},{6,30},{7,31},{8,0},{9,1... | collective-permute-start | bytes 1572872 | tf_op jit(solution)/shard_map/ppermute | solution.py:63
  40.8 46.2 %collective-permute-start.1 = (bf16[64,4096]{1,0:T(8,128)(2,1)}, bf16[64,4096]{1,0:T(8,128)(2,1)}, u32[]{:S(2)}, u32[]{:S(2)}) collective-permute-start(bf16[64,4096]{1,0:T(8,128)(2,1)} %slice.27), channel_id=1, source_target_pairs={{0,16},{1,17},{2,18},{3,19},{4,20},{5,21},{6,22},{7,23},{8,24},{9,... | collective-permute-start | bytes 1572872 | tf_op jit(solution)/shard_map/ppermute | solution.py:63
  46.6 3.6 %copy-start.3 = (bf16[8,4096]{1,0:T(8,128)(2,1)S(1)}, bf16[8,4096]{1,0:T(8,128)(2,1)}, u32[]{:S(2)}) copy-start(bf16[8,4096]{1,0:T(8,128)(2,1)} %param.13) | copy-start | bytes 196612
  46.6 22.8 %all-to-all-start.1 = ((bf16[4,64,1024]{2,1,0:T(8,128)(2,1)}), bf16[4,64,1024]{2,1,0:T(8,128)(2,1)S(1)}, u32[]{:S(2)}, u32[]{:S(2)}) async-start(bf16[4,64,1024]{2,1,0:T(8,128)(2,1)} %broadcast_in_dim.36), calls=%async_computation.1 | async-start | bytes 1048576 | tf_op jit(solution)/shard_map/all_to_all | solution.py:22
  54.4 1.1 %copy-start.17 = (s32[8]{0:T(128)S(1)}, s32[8]{0:T(128)}, u32[]{:S(2)}) copy-start(s32[8]{0:T(128)} %param.12) | copy-start | bytes 100
  55.5 0.7 copy-start.8
  55.5 0.7 copy-start.10
  57.3 0.7 copy-start.11
  59.5 9.9 %copy-start.9 = (pred[64]{0:T(512)(128)(4,1)S(1)}, pred[64]{0:T(512)(128)(4,1)}, u32[]{:S(2)}) copy-start(pred[64]{0:T(512)(128)(4,1)} %get-tuple-element.41) | copy-start | bytes 196
  73.3 28.4 %all-to-all-start.2 = ((f16[32,8,1152]{2,1,0:T(8,128)(2,1)}), f16[32,8,1152]{2,1,0:T(8,128)(2,1)S(1)}, u32[]{:S(2)}, u32[]{:S(2)}) async-start(f16[32,8,1152]{2,1,0:T(8,128)(2,1)} %maximum_bitcast_fusion), calls=%async_computation.2 | async-start | bytes 1179648 | tf_op jit(solution)/shard_map/all_to_all | solution.py:88
  85.0 0.6 copy-start.13
  87.0 0.6 copy-start.12
  89.0 1.1 %copy-start = (bf16[64,64,16]{1,2,0:T(8,128)(2,1)S(1)}, bf16[64,64,16]{1,2,0:T(8,128)(2,1)}, u32[]{:S(2)}) copy-start(bf16[64,64,16]{1,2,0:T(8,128)(2,1)} %copy.70) | copy-start | bytes 393220
  102.0 0.7 copy-start.7
  103.0 0.9 copy-start.2
  104.3 0.7 copy-start.6

commit v9 on v8

--- a/solution.py
+++ b/solution.py
@@ -1,6 +1,7 @@
 import jax
 import jax.numpy as jnp
 from jax import lax
+from jax.experimental import pallas as pl
 from jax.sharding import PartitionSpec as P
 
 BS = 64
@@ -36,6 +37,33 @@
     return high.astype(BF16), (values - high).astype(BF16)
 
 
+def select_rows(place, pieces):
+    slots = place.shape[0]
+    width = pieces[0].shape[1]
+    block = 1024
+
+    def kernel(place_ref, *refs):
+        out_ref = refs[-1]
+        first_row = 0
+        total = jnp.zeros(out_ref.shape, F32)
+        for ref in refs[:-1]:
+            rows = ref.shape[0]
+            column = lax.broadcasted_iota(jnp.int32, (slots, rows), 1) + first_row
+            chosen = (place_ref[...] == column).astype(F32).astype(BF16)
+            total += jnp.dot(chosen, ref[...], preferred_element_type=F32)
+            first_row += rows
+        out_ref[...] = total.astype(BF16)
+
+    return pl.pallas_call(
+        kernel,
+        grid=(width // block,),
+        in_specs=[pl.BlockSpec((slots, 1), lambda n: (0, 0))]
+        + [pl.BlockSpec((piece.shape[0], block), lambda n: (0, n)) for piece in pieces],
+        out_specs=pl.BlockSpec((slots, block), lambda n: (0, n)),
+        out_shape=jax.ShapeDtypeStruct((slots, width), BF16),
+    )(place[:, None], *pieces)
+
+
 def body(a_blocks, blk_row, blk_col, drop_mask, prolong, agg_label, inv_diag):
     slot_count = a_blocks.shape[0]
     per_device = prolong.shape[0]
@@ -58,9 +86,12 @@
         (both, col_panel, blk_row, blk_col, drop_mask, agg_label, inv_diag)
     )
     row_panel = spread(both[:, :width], X_GROUPS)
-    inv_parts = [both[:, width:]]
-    for k in (1, 2, 3):
-        inv_parts.append(lax.ppermute(inv_parts[0], "col", shift_x(k)))
+    inv_own = both[:, width:]
+    half = inv_own.shape[0] // 2
+    inv_left = lax.ppermute(inv_own, "col", shift_x(1))
+    inv_right = lax.ppermute(inv_own, "col", shift_x(-1))
+    inv_far_a = lax.ppermute(inv_left[:half], "col", shift_x(1))
+    inv_far_b = lax.ppermute(inv_right[half:], "col", shift_x(-1))
 
     keep = (drop_mask == 1) | (blk_row == blk_col)
     local_row = blk_row - panel_first
@@ -123,14 +154,11 @@
     )
 
     part_rows = NZ * per_device
-    row_x = local_row // part_rows
-    inverse = None
-    for k in range(NX):
-        at = jnp.where((col_index // NZ - row_x) % NX == k, local_row % part_rows, -1)
-        pick = (at[:, None] == jnp.arange(part_rows)[None, :]).astype(BF16)
-        piece = jnp.dot(pick, inv_parts[k], preferred_element_type=F32)
-        inverse = piece if inverse is None else inverse + piece
-    inverse = inverse.astype(BF16)
+    distance = (col_index // NZ - local_row // part_rows) % NX
+    inverse = select_rows(
+        distance * part_rows + local_row % part_rows,
+        (inv_own, inv_left, inv_far_a, inv_far_b, inv_right),
+    )
     inverse = inverse.reshape(slot_count, BS, BS)
     parts = [part.reshape(slot_count, BS, PC) for part in two_parts(grouped)]
     coarse = jnp.einsum(

time: 107 us -> 101 us (0.944)
  the two profiles are of different devices: /device:TPU:64 before, /device:TPU:1 now
where the time goes in v9:
time: 101 us
  starting transfers between devices  36.1 us (36%)
  waiting for transfers between devices  20.1 us (20%)
  blocking collectives  19.2 us (19%)
  local copies, waits for them, and re-layouts  13.1 us (13%)
  matrix products  4.74 us (5%)
  Pallas kernels  4.29 us (4%)
  other arithmetic  2.93 us (3%)
    all_gather x1, blocking collectives, body(): col_panel = lax.all_gather(labelled, 'row', axis=0, tiled=True)  19.2 us
    all_to_all x2, starting transfers between devices, spread(): lax.all_to_all(copies, 'col', 0, 0, axis_index_groups=groups, tiled=True)  14.9 us
    all_to_all x2, waiting for transfers between devices, spread(): lax.all_to_all(copies, 'col', 0, 0, axis_index_groups=groups, tiled=True)  11.6 us
    all_to_all x1, starting transfers between devices, body(): arrived = lax.all_to_all(sums, 'col', 0, 0, tiled=True)  8.59 us
    ppermute x1, waiting for transfers between devices, body(): inv_far_a = lax.ppermute(inv_left[:half], 'col', shift_x(1))  5.55 us
    ppermute x1, starting transfers between devices, body(): inv_far_b = lax.ppermute(inv_right[half:], 'col', shift_x(-1))  4.39 us
    ppermute x1, starting transfers between devices, body(): inv_right = lax.ppermute(inv_own, 'col', shift_x(-1))  4.39 us
    pallas_call x1, Pallas kernels, select_rows(): pl.pallas_call(kernel, grid=(width // block,), in_specs=[pl.BlockSpec((sl...  4.29 us
  transfers between devices with their start and end apart: 7, of which 3 were waited for; matrix products, arithmetic and copies ran while one was open for 15% of the time, Pallas kernels for 4%

profile of v9, /device:TPU:1, one launch (start us, length us, event | category | flops | bytes accessed | tf_op | source)
XLA Modules:
  0.0 100.8 jit_solution(18020072152541393495)
XLA Ops:
  0.0 0.8 pad_maximum_fusion.1
  0.8 0.9 broadcast_in_dim.28
  1.7 11.0 %all-to-all-start = ((bf16[8,8,5120]{2,1,0:T(8,128)(2,1)}), bf16[8,8,5120]{2,1,0:T(8,128)(2,1)S(1)}, u32[]{:S(2)}, u32[]{:S(2)}) async-start(bf16[8,8,5120]{2,1,0:T(8,128)(2,1)} %broadcast_in_dim.28), calls=%async_computation | async-start | bytes 1310720 | tf_op jit(solution)/shard_map/all_to_all | solution.py:23
  12.7 0.6 copy-done.8
  13.4 1.1 %reshape.92 = bf16[64,64,64]{2,1,0:T(8,128)(2,1)S(1)} reshape(bf16[64,4096]{1,0:T(8,128)(2,1)S(1)} %copy-done.2) | data formatting | bytes 1048576 | tf_op jit(solution)/shard_map/reshape | solution.py:98
  14.6 19.2 %all_gather.3 = bf16[128,1152]{1,0:T(8,128)(2,1)S(1)} all-gather(bf16[8,1152]{1,0:T(8,128)(2,1)S(1)} %pad_maximum_fusion.4), channel_id=1, replica_groups=mesh['row'=16,'col'=32] {'row'}, dimensions={0}, use_global_device_ids=true | all-gather | bytes 313344 | tf_op jit(solution)/shard_map/all_gather | solution.py:83
  33.9 4.4 %collective-permute-start.2 = (bf16[64,4096]{1,0:T(8,128)(2,1)S(1)}, bf16[64,4096]{1,0:T(8,128)(2,1)S(1)}, u32[]{:S(2)}, u32[]{:S(2)}) collective-permute-start(bf16[64,4096]{1,0:T(8,128)(2,1)S(1)} %slice.33.refs_0_), channel_id=1, source_target_pairs={{0,24},{1,25},{2,26},{3,27},{4,28},{5,29},{6,30},{7,31},{8,0},{9,1... | collective-permute-start | bytes 1572872 | tf_op jit(solution)/shard_map/ppermute | solution.py:92
  38.3 1.9 %collective-permute-start = (bf16[64,4096]{1,0:T(8,128)(2,1)S(1)}, bf16[64,4096]{1,0:T(8,128)(2,1)}, u32[]{:S(2)}, u32[]{:S(2)}) collective-permute-start(bf16[64,4096]{1,0:T(8,128)(2,1)S(1)} %slice.33.refs_0_), channel_id=1, source_target_pairs={{0,8},{1,9},{2,10},{3,11},{4,12},{5,13},{6,14},{7,15},{8,16},{9,17... | collective-permute-start | bytes 1572872 | tf_op jit(solution)/shard_map/ppermute | solution.py:91
  41.8 0.9 broadcast_in_dim.31
  42.7 3.9 %all-to-all-start.1 = ((bf16[4,64,1024]{2,1,0:T(8,128)(2,1)}), bf16[4,64,1024]{2,1,0:T(8,128)(2,1)S(1)}, u32[]{:S(2)}, u32[]{:S(2)}) async-start(bf16[4,64,1024]{2,1,0:T(8,128)(2,1)} %broadcast_in_dim.31), calls=%async_computation.1 | async-start | bytes 1048576 | tf_op jit(solution)/shard_map/all_to_all | solution.py:23
  47.4 11.6 %all-to-all-done.1 = bf16[4,64,1024]{2,1,0:T(8,128)(2,1)S(1)} async-done(((bf16[4,64,1024]{2,1,0:T(8,128)(2,1)}), bf16[4,64,1024]{2,1,0:T(8,128)(2,1)S(1)}, u32[]{:S(2)}, u32[]{:S(2)}) %all-to-all-start.1) | async-done | bytes 524320 | tf_op jit(solution)/shard_map/all_to_all | solution.py:23
  59.9 0.8 abs_reduce_fusion
  61.9 1.0 maximum_bitcast_fusion
  62.9 8.6 %all-to-all-start.2 = ((f16[32,8,1152]{2,1,0:T(8,128)(2,1)}), f16[32,8,1152]{2,1,0:T(8,128)(2,1)S(1)}, u32[]{:S(2)}, u32[]{:S(2)}) async-start(f16[32,8,1152]{2,1,0:T(8,128)(2,1)} %maximum_bitcast_fusion), calls=%async_computation.2 | async-start | bytes 1179648 | tf_op jit(solution)/shard_map/all_to_all | solution.py:119
  72.0 4.4 %collective-permute-start.3 = (bf16[32,4096]{1,0:T(8,128)(2,1)S(1)}, bf16[32,4096]{1,0:T(8,128)(2,1)}, u32[]{:S(2)}, u32[]{:S(2)}) collective-permute-start(bf16[32,4096]{1,0:T(8,128)(2,1)S(1)} %slice.45), channel_id=1, source_target_pairs={{0,24},{1,25},{2,26},{3,27},{4,28},{5,29},{6,30},{7,31},{8,0},{9,1... | collective-permute-start | bytes 786440 | tf_op jit(solution)/shard_map/ppermute | solution.py:94
  76.5 1.7 %slice.44 = bf16[32,4096]{1,0:T(8,128)(2,1)} slice(bf16[64,4096]{1,0:T(8,128)(2,1)} %collective-permute-done.refs_1_), slice={[0:32], [0:4096]} | slice | bytes 524288 | tf_op jit(solution)/shard_map/slice | solution.py:93
  78.1 1.9 %collective-permute-start.1 = (bf16[32,4096]{1,0:T(8,128)(2,1)}, bf16[32,4096]{1,0:T(8,128)(2,1)}, u32[]{:S(2)}, u32[]{:S(2)}) collective-permute-start(bf16[32,4096]{1,0:T(8,128)(2,1)} %slice.44), channel_id=1, source_target_pairs={{0,8},{1,9},{2,10},{3,11},{4,12},{5,13},{6,14},{7,15},{8,16},{9,17... | collective-permute-start | bytes 786440 | tf_op jit(solution)/shard_map/ppermute | solution.py:93
  80.4 0.7 copy.68.place_ref
  82.5 2.9 %collective-permute-done.3.refs_3_ = bf16[32,4096]{1,0:T(8,128)(2,1)} collective-permute-done((bf16[32,4096]{1,0:T(8,128)(2,1)S(1)}, bf16[32,4096]{1,0:T(8,128)(2,1)}, u32[]{:S(2)}, u32[]{:S(2)}) %collective-permute-start.3) | collective-permute-done | bytes 262176 | tf_op jit(solution)/shard_map/ppermute | solution.py:94
  85.4 5.5 %collective-permute-done.1.refs_2_ = bf16[32,4096]{1,0:T(8,128)(2,1)} collective-permute-done((bf16[32,4096]{1,0:T(8,128)(2,1)}, bf16[32,4096]{1,0:T(8,128)(2,1)}, u32[]{:S(2)}, u32[]{:S(2)}) %collective-permute-start.1) | collective-permute-done | bytes 262176 | tf_op jit(solution)/shard_map/ppermute | solution.py:93
  90.9 4.3 %shard_map.73 = bf16[64,4096]{1,0:T(8,128)(2,1)} custom-call(s32[64,1]{1,0:T(8,128)} %copy.68.place_ref, bf16[64,4096]{1,0:T(8,128)(2,1)} %copy-done, bf16[64,4096]{1,0:T(8,128)(2,1)} %collective-permute-done.refs_1_, bf16[32,4096]{1,0:T(8,128)(2,1)} %collective-permute-done.1.refs_2_, bf16[32,4096]{1,0:T(8,128)(2,1)} %collective-permute-done.3.refs_3_, ...), custom_call_target="tpu_custom_call" | custom-call | tf_op jit(solution)/shard_map/pallas_call | solution.py:57
  95.2 2.1 %reshape.90 = bf16[64,64,64]{2,1,0:T(8,128)(2,1)S(1)} reshape(bf16[64,4096]{1,0:T(8,128)(2,1)} %shard_map.73) | data formatting | bytes 1048576 | tf_op jit(solution)/shard_map/reshape | solution.py:162
  97.3 0.6 fusion.2
  99.9 0.9 convolution_add_fusion
  (73 shorter events, 8.6 us)
Async XLA Ops:
  1.7 11.7 %copy-start.2 = (bf16[64,4096]{1,0:T(8,128)(2,1)S(1)}, bf16[64,4096]{1,0:T(8,128)(2,1)}, u32[]{:S(2)}) copy-start(bf16[64,4096]{1,0:T(8,128)(2,1)} %param.7) | copy-start | bytes 1572868
  1.7 32.1 %all-to-all-start = ((bf16[8,8,5120]{2,1,0:T(8,128)(2,1)}), bf16[8,8,5120]{2,1,0:T(8,128)(2,1)S(1)}, u32[]{:S(2)}, u32[]{:S(2)}) async-start(bf16[8,8,5120]{2,1,0:T(8,128)(2,1)} %broadcast_in_dim.28), calls=%async_computation | async-start | bytes 1310720 | tf_op jit(solution)/shard_map/all_to_all | solution.py:23
  12.7 0.7 copy-start.8
  13.4 1.2 %copy-start.4 = (bf16[8,1024]{1,0:T(8,128)(2,1)S(1)}, bf16[8,1024]{1,0:T(8,128)(2,1)}, u32[]{:S(2)}) copy-start(bf16[8,1024]{1,0:T(8,128)(2,1)} %param.11) | copy-start | bytes 49156
  33.8 6.4 %copy-start.6 = (s32[64]{0:T(128)S(1)}, s32[64]{0:T(128)}, u32[]{:S(2)}) copy-start(s32[64]{0:T(128)} %param.9) | copy-start | bytes 772
  33.9 7.6 %copy-start = (bf16[64,4096]{1,0:T(8,128)(2,1)}, bf16[64,4096]{1,0:T(8,128)(2,1)S(1)}, u32[]{:S(2)}) copy-start(bf16[64,4096]{1,0:T(8,128)(2,1)S(1)} %slice.33.refs_0_) | copy-start | bytes 1572868
  33.9 38.1 %collective-permute-start.2 = (bf16[64,4096]{1,0:T(8,128)(2,1)S(1)}, bf16[64,4096]{1,0:T(8,128)(2,1)S(1)}, u32[]{:S(2)}, u32[]{:S(2)}) collective-permute-start(bf16[64,4096]{1,0:T(8,128)(2,1)S(1)} %slice.33.refs_0_), channel_id=1, source_target_pairs={{0,24},{1,25},{2,26},{3,27},{4,28},{5,29},{6,30},{7,31},{8,0},{9,1... | collective-permute-start | bytes 1572872 | tf_op jit(solution)/shard_map/ppermute | solution.py:92
  38.3 38.2 %collective-permute-start = (bf16[64,4096]{1,0:T(8,128)(2,1)S(1)}, bf16[64,4096]{1,0:T(8,128)(2,1)}, u32[]{:S(2)}, u32[]{:S(2)}) collective-permute-start(bf16[64,4096]{1,0:T(8,128)(2,1)S(1)} %slice.33.refs_0_), channel_id=1, source_target_pairs={{0,8},{1,9},{2,10},{3,11},{4,12},{5,13},{6,14},{7,15},{8,16},{9,17... | collective-permute-start | bytes 1572872 | tf_op jit(solution)/shard_map/ppermute | solution.py:91
  40.5 0.7 copy-start.5
  40.5 0.7 copy-start.7
  42.7 16.4 %all-to-all-start.1 = ((bf16[4,64,1024]{2,1,0:T(8,128)(2,1)}), bf16[4,64,1024]{2,1,0:T(8,128)(2,1)S(1)}, u32[]{:S(2)}, u32[]{:S(2)}) async-start(bf16[4,64,1024]{2,1,0:T(8,128)(2,1)} %broadcast_in_dim.31), calls=%async_computation.1 | async-start | bytes 1048576 | tf_op jit(solution)/shard_map/all_to_all | solution.py:23
  62.9 35.7 %all-to-all-start.2 = ((f16[32,8,1152]{2,1,0:T(8,128)(2,1)}), f16[32,8,1152]{2,1,0:T(8,128)(2,1)S(1)}, u32[]{:S(2)}, u32[]{:S(2)}) async-start(f16[32,8,1152]{2,1,0:T(8,128)(2,1)} %maximum_bitcast_fusion), calls=%async_computation.2 | async-start | bytes 1179648 | tf_op jit(solution)/shard_map/all_to_all | solution.py:119
  72.0 6.1 %copy-start.1 = (bf16[64,4096]{1,0:T(8,128)(2,1)}, bf16[64,4096]{1,0:T(8,128)(2,1)S(1)}, u32[]{:S(2)}) copy-start(bf16[64,4096]{1,0:T(8,128)(2,1)S(1)} %collective-permute-done.2.refs_4_) | copy-start | bytes 1572868
  72.0 13.3 %collective-permute-start.3 = (bf16[32,4096]{1,0:T(8,128)(2,1)S(1)}, bf16[32,4096]{1,0:T(8,128)(2,1)}, u32[]{:S(2)}, u32[]{:S(2)}) collective-permute-start(bf16[32,4096]{1,0:T(8,128)(2,1)S(1)} %slice.45), channel_id=1, source_target_pairs={{0,24},{1,25},{2,26},{3,27},{4,28},{5,29},{6,30},{7,31},{8,0},{9,1... | collective-permute-start | bytes 786440 | tf_op jit(solution)/shard_map/ppermute | solution.py:94
  78.1 12.8 %collective-permute-start.1 = (bf16[32,4096]{1,0:T(8,128)(2,1)}, bf16[32,4096]{1,0:T(8,128)(2,1)}, u32[]{:S(2)}, u32[]{:S(2)}) collective-permute-start(bf16[32,4096]{1,0:T(8,128)(2,1)} %slice.44), channel_id=1, source_target_pairs={{0,8},{1,9},{2,10},{3,11},{4,12},{5,13},{6,14},{7,15},{8,16},{9,17... | collective-permute-start | bytes 786440 | tf_op jit(solution)/shard_map/ppermute | solution.py:93
  80.0 1.0 %copy-start.3 = (bf16[8,4096]{1,0:T(8,128)(2,1)S(1)}, bf16[8,4096]{1,0:T(8,128)(2,1)}, u32[]{:S(2)}) copy-start(bf16[8,4096]{1,0:T(8,128)(2,1)} %param.13) | copy-start | bytes 196612

commit v10 on v6

--- a/solution.py
+++ b/solution.py
@@ -47,11 +47,13 @@
     panel_first = row_index * span
     own_first = panel_first + col_index * per_device
 
-    both = spread(jnp.concatenate([prolong, inv_diag], axis=1), Z_GROUPS)
-
     labelled = jnp.concatenate(
         [prolong, jnp.broadcast_to(agg_label.astype(BF16)[:, None], (per_device, 128))], axis=1
     )
+    joined = jnp.concatenate([prolong, inv_diag], axis=1)
+    joined, labelled = lax.optimization_barrier((joined, labelled))
+    both = spread(joined, Z_GROUPS)
+
     col_panel = lax.all_gather(labelled, "row", axis=0, tiled=True)
 
     both, col_panel, a_blocks, blk_row, blk_col, drop_mask, own_label, own_inv = (
@@ -92,8 +94,10 @@
     factor = power_of_two(arrived[:, :, width:].astype(F32))[:, :, :1]
     own = (blk_row[None, :] == own_first + jnp.arange(per_device)[:, None]) & ~keep[None, :]
     own = own.astype(BF16)
-    lumped = jnp.dot(jnp.concatenate([own, own], axis=1), drop_parts, preferred_element_type=F32)
-    lumped = lumped + jnp.sum(arrived[:, :, :width].astype(F32) * factor, axis=0)
+    own_lumped = lax.optimization_barrier(
+        jnp.dot(jnp.concatenate([own, own], axis=1), drop_parts, preferred_element_type=F32)
+    )
+    lumped = own_lumped + jnp.sum(arrived[:, :, :width].astype(F32) * factor, axis=0)
     scaled_lumped = jnp.einsum(
         "eij,ejk->eik",
         own_inv.astype(F32).reshape(per_device, BS, BS),

time: 105 us -> 105 us (level)
  transfers between devices with their start and end apart: 6 -> 6, of which waited for: 2 -> 2; matrix products, arithmetic and copies ran while one was open for 21% -> 22% of each run, Pallas kernels for 0% -> 0%
where the time goes in v10:
time: 105 us; the launch traced here: 104 us
  starting transfers between devices  34.9 us (33%)
  blocking collectives  18.4 us (18%)
  waiting for transfers between devices  17.6 us (17%)
  local copies, waits for them, and re-layouts  15.9 us (15%)
  matrix products  9.78 us (9%)
  other arithmetic  7.43 us (7%)
    all_gather x1, blocking collectives, body(): col_panel = lax.all_gather(labelled, 'row', axis=0, tiled=True)  18.4 us
    all_to_all x2, starting transfers between devices, spread(): lax.all_to_all(copies, 'col', 0, 0, axis_index_groups=groups, tiled=True)  13.6 us
    ppermute x3, starting transfers between devices, body(): inv_parts.append(lax.ppermute(inv_parts[0], 'col', shift_x(k)))  10.9 us
    all_to_all x1, starting transfers between devices, body(): arrived = lax.all_to_all(sums, 'col', 0, 0, tiled=True)  10.5 us
    all_to_all x1, waiting for transfers between devices, body(): arrived = lax.all_to_all(sums, 'col', 0, 0, tiled=True)  9.34 us
    all_to_all x2, waiting for transfers between devices, spread(): lax.all_to_all(copies, 'col', 0, 0, axis_index_groups=groups, tiled=True)  8.27 us
    unnamed x38, local copies, waits for them, and re-layouts  5.19 us
    dot_general x4, matrix products, body(): piece = jnp.dot(pick, inv_parts[k], preferred_element_type=F32)  4.46 us
  transfers between devices with their start and end apart: 6, of which 2 were waited for; matrix products, arithmetic and copies ran while one was open for 22% of the time, Pallas kernels for 0%

profile of v10, /device:TPU:64, one launch (start us, length us, event | category | flops | bytes accessed | tf_op | source)
XLA Modules:
  0.0 104.5 jit_solution(14409974042618386273)
XLA Ops:
  0.7 0.9 pad_maximum_fusion.1
  1.6 0.9 broadcast_in_dim.31
  2.5 10.0 %all-to-all-start = ((bf16[8,8,5120]{2,1,0:T(8,128)(2,1)}), bf16[8,8,5120]{2,1,0:T(8,128)(2,1)S(1)}, u32[]{:S(2)}, u32[]{:S(2)}) async-start(bf16[8,8,5120]{2,1,0:T(8,128)(2,1)} %broadcast_in_dim.31), calls=%async_computation | async-start | bytes 1310720 | tf_op jit(solution)/shard_map/all_to_all | solution.py:22
  13.1 18.4 %all_gather.3 = bf16[128,1152]{1,0:T(8,128)(2,1)S(1)} all-gather(bf16[8,1152]{1,0:T(8,128)(2,1)S(1)} %pad_maximum_fusion.4), channel_id=1, replica_groups=mesh['row'=16,'col'=32] {'row'}, dimensions={0}, use_global_device_ids=true | all-gather | bytes 313344 | tf_op jit(solution)/shard_map/all_gather | solution.py:57
  31.4 0.8 slice.27
  32.3 3.5 %collective-permute-start = (bf16[64,4096]{1,0:T(8,128)(2,1)}, bf16[64,4096]{1,0:T(8,128)(2,1)}, u32[]{:S(2)}, u32[]{:S(2)}) collective-permute-start(bf16[64,4096]{1,0:T(8,128)(2,1)} %slice.27), channel_id=1, source_target_pairs={{0,8},{1,9},{2,10},{3,11},{4,12},{5,13},{6,14},{7,15},{8,16},{9,17... | collective-permute-start | bytes 1572872 | tf_op jit(solution)/shard_map/ppermute | solution.py:67
  35.8 3.7 %collective-permute-start.2 = (bf16[64,4096]{1,0:T(8,128)(2,1)}, bf16[64,4096]{1,0:T(8,128)(2,1)}, u32[]{:S(2)}, u32[]{:S(2)}) collective-permute-start(bf16[64,4096]{1,0:T(8,128)(2,1)} %slice.27), channel_id=1, source_target_pairs={{0,24},{1,25},{2,26},{3,27},{4,28},{5,29},{6,30},{7,31},{8,0},{9,1... | collective-permute-start | bytes 1572872 | tf_op jit(solution)/shard_map/ppermute | solution.py:67
  39.5 3.7 %collective-permute-start.1 = (bf16[64,4096]{1,0:T(8,128)(2,1)}, bf16[64,4096]{1,0:T(8,128)(2,1)}, u32[]{:S(2)}, u32[]{:S(2)}) collective-permute-start(bf16[64,4096]{1,0:T(8,128)(2,1)} %slice.27), channel_id=1, source_target_pairs={{0,16},{1,17},{2,18},{3,19},{4,20},{5,21},{6,22},{7,23},{8,24},{9,... | collective-permute-start | bytes 1572872 | tf_op jit(solution)/shard_map/ppermute | solution.py:67
  44.3 0.9 broadcast_in_dim.36
  45.2 3.6 %all-to-all-start.1 = ((bf16[4,64,1024]{2,1,0:T(8,128)(2,1)}), bf16[4,64,1024]{2,1,0:T(8,128)(2,1)S(1)}, u32[]{:S(2)}, u32[]{:S(2)}) async-start(bf16[4,64,1024]{2,1,0:T(8,128)(2,1)} %broadcast_in_dim.36), calls=%async_computation.1 | async-start | bytes 1048576 | tf_op jit(solution)/shard_map/all_to_all | solution.py:22
  48.8 1.1 %reshape.95 = bf16[64,64,64]{2,1,0:T(8,128)(2,1)S(1)} reshape(bf16[64,4096]{1,0:T(8,128)(2,1)S(1)} %copy-done.1) | data formatting | bytes 1048576 | tf_op jit(solution)/shard_map/reshape | solution.py:71
  50.0 0.8 reshape.101
  54.7 1.1 %copy.70 = bf16[64,64,16]{1,2,0:T(8,128)(2,1)} copy(bf16[64,64,16]{0,2,1:T(8,128)(2,1)S(1)} %bitcast.36) | data formatting | bytes 262144 | tf_op jit(solution)/shard_map/reshape | solution.py:141
  59.8 8.3 %all-to-all-done.1 = bf16[4,64,1024]{2,1,0:T(8,128)(2,1)S(1)} async-done(((bf16[4,64,1024]{2,1,0:T(8,128)(2,1)}), bf16[4,64,1024]{2,1,0:T(8,128)(2,1)S(1)}, u32[]{:S(2)}, u32[]{:S(2)}) %all-to-all-start.1) | async-done | bytes 524320 | tf_op jit(solution)/shard_map/all_to_all | solution.py:22
  68.9 0.8 abs_reduce_fusion
  70.9 1.0 maximum_bitcast_fusion
  71.9 10.5 %all-to-all-start.2 = ((f16[32,8,1152]{2,1,0:T(8,128)(2,1)}), f16[32,8,1152]{2,1,0:T(8,128)(2,1)S(1)}, u32[]{:S(2)}, u32[]{:S(2)}) async-start(f16[32,8,1152]{2,1,0:T(8,128)(2,1)} %maximum_bitcast_fusion), calls=%async_computation.2 | async-start | bytes 1179648 | tf_op jit(solution)/shard_map/all_to_all | solution.py:92
  82.4 0.9 fusion.20
  83.3 1.4 %fusion.28 = f32[64,4096]{1,0:T(8,128)S(1)} fusion(bf16[64,4096]{1,0:T(8,128)(2,1)} %collective-permute-done.2, s32[64]{0:T(128)S(1)} %get-tuple-element.45), kind=kOutput, calls=%fused_computation.58 | convolution fusion | flops 33558528 | bytes 1573120 | tf_op jit(solution)/shard_map/dot_general | solution.py:137
  85.3 1.4 %convolution_add_fusion.1 = f32[64,4096]{1,0:T(8,128)S(1)} fusion(f32[64,4096]{1,0:T(8,128)S(1)} %fusion.27, bf16[64,4096]{1,0:T(8,128)(2,1)} %collective-permute-done, s32[64]{0:T(128)S(1)} %copy-done.15), kind=kOutput, calls=%fused_computation.1 | convolution fusion | flops 33820672 | bytes 2621696 | tf_op jit(solution)/shard_map/dot_general | solution.py:137
  87.3 1.4 %fusion.1 = bf16[64,4096]{1,0:T(8,128)(2,1)S(1)} fusion(f32[64,4096]{1,0:T(8,128)S(1)} %fusion.28, f32[64,4096]{1,0:T(8,128)S(1)} %convolution_add_fusion.1, bf16[64,4096]{1,0:T(8,128)(2,1)} %collective-permute-done.1, s32[64]{0:T(128)S(1)} %copy-done.14), kind=kOutput, calls=%fused_computation.3 | convolution fusion | flops 34344960 | bytes 3145984 | tf_op jit(solution)/shard_map/dot_general | solution.py:137
  88.7 1.1 %reshape.94 = bf16[64,64,64]{2,1,0:T(8,128)(2,1)S(1)} reshape(bf16[64,4096]{1,0:T(8,128)(2,1)S(1)} %fusion.1) | data formatting | bytes 1048576 | tf_op jit(solution)/shard_map/reshape | solution.py:140
  91.2 9.3 %all-to-all-done.2 = f16[32,8,1152]{2,1,0:T(8,128)(2,1)S(1)} async-done(((f16[32,8,1152]{2,1,0:T(8,128)(2,1)}), f16[32,8,1152]{2,1,0:T(8,128)(2,1)S(1)}, u32[]{:S(2)}, u32[]{:S(2)}) %all-to-all-start.2) | async-done | bytes 589856 | tf_op jit(solution)/shard_map/all_to_all | solution.py:92
  103.6 0.9 convolution_add_fusion.2
  (93 shorter events, 17.8 us)
Async XLA Ops:
  0.7 0.9 copy-start.5
  2.5 28.9 %all-to-all-start = ((bf16[8,8,5120]{2,1,0:T(8,128)(2,1)}), bf16[8,8,5120]{2,1,0:T(8,128)(2,1)S(1)}, u32[]{:S(2)}, u32[]{:S(2)}) async-start(bf16[8,8,5120]{2,1,0:T(8,128)(2,1)} %broadcast_in_dim.31), calls=%async_computation | async-start | bytes 1310720 | tf_op jit(solution)/shard_map/all_to_all | solution.py:22
  31.4 11.8 %copy-start.16 = (s32[64]{0:T(128)S(1)}, s32[64]{0:T(128)}, u32[]{:S(2)}) copy-start(s32[64]{0:T(128)} %param.9) | copy-start | bytes 772
  32.3 11.0 %copy-start.6 = (s32[64]{0:T(128)S(1)}, s32[64]{0:T(128)}, u32[]{:S(2)}) copy-start(s32[64]{0:T(128)} %param.8) | copy-start | bytes 772
  32.3 11.0 %copy-start.17 = (s32[64]{0:T(128)S(1)}, s32[64]{0:T(128)}, u32[]{:S(2)}) copy-start(s32[64]{0:T(128)} %param.10) | copy-start | bytes 772
  32.3 52.4 %collective-permute-start = (bf16[64,4096]{1,0:T(8,128)(2,1)}, bf16[64,4096]{1,0:T(8,128)(2,1)}, u32[]{:S(2)}, u32[]{:S(2)}) collective-permute-start(bf16[64,4096]{1,0:T(8,128)(2,1)} %slice.27), channel_id=1, source_target_pairs={{0,8},{1,9},{2,10},{3,11},{4,12},{5,13},{6,14},{7,15},{8,16},{9,17... | collective-permute-start | bytes 1572872 | tf_op jit(solution)/shard_map/ppermute | solution.py:67
  35.8 47.5 %collective-permute-start.2 = (bf16[64,4096]{1,0:T(8,128)(2,1)}, bf16[64,4096]{1,0:T(8,128)(2,1)}, u32[]{:S(2)}, u32[]{:S(2)}) collective-permute-start(bf16[64,4096]{1,0:T(8,128)(2,1)} %slice.27), channel_id=1, source_target_pairs={{0,24},{1,25},{2,26},{3,27},{4,28},{5,29},{6,30},{7,31},{8,0},{9,1... | collective-permute-start | bytes 1572872 | tf_op jit(solution)/shard_map/ppermute | solution.py:67
  39.5 47.2 %collective-permute-start.1 = (bf16[64,4096]{1,0:T(8,128)(2,1)}, bf16[64,4096]{1,0:T(8,128)(2,1)}, u32[]{:S(2)}, u32[]{:S(2)}) collective-permute-start(bf16[64,4096]{1,0:T(8,128)(2,1)} %slice.27), channel_id=1, source_target_pairs={{0,16},{1,17},{2,18},{3,19},{4,20},{5,21},{6,22},{7,23},{8,24},{9,... | collective-permute-start | bytes 1572872 | tf_op jit(solution)/shard_map/ppermute | solution.py:67
  45.2 3.6 %copy-start.1 = (bf16[64,4096]{1,0:T(8,128)(2,1)S(1)}, bf16[64,4096]{1,0:T(8,128)(2,1)}, u32[]{:S(2)}) copy-start(bf16[64,4096]{1,0:T(8,128)(2,1)} %param.7) | copy-start | bytes 1572868
  45.2 22.9 %all-to-all-start.1 = ((bf16[4,64,1024]{2,1,0:T(8,128)(2,1)}), bf16[4,64,1024]{2,1,0:T(8,128)(2,1)S(1)}, u32[]{:S(2)}, u32[]{:S(2)}) async-start(bf16[4,64,1024]{2,1,0:T(8,128)(2,1)} %broadcast_in_dim.36), calls=%async_computation.1 | async-start | bytes 1048576 | tf_op jit(solution)/shard_map/all_to_all | solution.py:22
  48.8 1.1 %copy-start.3 = (bf16[8,4096]{1,0:T(8,128)(2,1)S(1)}, bf16[8,4096]{1,0:T(8,128)(2,1)}, u32[]{:S(2)}) copy-start(bf16[8,4096]{1,0:T(8,128)(2,1)} %param.13) | copy-start | bytes 196612
  52.9 0.7 copy-start.7
  54.7 1.1 %copy-start.18 = (s32[8]{0:T(128)S(1)}, s32[8]{0:T(128)}, u32[]{:S(2)}) copy-start(s32[8]{0:T(128)} %param.12) | copy-start | bytes 100
  55.8 0.7 copy-start.12
  57.7 0.6 copy-start.13
  59.8 8.3 %copy-start.11 = (pred[64]{0:T(512)(128)(4,1)S(1)}, pred[64]{0:T(512)(128)(4,1)}, u32[]{:S(2)}) copy-start(pred[64]{0:T(512)(128)(4,1)} %get-tuple-element.47) | copy-start | bytes 196
  71.9 10.5 %copy-start.9 = (pred[8,64]{1,0:T(8,128)(4,1)S(1)}, pred[8,64]{1,0:T(8,128)(4,1)}, u32[]{:S(2)}) copy-start(pred[8,64]{1,0:T(8,128)(4,1)} %compare_and_fusion.1) | copy-start | bytes 1540
  71.9 28.6 %all-to-all-start.2 = ((f16[32,8,1152]{2,1,0:T(8,128)(2,1)}), f16[32,8,1152]{2,1,0:T(8,128)(2,1)S(1)}, u32[]{:S(2)}, u32[]{:S(2)}) async-start(f16[32,8,1152]{2,1,0:T(8,128)(2,1)} %maximum_bitcast_fusion), calls=%async_computation.2 | async-start | bytes 1179648 | tf_op jit(solution)/shard_map/all_to_all | solution.py:92
  84.7 0.7 copy-start.15
  86.7 0.6 copy-start.14
  88.7 1.1 %copy-start = (bf16[64,64,16]{1,2,0:T(8,128)(2,1)S(1)}, bf16[64,64,16]{1,2,0:T(8,128)(2,1)}, u32[]{:S(2)}) copy-start(bf16[64,64,16]{1,2,0:T(8,128)(2,1)} %copy.70) | copy-start | bytes 393220
  100.8 0.8 copy-start.4
  101.6 0.9 copy-start.2
  102.9 0.6 copy-start.8
  (1 other events, 0.6 us)
